TPU v7x, 32 devices: a whole 2x2x4 slice. The times are simulated.
32 devices in a mesh: band: 8 (over z, y), col: 4 (over x, core).
Axes of the slice: x: 2, y: 2, z: 4, core: 2. Of those that a mesh axis runs over, the one named last changes fastest.
Arguments:
- demand: float32 [32768, 16], P(('band', 'col')), may hold values from -16 to 16
- lead_periods: int32 [32768], P(('band', 'col')), may hold values from 1 to 4
- matrix_tiles: float32 [8, 4, 128, 128, 128], P('band', 'col'), may hold values from -0.125 to 0.125
- tile_pos: int32 [8, 4, 128], P('band', 'col'), may hold values from 0 to 2047, as said below
- cost_vector: float32 [32768], P(('band', 'col')), may hold values from 0.05 to 7
- primal_init: float32 [32768, 16], P(('band', 'col')), may hold values from 0 to 2
- dual_init: float32 [32768, 16], P(('band', 'col')), may hold values from -6 to 6
- weight_init: float32 [16], replicated, may hold values from 0.5 to 2
Outputs:
- primal: float32 [32768, 16], P(('band', 'col'))
- dual_vars: float32 [32768, 16], P(('band', 'col'))
- weight: float32 [16], replicated
Inputs may be any that keep to these rules, and one draw needn't show every extreme that they name: `tile_pos`: within one period and column block the 128 entries are different; entry v places its tile at row tile v // 64 of that period and column tile v % (64) of that column block.
All inputs are finite; a program needn't handle non-finite values.
Results may differ from a plain program's by a relative error of at most 0.0003.
Values sent between devices are 32-bit elements; how exact they have to be, the bound alone decides.
No kernel may reach another device: no remote copies, remote signals or barrier semaphores. Data moves between devices by JAX's collectives and lax.ppermute only.
A program may use at most 64 MiB of HBM per device.

v0:
```python
import jax
import jax.numpy as jnp
from jax import lax
from jax.sharding import PartitionSpec as P

ITERS = 3
LEAD_MAX = 4


step_scale = 0.45
return_share = 0.6
epsilon = 1e-06
highest = lax.Precision.HIGHEST


def passed_along(value, axis, steps):
    count = lax.axis_size(axis)
    pairs = [(source, (source + steps) % count) for source in range(count)]
    return lax.ppermute(value, axis, pairs)


def forward_part(matrix_tiles, positions, column_block, units_col, units_row):
    tile_size = matrix_tiles.shape[-1]
    scen_count = column_block.shape[-1]
    blocks = column_block.reshape(-1, tile_size, scen_count)
    picked = blocks[positions % units_col]
    product = jnp.einsum("tij,tjs->tis", matrix_tiles, picked, precision=highest)
    onehot = (
        positions[None, :] // units_col == jnp.arange(units_row, dtype=jnp.int32)[:, None]
    ).astype(jnp.float32)
    result = jnp.dot(onehot, product.reshape(product.shape[0], -1), precision=highest)
    return result.reshape(units_row * tile_size, scen_count)


def backward_part(matrix_tiles, positions, band_dual, units_col):
    tile_size = matrix_tiles.shape[-1]
    scen_count = band_dual.shape[-1]
    blocks = band_dual.reshape(-1, tile_size, scen_count)
    picked = blocks[positions // units_col]
    product = jnp.einsum("tij,tis->tjs", matrix_tiles, picked, precision=highest)
    result = jax.ops.segment_sum(product, positions % units_col, num_segments=units_col)
    return result.reshape(units_col * tile_size, scen_count)


def on_device(
    demand, lead_periods, matrix_tiles, tile_pos, cost_vector, primal_init, dual_init, weight_init
):
    band_count = lax.axis_size("band")
    column_count = lax.axis_size("col")
    matrix_tiles = matrix_tiles.reshape(matrix_tiles.shape[2:])
    positions = tile_pos.reshape(-1)
    tile_size = matrix_tiles.shape[-1]
    block_rows = demand.shape[0]
    sub_count = block_rows // tile_size
    units_col = band_count * sub_count
    units_row = column_count * sub_count
    earlier = demand
    lagged = jnp.zeros_like(demand)
    for lead in range(1, LEAD_MAX + 1):
        earlier = passed_along(earlier, "band", 1)
        lagged = jnp.where(lead_periods[:, None] == lead, earlier, lagged)
    right_side = demand - return_share * lagged
    primal, block_cost = (
        lax.all_gather(primal_init, "band", axis=0, tiled=True),
        lax.all_gather(cost_vector, "band", axis=0, tiled=True),
    )
    offset = lax.axis_index("band") * block_rows
    dual_vars = dual_init
    weight = weight_init
    for iteration in range(ITERS):
        primal_step = (step_scale / weight)[None, :]
        dual_step = (step_scale * weight)[None, :]
        band_dual = lax.all_gather(dual_vars, "col", axis=0, tiled=True)
        partial_value = backward_part(matrix_tiles, positions, band_dual, units_col)
        pull_terms = lax.psum(partial_value, "band")
        primal_new = jnp.maximum(primal - primal_step * (block_cost[:, None] - pull_terms), 0.0)
        primal_change = lax.dynamic_slice_in_dim(primal_new - primal, offset, block_rows, 0)
        column_block = 2.0 * primal_new - primal
        primal_local = jnp.sum(primal_change * primal_change, axis=0)
        primal_square = lax.psum(primal_local, ("band", "col"))
        push_part = forward_part(matrix_tiles, positions, column_block, units_col, units_row)
        push_terms = lax.psum_scatter(push_part, "col", scatter_dimension=0, tiled=True)
        dual_new = dual_vars + dual_step * (right_side - push_terms)
        dual_change = dual_new - dual_vars
        dual_local = jnp.sum(dual_change * dual_change, axis=0)
        dual_square = lax.psum(dual_local, ("band", "col"))
        weight = jnp.sqrt(weight * jnp.sqrt((primal_square + epsilon) / (dual_square + epsilon)))
        primal = primal_new
        dual_vars = dual_new
    primal = lax.dynamic_slice_in_dim(primal, offset, block_rows, 0)
    return (primal, dual_vars, weight)


def solution(mesh):
    in_specs = (
        P(("band", "col"), None),
        P(("band", "col")),
        P("band", "col", None, None, None),
        P("band", "col", None),
        P(("band", "col")),
        P(("band", "col"), None),
        P(("band", "col"), None),
        P(),
    )
    out_specs = (P(("band", "col"), None), P(("band", "col"), None), P())
    return jax.shard_map(
        on_device, mesh=mesh, in_specs=in_specs, out_specs=out_specs, check_vma=False
    )
```

profile of v0, /device:TPU:0, one launch (start us, length us, event | category | flops | bytes accessed | tf_op | source)
XLA Modules:
  0.0 476.5 jit_solution(1423879935597722344)
XLA Ops:
  8.6 7.4 %all_gather.17 = f32[4096,16]{0,1:T(8,128)S(1)} all-gather(f32[1024,16]{0,1:T(8,128)} %param.14), channel_id=1, replica_groups=mesh['band'=8,'col'=4] {'col'}, dimensions={0}, use_global_device_ids=true | all-gather | bytes 327680 | tf_op jit(solution)/shard_map/all_gather | solution.py:73
  16.8 9.5 %fusion.12 = f32[128,128,16]{1,2,0:T(8,128)S(1)} fusion(f32[128,128,16]{1,2,0:T(8,128)S(1)} %gather_fusion, f32[1,1,128,128,128]{4,3,2,1,0:T(8,128)} %param.10), kind=kOutput, calls=%fused_computation.21 | convolution fusion | flops 402653184 | bytes 10485760 | tf_op jit(solution)/shard_map/tij,tis->tjs/dot_general | solution.py:40
  26.4 5.2 %scatter_fusion = f32[64,128,16]{1,2,0:T(8,128)S(1)} fusion(f32[64,128,16]{1,2,0:T(8,128)S(1)} %broadcast.213.clone, s32[128]{0:T(128)S(1)} %get-tuple-element.46, f32[128,128,16]{1,2,0:T(8,128)S(1)} %fusion.12), kind=kCustom, calls=%fused_computation.6 | custom fusion | flops 262144 | bytes 3146240 | tf_op jit(solution)/shard_map/scatter-add | solution.py:41
  32.5 31.1 %all_gather.16 = f32[8192]{0:T(1024)S(1)} all-gather(f32[1024]{0:T(1024)S(1)} %copy-done.5), channel_id=1, replica_groups=mesh['band'=8,'col'=4] {'band'}, dimensions={0}, use_global_device_ids=true | all-gather | bytes 36864 | tf_op jit(solution)/shard_map/all_gather | solution.py:65
  63.7 31.7 %all_gather.15 = f32[8192,16]{0,1:T(8,128)S(1)} all-gather(f32[1024,16]{0,1:T(8,128)S(1)} %copy-done.3), channel_id=1, replica_groups=mesh['band'=8,'col'=4] {'band'}, dimensions={0}, use_global_device_ids=true | all-gather | bytes 589824 | tf_op jit(solution)/shard_map/all_gather | solution.py:64
  95.4 11.5 %all-reduce.7.cloned.1.call-done = f32[8192,16]{0,1:T(8,128)} async-done(((f32[8192,16]{0,1:T(8,128)}), f32[8192,16]{0,1:T(8,128)}) %all-reduce.7.cloned.1.call-update) | async-done | bytes 524304 | tf_op jit(solution)/shard_map/psum | solution.py:75
  109.0 15.4 %fusion.15 = f32[128,128,16]{1,2,0:T(8,128)S(1)} fusion(f32[128,128,16]{1,2,0:T(8,128)S(1)} %gather_fusion.1, f32[1,1,128,128,128]{4,3,2,1,0:T(8,128)} %param.10), kind=kOutput, calls=%fused_computation.22 | convolution fusion | flops 402653184 | bytes 10485760 | tf_op jit(solution)/shard_map/tij,tjs->tis/dot_general | solution.py:27
  126.5 1.3 copy.67
  128.7 6.2 %collective-permute-done = f32[1024,16]{0,1:T(8,128)S(1)} collective-permute-done((f32[1024,16]{0,1:T(8,128)S(1)}, f32[1024,16]{0,1:T(8,128)S(1)}, u32[]{:S(2)}, u32[]{:S(2)}) %collective-permute-start) | collective-permute-done | bytes 65568 | tf_op jit(solution)/shard_map/ppermute | solution.py:19
  134.9 7.0 %collective-permute-done.1 = f32[1024,16]{0,1:T(8,128)S(1)} collective-permute-done((f32[1024,16]{0,1:T(8,128)S(1)}, f32[1024,16]{0,1:T(8,128)S(1)}, u32[]{:S(2)}, u32[]{:S(2)}) %collective-permute-start.1) | collective-permute-done | bytes 65568 | tf_op jit(solution)/shard_map/ppermute | solution.py:19
  141.9 7.0 %collective-permute-done.2 = f32[1024,16]{0,1:T(8,128)S(1)} collective-permute-done((f32[1024,16]{0,1:T(8,128)S(1)}, f32[1024,16]{0,1:T(8,128)S(1)}, u32[]{:S(2)}, u32[]{:S(2)}) %collective-permute-start.2) | collective-permute-done | bytes 65568 | tf_op jit(solution)/shard_map/ppermute | solution.py:19
  148.9 6.9 %collective-permute-done.3 = f32[1024,16]{0,1:T(8,128)S(1)} collective-permute-done((f32[1024,16]{0,1:T(8,128)S(1)}, f32[1024,16]{0,1:T(8,128)S(1)}, u32[]{:S(2)}, u32[]{:S(2)}) %collective-permute-start.3) | collective-permute-done | bytes 65568 | tf_op jit(solution)/shard_map/ppermute | solution.py:19
  156.9 6.4 %all_gather.18 = f32[4096,16]{0,1:T(8,128)S(1)} all-gather(f32[1024,16]{0,1:T(8,128)S(1)} %get-tuple-element.33), channel_id=1, replica_groups=mesh['band'=8,'col'=4] {'col'}, dimensions={0}, use_global_device_ids=true | all-gather | bytes 327680 | tf_op jit(solution)/shard_map/all_gather | solution.py:73
  164.0 9.5 %fusion.18 = f32[128,128,16]{1,2,0:T(8,128)S(1)} fusion(f32[128,128,16]{1,2,0:T(8,128)S(1)} %gather_fusion.2, f32[1,1,128,128,128]{4,3,2,1,0:T(8,128)} %param.10), kind=kOutput, calls=%fused_computation.23 | convolution fusion | flops 402653184 | bytes 10485760 | tf_op jit(solution)/shard_map/tij,tis->tjs/dot_general | solution.py:40
  173.5 5.2 %scatter_fusion.1 = f32[64,128,16]{1,2,0:T(8,128)S(1)} fusion(f32[64,128,16]{1,2,0:T(8,128)S(1)} %broadcast.213.clone.1, s32[128]{0:T(128)S(1)} %get-tuple-element.46, f32[128,128,16]{1,2,0:T(8,128)S(1)} %fusion.18), kind=kCustom, calls=%fused_computation.7 | custom fusion | flops 262144 | bytes 3146240 | tf_op jit(solution)/shard_map/scatter-add | solution.py:41
  180.6 37.3 %all-reduce.2 = (f32[16]{0:T(128)S(1)}, f32[16]{0:T(128)S(1)}) all-reduce(f32[16]{0:T(128)S(1)} %get-tuple-element.32, f32[16]{0:T(128)S(1)} %fusion.31), channel_id=1, replica_groups=mesh['band'=8,'col'=4] {'band','col'}, use_global_device_ids=true, to_apply=%region_6.7 | all-reduce | flops 32 | bytes 256 | tf_op jit(solution)/shard_map/psum | solution.py:86
  218.0 31.7 %all-reduce.9.cloned.1.call-done = f32[8192,16]{0,1:T(8,128)} async-done(((f32[8192,16]{0,1:T(8,128)}), f32[8192,16]{0,1:T(8,128)}) %all-reduce.9.cloned.1.call-update) | async-done | bytes 524304 | tf_op jit(solution)/shard_map/psum | solution.py:75
  249.7 2.0 subtract_bitcast_fusion.1
  252.5 15.4 %fusion.21 = f32[128,128,16]{1,2,0:T(8,128)S(1)} fusion(f32[128,128,16]{1,2,0:T(8,128)S(1)} %gather_fusion.3, f32[1,1,128,128,128]{4,3,2,1,0:T(8,128)} %param.10), kind=kOutput, calls=%fused_computation.24 | convolution fusion | flops 402653184 | bytes 10485760 | tf_op jit(solution)/shard_map/tij,tjs->tis/dot_general | solution.py:27
  270.0 1.3 copy.72
  271.3 19.3 %reduce-scatter.6.cloned.1.call-done = f32[1024,16]{0,1:T(8,128)} async-done(((f32[4096,16]{0,1:T(8,128)}), f32[1024,16]{0,1:T(8,128)}) %reduce-scatter.6.cloned.1.call-update) | async-done | bytes 65552 | tf_op jit(solution)/shard_map/reduce_scatter | solution.py:82
  291.7 6.0 %all_gather.19 = f32[4096,16]{0,1:T(8,128)S(1)} all-gather(f32[1024,16]{0,1:T(8,128)S(1)} %get-tuple-element.27), channel_id=1, replica_groups=mesh['band'=8,'col'=4] {'col'}, dimensions={0}, use_global_device_ids=true | all-gather | bytes 327680 | tf_op jit(solution)/shard_map/all_gather | solution.py:73
  298.5 9.5 %fusion.24 = f32[128,128,16]{1,2,0:T(8,128)S(1)} fusion(f32[128,128,16]{1,2,0:T(8,128)S(1)} %gather_fusion.4, f32[1,1,128,128,128]{4,3,2,1,0:T(8,128)} %param.10), kind=kOutput, calls=%fused_computation.25 | convolution fusion | flops 402653184 | bytes 10485760 | tf_op jit(solution)/shard_map/tij,tis->tjs/dot_general | solution.py:40
  308.0 5.2 %scatter_fusion.2 = f32[64,128,16]{1,2,0:T(8,128)S(1)} fusion(f32[64,128,16]{1,2,0:T(8,128)S(1)} %broadcast.213, s32[128]{0:T(128)S(1)} %get-tuple-element.46, f32[128,128,16]{1,2,0:T(8,128)S(1)} %fusion.24), kind=kCustom, calls=%fused_computation.8 | custom fusion | flops 262144 | bytes 3146240 | tf_op jit(solution)/shard_map/scatter-add | solution.py:41
  314.3 39.7 %all-reduce.1 = (f32[16]{0:T(128)S(1)}, f32[16]{0:T(128)S(1)}) all-reduce(f32[16]{0:T(128)S(1)} %get-tuple-element.26, f32[16]{0:T(128)S(1)} %multiply_reduce_fusion.3), channel_id=1, replica_groups=mesh['band'=8,'col'=4] {'band','col'}, use_global_device_ids=true, to_apply=%region_13.14 | all-reduce | flops 32 | bytes 256 | tf_op jit(solution)/shard_map/psum | solution.py:86
  354.1 32.9 %all-reduce.11.cloned.1.call-done = f32[8192,16]{0,1:T(8,128)} async-done(((f32[8192,16]{0,1:T(8,128)}), f32[8192,16]{0,1:T(8,128)}) %all-reduce.11.cloned.1.call-update) | async-done | bytes 524304 | tf_op jit(solution)/shard_map/psum | solution.py:75
  387.0 2.0 subtract_bitcast_fusion
  389.8 15.4 %fusion.27 = f32[128,128,16]{1,2,0:T(8,128)S(1)} fusion(f32[128,128,16]{1,2,0:T(8,128)S(1)} %gather_fusion.5, f32[1,1,128,128,128]{4,3,2,1,0:T(8,128)} %param.10), kind=kOutput, calls=%fused_computation.26 | convolution fusion | flops 402653184 | bytes 10485760 | tf_op jit(solution)/shard_map/tij,tjs->tis/dot_general | solution.py:27
  408.5 1.6 multiply_reduce_fusion.1
  410.1 17.8 %reduce-scatter.8.cloned.1.call-done = f32[1024,16]{0,1:T(8,128)} async-done(((f32[4096,16]{0,1:T(8,128)}), f32[1024,16]{0,1:T(8,128)}) %reduce-scatter.8.cloned.1.call-update) | async-done | bytes 65552 | tf_op jit(solution)/shard_map/reduce_scatter | solution.py:82
  427.9 1.7 multiply_reduce_fusion
  429.6 39.3 %all-reduce = (f32[16]{0:T(128)S(1)}, f32[16]{0:T(128)S(1)}) all-reduce(f32[16]{0:T(128)S(1)} %get-tuple-element.20, f32[16]{0:T(128)S(1)} %get-tuple-element.18), channel_id=1, replica_groups=mesh['band'=8,'col'=4] {'band','col'}, use_global_device_ids=true, to_apply=%region_20.21 | all-reduce | flops 32 | bytes 256 | tf_op jit(solution)/shard_map/psum | solution.py:86
  (80 shorter events, 22.4 us)
Async XLA Ops:
  7.2 99.8 %all-reduce.7.cloned.1.call-start = ((), (), s32[]{:S(2)}) async-start(), calls=%async_computation.3 | async-start | bytes 1048576 | tf_op jit(solution)/shard_map/psum | solution.py:75
  16.8 15.7 %copy-start.8 = (s32[1,1,128]{2,1,0:T(1,128)S(1)}, s32[1,1,128]{2,1,0:T(1,128)}, u32[]{:S(2)}) copy-start(s32[1,1,128]{2,1,0:T(1,128)} %param.11) | copy-start | bytes 1540
  16.8 15.7 %copy-start.5 = (f32[1024]{0:T(1024)S(1)}, f32[1024]{0:T(1024)}, u32[]{:S(2)}) copy-start(f32[1024]{0:T(1024)} %param.12) | copy-start | bytes 12292
  16.8 46.9 %copy-start.7 = (f32[16]{0:T(128)S(1)}, f32[16]{0:T(128)}, u32[]{:S(2)}) copy-start(f32[16]{0:T(128)} %param.15) | copy-start | bytes 196
  16.8 46.9 %copy-start.3 = (f32[1024,16]{0,1:T(8,128)S(1)}, f32[1024,16]{0,1:T(8,128)}, u32[]{:S(2)}) copy-start(f32[1024,16]{0,1:T(8,128)} %param.13) | copy-start | bytes 196612
  32.5 123.4 %reduce-scatter.4.cloned.1.call-start = ((), (), s32[]{:S(2)}) async-start(), calls=%async_computation.4 | async-start | bytes 327680 | tf_op jit(solution)/shard_map/reduce_scatter | solution.py:82
  95.4 12.7 %copy-start.1 = (f32[8192,16]{0,1:T(8,128)}, f32[8192,16]{0,1:T(8,128)S(1)}, u32[]{:S(2)}) copy-start(f32[8192,16]{0,1:T(8,128)S(1)} %all_gather.15) | copy-start | bytes 1572868
  108.9 18.9 %copy-start.4 = (f32[1024,16]{0,1:T(8,128)S(1)}, f32[1024,16]{0,1:T(8,128)}, u32[]{:S(2)}) copy-start(f32[1024,16]{0,1:T(8,128)} %param.8) | copy-start | bytes 196612
  109.0 39.9 %copy-start.6 = (s32[1024]{0:T(1024)S(1)}, s32[1024]{0:T(1024)}, u32[]{:S(2)}) copy-start(s32[1024]{0:T(1024)} %param.9) | copy-start | bytes 12292
  109.0 46.8 %copy-start.2 = (f32[1024,16]{0,1:T(8,128)S(1)}, f32[1024,16]{0,1:T(8,128)}, u32[]{:S(2)}) copy-start(f32[1024,16]{0,1:T(8,128)} %param.14) | copy-start | bytes 196612
  127.8 121.9 %all-reduce.9.cloned.1.call-start = ((), (), s32[]{:S(2)}) async-start(), calls=%async_computation.5 | async-start | bytes 1048576 | tf_op jit(solution)/shard_map/psum | solution.py:75
  127.9 7.0 %collective-permute-start = (f32[1024,16]{0,1:T(8,128)S(1)}, f32[1024,16]{0,1:T(8,128)S(1)}, u32[]{:S(2)}, u32[]{:S(2)}) collective-permute-start(f32[1024,16]{0,1:T(8,128)S(1)} %copy-done.4), channel_id=1, source_target_pairs={{0,4},{4,8},{8,12},{12,16},{16,20},{20,24},{24,28},{28,0},{1,5},{5... | collective-permute-start | bytes 196616 | tf_op jit(solution)/shard_map/ppermute | solution.py:19
  134.9 7.0 %collective-permute-start.1 = (f32[1024,16]{0,1:T(8,128)S(1)}, f32[1024,16]{0,1:T(8,128)S(1)}, u32[]{:S(2)}, u32[]{:S(2)}) collective-permute-start(f32[1024,16]{0,1:T(8,128)S(1)} %collective-permute-done), channel_id=1, source_target_pairs={{0,4},{4,8},{8,12},{12,16},{16,20},{20,24},{24,28},{28,0},{1,5},{5... | collective-permute-start | bytes 196616 | tf_op jit(solution)/shard_map/ppermute | solution.py:19
  141.8 7.0 %collective-permute-start.2 = (f32[1024,16]{0,1:T(8,128)S(1)}, f32[1024,16]{0,1:T(8,128)S(1)}, u32[]{:S(2)}, u32[]{:S(2)}) collective-permute-start(f32[1024,16]{0,1:T(8,128)S(1)} %collective-permute-done.1), channel_id=1, source_target_pairs={{0,4},{4,8},{8,12},{12,16},{16,20},{20,24},{24,28},{28,0},{1,5},{5... | collective-permute-start | bytes 196616 | tf_op jit(solution)/shard_map/ppermute | solution.py:19
  148.8 7.0 %collective-permute-start.3 = (f32[1024,16]{0,1:T(8,128)S(1)}, f32[1024,16]{0,1:T(8,128)S(1)}, u32[]{:S(2)}, u32[]{:S(2)}) collective-permute-start(f32[1024,16]{0,1:T(8,128)S(1)} %collective-permute-done.2), channel_id=1, source_target_pairs={{0,4},{4,8},{8,12},{12,16},{16,20},{20,24},{24,28},{28,0},{1,5},{5... | collective-permute-start | bytes 196616 | tf_op jit(solution)/shard_map/ppermute | solution.py:19
  179.6 111.0 %reduce-scatter.6.cloned.1.call-start = ((), (), s32[]{:S(2)}) async-start(), calls=%async_computation.6 | async-start | bytes 327680 | tf_op jit(solution)/shard_map/reduce_scatter | solution.py:82
  271.3 115.7 %all-reduce.11.cloned.1.call-start = ((), (), s32[]{:S(2)}) async-start(), calls=%async_computation.7 | async-start | bytes 1048576 | tf_op jit(solution)/shard_map/psum | solution.py:75
  298.4 15.7 %copy-start = (f32[8192,16]{0,1:T(8,128)S(1)}, f32[8192,16]{0,1:T(8,128)}, u32[]{:S(2)}) copy-start(f32[8192,16]{0,1:T(8,128)} %get-tuple-element.31) | copy-start | bytes 1572868
  314.1 113.8 %reduce-scatter.8.cloned.1.call-start = ((), (), s32[]{:S(2)}) async-start(), calls=%async_computation.8 | async-start | bytes 327680 | tf_op jit(solution)/shard_map/reduce_scatter | solution.py:82
Sparse Core Ops, SparseCore 0:
  32.6 74.2 all-reduce.6
  127.9 19.2 reduce-scatter.3
  179.7 69.9 all-reduce.8
  271.4 19.2 reduce-scatter.5
  314.2 72.6 all-reduce.10
  408.7 19.2 reduce-scatter.7
where the time goes:
time: 481 us; the launch traced here: 477 us
  blocking collectives  199 us (41%)
  waiting for transfers between devices  140 us (29%)
  matrix products  76.6 us (16%)
  other arithmetic  29.2 us (6%)
  local copies, waits for them, and re-layouts  15.5 us (3%)
  between operations  14.8 us (3%)
    psum x3, blocking collectives, on_device(): dual_square = lax.psum(dual_local, ('band', 'col'))  116 us
    psum x3, waiting for transfers between devices, on_device(): pull_terms = lax.psum(partial_value, 'band')  76.1 us
    dot_general x3, matrix products, forward_part(): jnp.einsum('tij,tjs->tis', matrix_tiles, picked, precision=highest)  46.1 us
    reduce_scatter x3, waiting for transfers between devices, on_device(): lax.psum_scatter(push_part, 'col', scatter_dimension=0, tiled=True)  37.1 us
    all_gather x1, blocking collectives, on_device(): lax.all_gather(primal_init, 'band', axis=0, tiled=True)  31.7 us
    all_gather x1, blocking collectives, on_device(): lax.all_gather(cost_vector, 'band', axis=0, tiled=True)  31.1 us
    dot_general x3, matrix products, backward_part(): jnp.einsum('tij,tis->tjs', matrix_tiles, picked, precision=highest)  28.5 us
    ppermute x4, waiting for transfers between devices, passed_along(): return lax.ppermute(value, axis, pairs)  27.1 us
  transfers between devices with their start and end apart: 10, of which 9 were waited for; matrix products, arithmetic and copies ran while one was open for 1% of the time, Pallas kernels for 0%

commit v1 on v0

v1 whole, which is shorter than its diff:
```python
import jax
import jax.numpy as jnp
from jax import lax
from jax.experimental import pallas as pl
from jax.experimental.pallas import tpu as pltpu
from jax.sharding import PartitionSpec as P

ITERS = 3
LEAD_MAX = 4
GROUP = 32

step_scale = 0.45
return_share = 0.6
epsilon = 1e-06
F32 = jnp.float32
BF16 = jnp.bfloat16


def bit_count(count):
    bits = count.bit_length() - 1
    assert count == 1 << bits and bits >= 2
    return bits


def bit_position(relative, order):
    bits = len(order)
    place = 0
    for step, bit in enumerate(order):
        place = place + (((relative >> bit) & 1) << (bits - 1 - step))
    return place


def exchanged(value, axis, mask):
    count = lax.axis_size(axis)
    return lax.ppermute(value, axis, [(source, source ^ mask) for source in range(count)])


def passed_along(value, axis, steps):
    count = lax.axis_size(axis)
    return lax.ppermute(value, axis, [(source, (source + steps) % count) for source in range(count)])


def halves(value):
    high = value.astype(BF16)
    low = (value - high.astype(F32)).astype(BF16)
    return high, low


def stacked(value):
    high, low = halves(value)
    return jnp.concatenate(
        [jnp.concatenate([high, high], 1), jnp.concatenate([low, low], 1)], 0
    )


def whole_spec(array):
    rank = len(array.shape)
    return pl.BlockSpec(array.shape, lambda step, *refs: (0,) * rank)


def call_once(body, inputs, outputs):
    return pl.pallas_call(
        body, out_shape=[jax.ShapeDtypeStruct(shape, F32) for shape in outputs]
    )(*inputs)


def to_units(block, tile):
    return [block[:, k * tile : (k + 1) * tile] for k in range(block.shape[1] // tile)]


def prepare(dual_rows, primal_rows, cost, tile):
    scen, rows = dual_rows.shape
    sub = rows // tile

    def body(dual_ref, primal_ref, cost_ref, units_ref, message_ref):
        for k in range(sub):
            lanes = slice(k * tile, (k + 1) * tile)
            units_ref[k] = dual_ref[:, lanes]
            message_ref[k] = primal_ref[:, lanes]
        message_ref[sub] = jnp.zeros((scen, tile), F32)
        message_ref[sub, :sub, :] = cost_ref[...]

    return call_once(
        body,
        (dual_rows, primal_rows, cost),
        ((sub, scen, tile), (sub + 1, scen, tile)),
    )


def right_side_of(demand_rows, earlier, lead, tile):
    scen, rows = demand_rows.shape
    sub = rows // tile

    def body(demand_ref, *refs):
        lead_ref, out_ref = refs[-2:]
        for k in range(sub):
            lanes = slice(k * tile, (k + 1) * tile)
            wanted = lead_ref[k : k + 1, :]
            lagged = jnp.zeros((scen, tile), F32)
            for steps in range(1, LEAD_MAX + 1):
                lagged = jnp.where(wanted == steps, refs[steps - 1][:, lanes], lagged)
            out_ref[k] = demand_ref[:, lanes] - return_share * lagged

    return call_once(body, (demand_rows, *earlier, lead), ((sub, scen, tile),))[0]


def backward_kernel(index, own, other, matrix_tiles, order_a, order_b, sub):
    count, tile, _ = matrix_tiles.shape
    scen = own.shape[1]
    half_scen = scen // 2
    per_half = own.shape[0] - 1
    chunks = 1 << len(order_a)
    units = chunks * sub
    half = units // 2
    group = min(GROUP, count)

    def body(index_ref, own_ref, other_ref, tiles_ref, *refs):
        send_a, keep_a, send_b, keep_b, total, operand = refs
        step = pl.program_id(0)

        @pl.when(step == 0)
        def _():
            total[...] = jnp.zeros_like(total)
            for u in range(per_half):
                operand[u] = stacked(own_ref[u])
                operand[per_half + u] = stacked(other_ref[u])

        for k in range(group):
            t = step * group + k
            row = index_ref[t]
            column = index_ref[count + t]
            high, low = halves(tiles_ref[k])
            product = lax.dot_general(
                operand[row],
                jnp.concatenate([high, low], 0),
                (((1,), (0,)), ((), ())),
                preferred_element_type=F32,
            )
            total[column] += product[:scen] + product[scen:]

        @pl.when(step == pl.num_programs(0) - 1)
        def _():
            for relative in range(chunks):
                place_a = bit_position(relative, order_a) * sub
                place_b = bit_position(relative, order_b) * sub
                for k in range(sub):
                    value = total[place_a + k]
                    for place, send, keep, part in (
                        (place_a + k, send_a, keep_a, value[:half_scen]),
                        (place_b + k, send_b, keep_b, value[half_scen:]),
                    ):
                        if place >= half:
                            send[place - half] = part
                        else:
                            keep[place] = part
            square = own_ref[per_half] + other_ref[per_half]
            send_a[half] = square[:half_scen]
            send_b[half] = square[half_scen:]

    shapes = [(half + 1, half_scen, tile), (half, half_scen, tile)] * 2
    outs = [jax.ShapeDtypeStruct(shape, F32) for shape in shapes]
    return pl.pallas_call(
        body,
        out_shape=outs,
        grid_spec=pltpu.PrefetchScalarGridSpec(
            num_scalar_prefetch=1,
            grid=(count // group,),
            in_specs=[
                whole_spec(own),
                whole_spec(other),
                pl.BlockSpec((group, tile, tile), lambda step, refs: (step, 0, 0)),
            ],
            out_specs=[whole_spec(out) for out in outs],
            scratch_shapes=[
                pltpu.VMEM((units, scen, tile), F32),
                pltpu.VMEM((2 * per_half, 2 * scen, 2 * tile), BF16),
            ],
        ),
        compiler_params=pltpu.CompilerParams(dimension_semantics=("arbitrary",)),
    )(index, own, other, matrix_tiles)


def forward_kernel(index, parts, matrix_tiles, order_a, order_b, units_row, sub):
    count, tile, _ = matrix_tiles.shape
    half_scen = parts[0].shape[1]
    scen = 2 * half_scen
    per_half = parts[0].shape[0] - 1
    chunks = 1 << len(order_a)
    half = units_row // 2
    group = min(GROUP, count)

    def body(index_ref, own_a, other_a, own_b, other_b, tiles_ref, *refs):
        send, keep, total, operand = refs
        step = pl.program_id(0)

        def unit(own, other, place):
            return other[place - per_half] if place >= per_half else own[place]

        @pl.when(step == 0)
        def _():
            total[...] = jnp.zeros_like(total)
            for relative in range(chunks):
                place_a = bit_position(relative, order_a) * sub
                place_b = bit_position(relative, order_b) * sub
                for k in range(sub):
                    value = jnp.concatenate(
                        [unit(own_a, other_a, place_a + k), unit(own_b, other_b, place_b + k)], 0
                    )
                    operand[place_a + k] = stacked(value)

        for k in range(group):
            t = step * group + k
            row = index_ref[t]
            column = index_ref[count + t]
            high, low = halves(tiles_ref[k])
            product = lax.dot_general(
                operand[column],
                jnp.concatenate([high, low], 1),
                (((1,), (1,)), ((), ())),
                preferred_element_type=F32,
            )
            total[row] += product[:scen] + product[scen:]

        @pl.when(step == pl.num_programs(0) - 1)
        def _():
            for u in range(half):
                keep[u] = total[u]
                send[u] = total[half + u]
            send[half, :half_scen, :] = own_a[per_half] + other_a[per_half]
            send[half, half_scen:, :] = own_b[per_half] + other_b[per_half]

    outs = [
        jax.ShapeDtypeStruct((half + 1, scen, tile), F32),
        jax.ShapeDtypeStruct((half, scen, tile), F32),
    ]
    return pl.pallas_call(
        body,
        out_shape=outs,
        grid_spec=pltpu.PrefetchScalarGridSpec(
            num_scalar_prefetch=1,
            grid=(count // group,),
            in_specs=[whole_spec(part) for part in parts]
            + [pl.BlockSpec((group, tile, tile), lambda step, refs: (step, 0, 0))],
            out_specs=[whole_spec(out) for out in outs],
            scratch_shapes=[
                pltpu.VMEM((units_row, scen, tile), F32),
                pltpu.VMEM((chunks * sub, 2 * scen, 2 * tile), BF16),
            ],
        ),
        compiler_params=pltpu.CompilerParams(dimension_semantics=("arbitrary",)),
    )(index, *parts, matrix_tiles)


def next_weight(weight, primal_square, dual_square):
    primal_sum = jnp.sum(primal_square, axis=-1, keepdims=True)
    dual_sum = jnp.sum(dual_square, axis=-1, keepdims=True)
    ratio = (primal_sum + epsilon) / (dual_sum + epsilon)
    return jnp.sqrt(weight * jnp.sqrt(ratio))


def primal_update(own, other, start_own, start_other, primal, weight, primal_square, sub, last):
    _, scen, tile = own.shape
    half_scen = scen // 2
    first = primal is None

    def body(*refs):
        refs = list(refs)
        own_ref, other_ref, start_refs = refs[0], refs[1], refs[2:4]
        weight_ref = refs[4]
        rest = refs[5:]
        if not first:
            primal_ref, square_ref = rest[:2]
            rest = rest[2:]
        new_ref, message_a, message_b = rest[:3]
        rest = rest[3:]
        weight_now = weight_ref[...]
        if not first:
            weight_now = next_weight(
                weight_now, square_ref[...], own_ref[2 * sub] + other_ref[2 * sub]
            )
            rest[0][...] = weight_now
            rest = rest[1:]
        primal_step = step_scale / weight_now
        squares = []
        for chunk in range(2):
            square = jnp.zeros((scen, tile), F32)
            for k in range(sub):
                here = chunk * sub + k
                pull = own_ref[here] + other_ref[(1 - chunk) * sub + k]
                before = start_refs[chunk][k] if first else primal_ref[here]
                cost = start_refs[chunk][sub, k : k + 1, :]
                after = jnp.maximum(before - primal_step * (cost - pull), 0.0)
                change = after - before
                square = square + change * change
                new_ref[here] = after
                ahead = 2.0 * after - before
                message_a[here] = ahead[:half_scen]
                message_b[here] = ahead[half_scen:]
                if last and chunk == 0:
                    rest[0][:, k * tile : (k + 1) * tile] = after
            squares.append(square)
        square = squares[0] + squares[1]
        message_a[2 * sub] = square[:half_scen]
        message_b[2 * sub] = square[half_scen:]

    inputs = [own, other, start_own, start_other, weight]
    outputs = [(2 * sub, scen, tile)] + [(2 * sub + 1, half_scen, tile)] * 2
    if not first:
        inputs += [primal, primal_square]
        outputs.append((scen, tile))
    if last:
        outputs.append((scen, sub * tile))
    return call_once(body, inputs, outputs)


def dual_update(own, other, duals, rights, weight, sub, last):
    _, scen, tile = own.shape
    pair = isinstance(duals, tuple)
    given = list(duals) if pair else [duals]

    def body(*refs):
        refs = list(refs)
        own_ref, other_ref, weight_ref = refs[:3]
        right_refs = refs[3:5]
        dual_refs = refs[5 : 5 + len(given)]
        rest = refs[5 + len(given) :]
        message, square_ref = rest[:2]
        square_ref[...] = own_ref[2 * sub] + other_ref[2 * sub]
        dual_step = step_scale * weight_ref[...]
        squares = []
        for chunk in range(2):
            square = jnp.zeros((scen, tile), F32)
            for k in range(sub):
                here = chunk * sub + k
                push = own_ref[here] + other_ref[(1 - chunk) * sub + k]
                before = dual_refs[chunk][k] if pair else dual_refs[0][here]
                after = before + dual_step * (right_refs[chunk][k] - push)
                change = after - before
                square = square + change * change
                message[here] = after
                if last and chunk == 0:
                    rest[2][:, k * tile : (k + 1) * tile] = after
            squares.append(square)
        message[2 * sub] = squares[0] + squares[1]

    outputs = [(2 * sub + 1, scen, tile), (scen, tile)]
    if last:
        outputs.append((scen, sub * tile))
    return call_once(body, [own, other, weight, *rights, *given], outputs)


def folded(send, keep, received):
    return keep + received[:-1], send[-1:] + received[-1:]


def on_device(
    demand, lead_periods, matrix_tiles, tile_pos, cost_vector, primal_init, dual_init, weight_init
):
    band_bits = bit_count(lax.axis_size("band"))
    col_bits = bit_count(lax.axis_size("col"))
    assert col_bits == 2
    matrix_tiles = matrix_tiles.reshape(matrix_tiles.shape[2:])
    positions = tile_pos.reshape(-1)
    tile = matrix_tiles.shape[-1]
    block_rows, scen = demand.shape
    sub = block_rows // tile
    units_col = sub << band_bits
    units_row = sub << col_bits
    order_a = tuple(range(band_bits))
    order_b = (1, 0) + order_a[2:]
    order_col = tuple(range(col_bits))

    def place_of(unit, axis, order):
        relative = (unit // sub) ^ lax.axis_index(axis)
        return bit_position(relative, order) * sub + unit % sub

    index = jnp.concatenate(
        [
            place_of(positions // units_col, "col", order_col),
            place_of(positions % units_col, "band", order_a),
        ]
    )
    demand_rows = demand.T
    dual_units, start_own = prepare(
        dual_init.T, primal_init.T, cost_vector.reshape(sub, tile), tile
    )
    dual_other = exchanged(dual_units, "col", 1 << order_col[-1])
    message = jnp.concatenate([dual_units, dual_other, jnp.zeros((1, scen, tile), F32)])
    start_other = exchanged(start_own, "band", 1 << order_a[-1])
    earlier = [passed_along(demand_rows, "band", steps) for steps in range(1, LEAD_MAX + 1)]
    right_own = right_side_of(demand_rows, earlier, lead_periods.reshape(sub, tile), tile)
    right_other = exchanged(right_own, "col", 1 << order_col[-1])
    duals = (dual_units, dual_other)
    weight = jnp.broadcast_to(weight_init[:, None], (scen, tile))
    primal = None
    primal_square = None
    for iteration in range(ITERS):
        last = iteration == ITERS - 1
        other = exchanged(message, "col", 1 << order_col[0])
        send_a, keep_a, send_b, keep_b = backward_kernel(
            index, message, other, matrix_tiles, order_a, order_b, sub
        )
        got_a = exchanged(send_a, "band", 1 << order_a[0])
        got_b = exchanged(send_b, "band", 1 << order_b[0])
        sides = []
        for order, send, keep, got in (
            (order_a, send_a, keep_a, got_a),
            (order_b, send_b, keep_b, got_b),
        ):
            total, square = folded(send, keep, got)
            half = total.shape[0] // 2
            sides.append((order[1], jnp.concatenate([total[half:], square]), total[:half]))
        sides = [
            folded(send, keep, exchanged(send, "band", 1 << bit)) for bit, send, keep in sides
        ]
        total, square = (jnp.concatenate(pair, 1) for pair in zip(*sides))
        for bit in order_a[2:-1]:
            half = total.shape[0] // 2
            send, keep = jnp.concatenate([total[half:], square]), total[:half]
            total, square = folded(send, keep, exchanged(send, "band", 1 << bit))
        own = jnp.concatenate([total, square])
        results = primal_update(
            own,
            exchanged(own, "band", 1 << order_a[-1]),
            start_own,
            start_other,
            primal,
            weight,
            primal_square,
            sub,
            last,
        )
        primal, ahead_a, ahead_b = results[:3]
        if iteration:
            weight = results[3]
        if last:
            primal_rows = results[-1]
        ahead = [ahead_a, ahead_b]
        for place in range(band_bits - 2, 0, -1):
            joined = []
            for order, own in zip((order_a, order_b), ahead):
                got = exchanged(own, "band", 1 << order[place])
                joined.append(
                    jnp.concatenate([own[:-1], got[:-1], own[-1:] + got[-1:]])
                )
            ahead = joined
        parts = []
        for order, own in zip((order_a, order_b), ahead):
            parts += [own, exchanged(own, "band", 1 << order[0])]
        send, keep = forward_kernel(index, parts, matrix_tiles, order_a, order_b, units_row, sub)
        total, square = folded(send, keep, exchanged(send, "col", 1 << order_col[0]))
        own = jnp.concatenate([total, square])
        results = dual_update(
            own,
            exchanged(own, "col", 1 << order_col[1]),
            duals,
            (right_own, right_other),
            weight,
            sub,
            last,
        )
        message, primal_square = results[:2]
        duals = message
        if last:
            dual_rows = results[2]
    square = message[-1]
    square = square + exchanged(square, "col", 1 << order_col[0])
    for bit in order_a:
        square = square + exchanged(square, "band", 1 << bit)
    weight = next_weight(weight, primal_square, square)[:, 0]
    return (primal_rows.T, dual_rows.T, weight)


def solution(mesh):
    in_specs = (
        P(("band", "col"), None),
        P(("band", "col")),
        P("band", "col", None, None, None),
        P("band", "col", None),
        P(("band", "col")),
        P(("band", "col"), None),
        P(("band", "col"), None),
        P(),
    )
    out_specs = (P(("band", "col"), None), P(("band", "col"), None), P())
    return jax.shard_map(
        on_device, mesh=mesh, in_specs=in_specs, out_specs=out_specs, check_vma=False
    )
```

time: 481 us -> 243 us (0.51)
  blocking collectives: 199 us -> 0 us
  matrix products: 76.6 us -> 0 us
  Pallas kernels: 0 us -> 56 us
  starting transfers between devices: 1.03 us -> 38.7 us
  waiting for transfers between devices: 140 us -> 107 us
  between operations: 14.8 us -> 1.15 us
  other arithmetic: 29.2 us -> 23.3 us
    psum x3 -> x0, blocking collectives: 116 us -> none  [on_device(): dual_square = lax.psum(dual_local, ('band', 'col'))]
    all_gather x5 -> x0, blocking collectives: 82.6 us -> none  [the longest x1 31.7 us: on_device(): lax.all_gather(primal_init, 'band', axis=0, tiled=True)]
    ppermute x4 -> x47, waiting for transfers between devices: 27.1 us -> 107 us  [the longest x43 99.2 us: exchanged(): lax.ppermute(value, axis, [(source, source ^ mask) for source in range(co...]
    dot_general x9 -> x0, matrix products: 76.6 us -> none  [the longest x3 46.1 us: forward_part(): jnp.einsum('tij,tjs->tis', matrix_tiles, picked, precision=highest)]
    psum x3 -> x0, waiting for transfers between devices: 76.1 us -> none  [on_device(): pull_terms = lax.psum(partial_value, 'band')]
    pallas_call x0 -> x14, Pallas kernels: none -> 56 us  [the longest x3 22.4 us: forward_kernel(): pl.pallas_call(body, out_shape=outs, grid_spec=pltpu.PrefetchScalarGridSp...]
    ppermute x4 -> x47, starting transfers between devices: 0.79 us -> 38.7 us  [the longest x43 34.2 us: exchanged(): lax.ppermute(value, axis, [(source, source ^ mask) for source in range(co...]
    reduce_scatter x3 -> x0, waiting for transfers between devices: 37.1 us -> none  [on_device(): lax.psum_scatter(push_part, 'col', scatter_dimension=0, tiled=True)]
  transfers between devices with their start and end apart: 10 -> 47, of which waited for: 9 -> 39; matrix products, arithmetic and copies ran while one was open for 1% -> 9% of each run, Pallas kernels for 0% -> 1%
where the time goes in v1:
time: 243 us; the launch traced here: 241 us
  waiting for transfers between devices  107 us (44%)
  Pallas kernels  56 us (23%)
  starting transfers between devices  38.7 us (16%)
  other arithmetic  23.3 us (10%)
  local copies, waits for them, and re-layouts  15.2 us (6%)
    ppermute x43, waiting for transfers between devices, exchanged(): lax.ppermute(value, axis, [(source, source ^ mask) for source in range(co...  99.2 us
    ppermute x43, starting transfers between devices, exchanged(): lax.ppermute(value, axis, [(source, source ^ mask) for source in range(co...  34.2 us
    pallas_call x3, Pallas kernels, forward_kernel(): pl.pallas_call(body, out_shape=outs, grid_spec=pltpu.PrefetchScalarGridSp...  22.4 us
    pallas_call x3, Pallas kernels, backward_kernel(): pl.pallas_call(body, out_shape=outs, grid_spec=pltpu.PrefetchScalarGridSp...  19.4 us
    add x30, other arithmetic, folded(): return (keep + received[:-1], send[-1:] + received[-1:])  14.5 us
    pallas_call x8, Pallas kernels, call_once(): pl.pallas_call(body, out_shape=[jax.ShapeDtypeStruct(shape, F32) for shap...  14.3 us
    unnamed x78, local copies, waits for them, and re-layouts  8.51 us
    ppermute x4, waiting for transfers between devices, passed_along(): lax.ppermute(value, axis, [(source, (source + steps) % count) for source...  7.54 us
  transfers between devices with their start and end apart: 47, of which 39 were waited for; matrix products, arithmetic and copies ran while one was open for 9% of the time, Pallas kernels for 1%

profile of v1, /device:TPU:0, one launch (start us, length us, event | category | flops | bytes accessed | tf_op | source)
XLA Modules:
  0.0 241.1 jit_solution(13630702915844981294)
XLA Ops:
  2.2 3.0 %collective-permute-start = (f32[8,16,128]{2,1,0:T(8,128)}, f32[8,16,128]{2,1,0:T(8,128)S(1)}, u32[]{:S(2)}, u32[]{:S(2)}) collective-permute-start(f32[8,16,128]{2,1,0:T(8,128)} %get-tuple-element.41.refs_5_), channel_id=1, source_target_pairs={{0,2},{1,3},{2,0},{3,1},{4,6},{5,7},{6,4},{7,5},{8,10},{9,11},{10,... | collective-permute-start | bytes 196616 | tf_op jit(solution)/shard_map/ppermute | solution.py:35
  5.2 2.4 collective-permute-done.refs_6_
  10.6 6.5 %shard_map.104 = (f32[33,8,128]{2,1,0:T(8,128)}, f32[32,8,128]{2,1,0:T(8,128)}, f32[33,8,128]{2,1,0:T(8,128)}, f32[32,8,128]{2,1,0:T(8,128)}) custom-call(s32[256]{0:T(256)} %pad_add_fusion.index_ref, f32[17,16,128]{2,1,0:T(8,128)} %copy-done.3, f32[17,16,128]{2,1,0:T(8,128)} %copy-done.17, f32[128,128,128]{2,1,0:T(8,128)} %bitcast.30), custom_call_target="tpu_custom_call" | custom-call | tf_op jit(solution)/shard_map/pallas_call | solution.py:162
  17.1 2.1 collective-permute-start.2
  20.7 2.7 %collective-permute-done.2 = f32[33,8,128]{2,1,0:T(8,128)S(1)} collective-permute-done((f32[33,8,128]{2,1,0:T(8,128)}, f32[33,8,128]{2,1,0:T(8,128)S(1)}, u32[]{:S(2)}, u32[]{:S(2)}) %collective-permute-start.2) | collective-permute-done | bytes 135200 | tf_op jit(solution)/shard_map/ppermute | solution.py:35
  30.2 2.8 %collective-permute-done.5 = f32[17,8,128]{2,1,0:T(8,128)S(1)} collective-permute-done((f32[17,8,128]{2,1,0:T(8,128)S(1)}, f32[17,8,128]{2,1,0:T(8,128)S(1)}, u32[]{:S(2)}, u32[]{:S(2)}) %collective-permute-start.5) | collective-permute-done | bytes 69664 | tf_op jit(solution)/shard_map/ppermute | solution.py:35
  33.0 2.7 %collective-permute-start.6 = (f32[17,16,128]{2,1,0:T(8,128)S(1)}, f32[17,16,128]{2,1,0:T(8,128)S(1)}, u32[]{:S(2)}, u32[]{:S(2)}) collective-permute-start(f32[17,16,128]{2,1,0:T(8,128)S(1)} %maximum_maximum_fusion.1.refs_0_), channel_id=1, source_target_pairs={{0,16},{4,20},{8,24},{12,28},{16,0},{20,4},{24,8},{28,12},{1,17},{... | collective-permute-start | bytes 417800 | tf_op jit(solution)/shard_map/ppermute | solution.py:35
  36.0 7.7 %collective-permute-done.7.refs_3_ = f32[9,16,128]{2,1,0:T(8,128)S(1)} collective-permute-done((f32[9,16,128]{2,1,0:T(8,128)S(1)}, f32[9,16,128]{2,1,0:T(8,128)S(1)}, u32[]{:S(2)}, u32[]{:S(2)}) %collective-permute-start.7) | collective-permute-done | bytes 73760 | tf_op jit(solution)/shard_map/ppermute | solution.py:35
  52.2 2.2 collective-permute-done.8
  56.5 3.7 %collective-permute-done.9.other_a = f32[33,8,128]{2,1,0:T(8,128)S(1)} collective-permute-done((f32[33,8,128]{2,1,0:T(8,128)S(1)}, f32[33,8,128]{2,1,0:T(8,128)S(1)}, u32[]{:S(2)}, u32[]{:S(2)}) %collective-permute-start.9) | collective-permute-done | bytes 135200 | tf_op jit(solution)/shard_map/ppermute | solution.py:35
  60.9 7.4 %shard_map.106 = (f32[17,16,128]{2,1,0:T(8,128)}, f32[16,16,128]{2,1,0:T(8,128)}) custom-call(s32[256]{0:T(256)} %pad_add_fusion.index_ref, f32[33,8,128]{2,1,0:T(8,128)} %copy-done.14, f32[33,8,128]{2,1,0:T(8,128)} %copy-done.30, f32[33,8,128]{2,1,0:T(8,128)} %copy-done.11, f32[33,8,128]{2,1,0:T(8,128)} %copy-done.27, f32[128,128,128]{2,1,0:T(8,128)} %bitcast.31), custom_call_target="tpu_custom_call" | custom-call | tf_op jit(solution)/shard_map/pallas_call | solution.py:236
  74.5 2.0 collective-permute-start.16
  77.5 2.1 collective-permute-done.17.refs_3_
  79.6 5.4 %collective-permute-done.16.refs_2_ = f32[16,1024]{1,0:T(8,128)S(1)} collective-permute-done((f32[16,1024]{1,0:T(8,128)S(1)}, f32[16,1024]{1,0:T(8,128)S(1)}, u32[]{:S(2)}, u32[]{:S(2)}) %collective-permute-start.16) | collective-permute-done | bytes 65568 | tf_op jit(solution)/shard_map/ppermute | solution.py:40
  87.9 3.9 %collective-permute-done.18.refs_4_ = f32[8,16,128]{2,1,0:T(8,128)S(1)} collective-permute-done((f32[8,16,128]{2,1,0:T(8,128)}, f32[8,16,128]{2,1,0:T(8,128)S(1)}, u32[]{:S(2)}, u32[]{:S(2)}) %collective-permute-start.18) | collective-permute-done | bytes 65568 | tf_op jit(solution)/shard_map/ppermute | solution.py:35
  97.1 6.4 %shard_map.109 = (f32[33,8,128]{2,1,0:T(8,128)}, f32[32,8,128]{2,1,0:T(8,128)}, f32[33,8,128]{2,1,0:T(8,128)}, f32[32,8,128]{2,1,0:T(8,128)}) custom-call(s32[256]{0:T(256)} %pad_add_fusion.index_ref, f32[17,16,128]{2,1,0:T(8,128)} %get-tuple-element.51.own_ref.refs_5_, f32[17,16,128]{2,1,0:T(8,128)} %copy-done.18, f32[128,128,128]{2,1,0:T(8,128)} %bitcast.32), custom_call_target="tpu_custom_call" | custom-call | tf_op jit(solution)/shard_map/pallas_call | solution.py:162
  103.6 5.8 %collective-permute-done.20 = f32[33,8,128]{2,1,0:T(8,128)S(1)} collective-permute-done((f32[33,8,128]{2,1,0:T(8,128)}, f32[33,8,128]{2,1,0:T(8,128)S(1)}, u32[]{:S(2)}, u32[]{:S(2)}) %collective-permute-start.20) | collective-permute-done | bytes 135200 | tf_op jit(solution)/shard_map/ppermute | solution.py:35
  113.1 2.3 collective-permute-done.21
  118.6 6.4 %collective-permute-done.24.refs_1_ = f32[17,16,128]{2,1,0:T(8,128)S(1)} collective-permute-done((f32[17,16,128]{2,1,0:T(8,128)S(1)}, f32[17,16,128]{2,1,0:T(8,128)S(1)}, u32[]{:S(2)}, u32[]{:S(2)}) %collective-permute-start.24) | collective-permute-done | bytes 139296 | tf_op jit(solution)/shard_map/ppermute | solution.py:35
  129.9 2.3 collective-permute-done.27
  140.7 7.4 %shard_map.111 = (f32[17,16,128]{2,1,0:T(8,128)}, f32[16,16,128]{2,1,0:T(8,128)}) custom-call(s32[256]{0:T(256)} %pad_add_fusion.index_ref, f32[33,8,128]{2,1,0:T(8,128)} %copy-done.15, f32[33,8,128]{2,1,0:T(8,128)} %copy-done.31, f32[33,8,128]{2,1,0:T(8,128)} %copy-done.12, f32[33,8,128]{2,1,0:T(8,128)} %copy-done.28, f32[128,128,128]{2,1,0:T(8,128)} %bitcast.33), custom_call_target="tpu_custom_call" | custom-call | tf_op jit(solution)/shard_map/pallas_call | solution.py:236
  151.9 5.2 %collective-permute-done.30.refs_1_ = f32[17,16,128]{2,1,0:T(8,128)S(1)} collective-permute-done((f32[17,16,128]{2,1,0:T(8,128)S(1)}, f32[17,16,128]{2,1,0:T(8,128)S(1)}, u32[]{:S(2)}, u32[]{:S(2)}) %collective-permute-start.30) | collective-permute-done | bytes 139296 | tf_op jit(solution)/shard_map/ppermute | solution.py:35
  161.8 6.5 %shard_map.113 = (f32[33,8,128]{2,1,0:T(8,128)}, f32[32,8,128]{2,1,0:T(8,128)}, f32[33,8,128]{2,1,0:T(8,128)}, f32[32,8,128]{2,1,0:T(8,128)}) custom-call(s32[256]{0:T(256)} %pad_add_fusion.index_ref, f32[17,16,128]{2,1,0:T(8,128)} %get-tuple-element.63.own_ref.refs_5_, f32[17,16,128]{2,1,0:T(8,128)} %copy-done.19, f32[128,128,128]{2,1,0:T(8,128)} %bitcast.34), custom_call_target="tpu_custom_call" | custom-call | tf_op jit(solution)/shard_map/pallas_call | solution.py:162
  170.2 3.9 %collective-permute-done.32 = f32[33,8,128]{2,1,0:T(8,128)S(1)} collective-permute-done((f32[33,8,128]{2,1,0:T(8,128)}, f32[33,8,128]{2,1,0:T(8,128)S(1)}, u32[]{:S(2)}, u32[]{:S(2)}) %collective-permute-start.32) | collective-permute-done | bytes 135200 | tf_op jit(solution)/shard_map/ppermute | solution.py:35
  180.2 2.5 %collective-permute-done.35 = f32[17,8,128]{2,1,0:T(8,128)S(1)} collective-permute-done((f32[17,8,128]{2,1,0:T(8,128)S(1)}, f32[17,8,128]{2,1,0:T(8,128)S(1)}, u32[]{:S(2)}, u32[]{:S(2)}) %collective-permute-start.35) | collective-permute-done | bytes 69664 | tf_op jit(solution)/shard_map/ppermute | solution.py:35
  184.6 5.6 %collective-permute-done.36.refs_1_ = f32[17,16,128]{2,1,0:T(8,128)S(1)} collective-permute-done((f32[17,16,128]{2,1,0:T(8,128)S(1)}, f32[17,16,128]{2,1,0:T(8,128)S(1)}, u32[]{:S(2)}, u32[]{:S(2)}) %collective-permute-start.36) | collective-permute-done | bytes 139296 | tf_op jit(solution)/shard_map/ppermute | solution.py:35
  203.1 3.1 %collective-permute-done.38.other_a = f32[33,8,128]{2,1,0:T(8,128)S(1)} collective-permute-done((f32[33,8,128]{2,1,0:T(8,128)S(1)}, f32[33,8,128]{2,1,0:T(8,128)S(1)}, u32[]{:S(2)}, u32[]{:S(2)}) %collective-permute-start.38) | collective-permute-done | bytes 135200 | tf_op jit(solution)/shard_map/ppermute | solution.py:35
  206.9 7.5 %shard_map.115 = (f32[17,16,128]{2,1,0:T(8,128)}, f32[16,16,128]{2,1,0:T(8,128)}) custom-call(s32[256]{0:T(256)} %pad_add_fusion.index_ref, f32[33,8,128]{2,1,0:T(8,128)} %copy-done.13, f32[33,8,128]{2,1,0:T(8,128)} %copy-done.29, f32[33,8,128]{2,1,0:T(8,128)} %copy-done.10, f32[33,8,128]{2,1,0:T(8,128)} %copy-done.26, f32[128,128,128]{2,1,0:T(8,128)} %bitcast.35), custom_call_target="tpu_custom_call" | custom-call | tf_op jit(solution)/shard_map/pallas_call | solution.py:236
  218.2 5.2 %collective-permute-done.42.refs_1_ = f32[17,16,128]{2,1,0:T(8,128)S(1)} collective-permute-done((f32[17,16,128]{2,1,0:T(8,128)S(1)}, f32[17,16,128]{2,1,0:T(8,128)S(1)}, u32[]{:S(2)}, u32[]{:S(2)}) %collective-permute-start.42) | collective-permute-done | bytes 139296 | tf_op jit(solution)/shard_map/ppermute | solution.py:35
  229.1 3.0 %collective-permute-done.44 = f32[16,128]{1,0:T(8,128)S(1)} collective-permute-done((f32[16,128]{1,0:T(8,128)S(1)}, f32[16,128]{1,0:T(8,128)S(1)}, u32[]{:S(2)}, u32[]{:S(2)}) %collective-permute-start.44) | collective-permute-done | bytes 8224 | tf_op jit(solution)/shard_map/ppermute | solution.py:35
  232.3 3.5 %collective-permute-done.45 = f32[16,128]{1,0:T(8,128)S(1)} collective-permute-done((f32[16,128]{1,0:T(8,128)S(1)}, f32[16,128]{1,0:T(8,128)S(1)}, u32[]{:S(2)}, u32[]{:S(2)}) %collective-permute-start.45) | collective-permute-done | bytes 8224 | tf_op jit(solution)/shard_map/ppermute | solution.py:35
  237.2 3.1 %collective-permute-done.46 = f32[16,128]{1,0:T(8,128)S(1)} collective-permute-done((f32[16,128]{1,0:T(8,128)S(1)}, f32[16,128]{1,0:T(8,128)S(1)}, u32[]{:S(2)}, u32[]{:S(2)}) %collective-permute-start.46) | collective-permute-done | bytes 8224 | tf_op jit(solution)/shard_map/ppermute | solution.py:35
  (239 shorter events, 103.7 us)
Async XLA Ops:
  2.2 5.4 %collective-permute-start = (f32[8,16,128]{2,1,0:T(8,128)}, f32[8,16,128]{2,1,0:T(8,128)S(1)}, u32[]{:S(2)}, u32[]{:S(2)}) collective-permute-start(f32[8,16,128]{2,1,0:T(8,128)} %get-tuple-element.41.refs_5_), channel_id=1, source_target_pairs={{0,2},{1,3},{2,0},{3,1},{4,6},{5,7},{6,4},{7,5},{8,10},{9,11},{10,... | collective-permute-start | bytes 196616 | tf_op jit(solution)/shard_map/ppermute | solution.py:35
  17.1 6.4 %collective-permute-start.2 = (f32[33,8,128]{2,1,0:T(8,128)}, f32[33,8,128]{2,1,0:T(8,128)S(1)}, u32[]{:S(2)}, u32[]{:S(2)}) collective-permute-start(f32[33,8,128]{2,1,0:T(8,128)} %get-tuple-element.43), channel_id=1, source_target_pairs={{0,4},{4,0},{8,12},{12,8},{16,20},{20,16},{24,28},{28,24},{1,5},{5... | collective-permute-start | bytes 405512 | tf_op jit(solution)/shard_map/ppermute | solution.py:35
  19.2 7.8 %collective-permute-start.4 = (f32[33,8,128]{2,1,0:T(8,128)}, f32[33,8,128]{2,1,0:T(8,128)S(1)}, u32[]{:S(2)}, u32[]{:S(2)}) collective-permute-start(f32[33,8,128]{2,1,0:T(8,128)} %get-tuple-element.45), channel_id=1, source_target_pairs={{0,8},{4,12},{8,0},{12,4},{16,24},{20,28},{24,16},{28,20},{1,9},{5... | collective-permute-start | bytes 405512 | tf_op jit(solution)/shard_map/ppermute | solution.py:35
  25.1 5.1 %collective-permute-start.3 = (f32[17,8,128]{2,1,0:T(8,128)S(1)}, f32[17,8,128]{2,1,0:T(8,128)S(1)}, u32[]{:S(2)}, u32[]{:S(2)}) collective-permute-start(f32[17,8,128]{2,1,0:T(8,128)S(1)} %pad_maximum_fusion.9), channel_id=1, source_target_pairs={{0,8},{4,12},{8,0},{12,4},{16,24},{20,28},{24,16},{28,20},{1,9},{5... | collective-permute-start | bytes 208904 | tf_op jit(solution)/shard_map/ppermute | solution.py:35
  33.0 10.7 %collective-permute-start.6 = (f32[17,16,128]{2,1,0:T(8,128)S(1)}, f32[17,16,128]{2,1,0:T(8,128)S(1)}, u32[]{:S(2)}, u32[]{:S(2)}) collective-permute-start(f32[17,16,128]{2,1,0:T(8,128)S(1)} %maximum_maximum_fusion.1.refs_0_), channel_id=1, source_target_pairs={{0,16},{4,20},{8,24},{12,28},{16,0},{20,4},{24,8},{28,12},{1,17},{... | collective-permute-start | bytes 417800 | tf_op jit(solution)/shard_map/ppermute | solution.py:35
  35.7 8.1 %collective-permute-start.7 = (f32[9,16,128]{2,1,0:T(8,128)S(1)}, f32[9,16,128]{2,1,0:T(8,128)S(1)}, u32[]{:S(2)}, u32[]{:S(2)}) collective-permute-start(f32[9,16,128]{2,1,0:T(8,128)S(1)} %copy-done), channel_id=1, source_target_pairs={{0,16},{4,20},{8,24},{12,28},{16,0},{20,4},{24,8},{28,12},{1,17},{... | collective-permute-start | bytes 221192 | tf_op jit(solution)/shard_map/ppermute | solution.py:35
  46.2 4.5 %collective-permute-start.10 = (f32[17,8,128]{2,1,0:T(8,128)}, f32[17,8,128]{2,1,0:T(8,128)S(1)}, u32[]{:S(2)}, u32[]{:S(2)}) collective-permute-start(f32[17,8,128]{2,1,0:T(8,128)} %get-tuple-element.48), channel_id=1, source_target_pairs={{0,4},{4,0},{8,12},{12,8},{16,20},{20,16},{24,28},{28,24},{1,5},{5... | collective-permute-start | bytes 208904 | tf_op jit(solution)/shard_map/ppermute | solution.py:35
  49.4 5.0 %collective-permute-start.8 = (f32[17,8,128]{2,1,0:T(8,128)}, f32[17,8,128]{2,1,0:T(8,128)S(1)}, u32[]{:S(2)}, u32[]{:S(2)}) collective-permute-start(f32[17,8,128]{2,1,0:T(8,128)} %get-tuple-element.47), channel_id=1, source_target_pairs={{0,8},{4,12},{8,0},{12,4},{16,24},{20,28},{24,16},{28,20},{1,9},{5... | collective-permute-start | bytes 208904 | tf_op jit(solution)/shard_map/ppermute | solution.py:35
  51.4 5.1 %collective-permute-start.11 = (f32[33,8,128]{2,1,0:T(8,128)S(1)}, f32[33,8,128]{2,1,0:T(8,128)S(1)}, u32[]{:S(2)}, u32[]{:S(2)}) collective-permute-start(f32[33,8,128]{2,1,0:T(8,128)S(1)} %pad_maximum_fusion.4.own_b), channel_id=1, source_target_pairs={{0,8},{4,12},{8,0},{12,4},{16,24},{20,28},{24,16},{28,20},{1,9},{5... | collective-permute-start | bytes 405512 | tf_op jit(solution)/shard_map/ppermute | solution.py:35
  55.1 5.1 %collective-permute-start.9 = (f32[33,8,128]{2,1,0:T(8,128)S(1)}, f32[33,8,128]{2,1,0:T(8,128)S(1)}, u32[]{:S(2)}, u32[]{:S(2)}) collective-permute-start(f32[33,8,128]{2,1,0:T(8,128)S(1)} %pad_maximum_fusion.3.own_a), channel_id=1, source_target_pairs={{0,4},{4,0},{8,12},{12,8},{16,20},{20,16},{24,28},{28,24},{1,5},{5... | collective-permute-start | bytes 405512 | tf_op jit(solution)/shard_map/ppermute | solution.py:35
  71.5 20.3 %collective-permute-start.13 = (f32[17,16,128]{2,1,0:T(8,128)S(1)}, f32[17,16,128]{2,1,0:T(8,128)S(1)}, u32[]{:S(2)}, u32[]{:S(2)}) collective-permute-start(f32[17,16,128]{2,1,0:T(8,128)S(1)} %pad_maximum_fusion.refs_0_), channel_id=1, source_target_pairs={{0,2},{1,3},{2,0},{3,1},{4,6},{5,7},{6,4},{7,5},{8,10},{9,11},{10,... | collective-permute-start | bytes 417800 | tf_op jit(solution)/shard_map/ppermute | solution.py:35
  73.0 6.6 %collective-permute-start.17 = (f32[16,1024]{1,0:T(8,128)S(1)}, f32[16,1024]{1,0:T(8,128)S(1)}, u32[]{:S(2)}, u32[]{:S(2)}) collective-permute-start(f32[16,1024]{1,0:T(8,128)S(1)} %bitcast.37), channel_id=1, source_target_pairs={{0,16},{4,20},{8,24},{12,28},{16,0},{20,4},{24,8},{28,12},{1,17},{... | collective-permute-start | bytes 196616 | tf_op jit(solution)/shard_map/ppermute | solution.py:40
  74.5 10.6 %collective-permute-start.16 = (f32[16,1024]{1,0:T(8,128)S(1)}, f32[16,1024]{1,0:T(8,128)S(1)}, u32[]{:S(2)}, u32[]{:S(2)}) collective-permute-start(f32[16,1024]{1,0:T(8,128)S(1)} %bitcast.38), channel_id=1, source_target_pairs={{0,12},{4,16},{8,20},{12,24},{16,28},{20,0},{24,4},{28,8},{1,13},{... | collective-permute-start | bytes 196616 | tf_op jit(solution)/shard_map/ppermute | solution.py:40
  76.5 8.6 %collective-permute-start.15 = (f32[16,1024]{1,0:T(8,128)S(1)}, f32[16,1024]{1,0:T(8,128)S(1)}, u32[]{:S(2)}, u32[]{:S(2)}) collective-permute-start(f32[16,1024]{1,0:T(8,128)S(1)} %bitcast.39), channel_id=1, source_target_pairs={{0,8},{4,12},{8,16},{12,20},{16,24},{20,28},{24,0},{28,4},{1,9},{5... | collective-permute-start | bytes 196616 | tf_op jit(solution)/shard_map/ppermute | solution.py:40
  76.8 8.3 %collective-permute-start.14 = (f32[16,1024]{1,0:T(8,128)S(1)}, f32[16,1024]{1,0:T(8,128)S(1)}, u32[]{:S(2)}, u32[]{:S(2)}) collective-permute-start(f32[16,1024]{1,0:T(8,128)S(1)} %bitcast.40), channel_id=1, source_target_pairs={{0,4},{4,8},{8,12},{12,16},{16,20},{20,24},{24,28},{28,0},{1,5},{5... | collective-permute-start | bytes 196616 | tf_op jit(solution)/shard_map/ppermute | solution.py:40
  103.5 5.8 %collective-permute-start.20 = (f32[33,8,128]{2,1,0:T(8,128)}, f32[33,8,128]{2,1,0:T(8,128)S(1)}, u32[]{:S(2)}, u32[]{:S(2)}) collective-permute-start(f32[33,8,128]{2,1,0:T(8,128)} %get-tuple-element.53), channel_id=1, source_target_pairs={{0,4},{4,0},{8,12},{12,8},{16,20},{20,16},{24,28},{28,24},{1,5},{5... | collective-permute-start | bytes 405512 | tf_op jit(solution)/shard_map/ppermute | solution.py:35
  103.5 7.5 %collective-permute-start.22 = (f32[33,8,128]{2,1,0:T(8,128)}, f32[33,8,128]{2,1,0:T(8,128)S(1)}, u32[]{:S(2)}, u32[]{:S(2)}) collective-permute-start(f32[33,8,128]{2,1,0:T(8,128)} %get-tuple-element.55), channel_id=1, source_target_pairs={{0,8},{4,12},{8,0},{12,4},{16,24},{20,28},{24,16},{28,20},{1,9},{5... | collective-permute-start | bytes 405512 | tf_op jit(solution)/shard_map/ppermute | solution.py:35
  117.1 7.9 %collective-permute-start.24 = (f32[17,16,128]{2,1,0:T(8,128)S(1)}, f32[17,16,128]{2,1,0:T(8,128)S(1)}, u32[]{:S(2)}, u32[]{:S(2)}) collective-permute-start(f32[17,16,128]{2,1,0:T(8,128)S(1)} %maximum_maximum_fusion.2.refs_0_), channel_id=1, source_target_pairs={{0,16},{4,20},{8,24},{12,28},{16,0},{20,4},{24,8},{28,12},{1,17},{... | collective-permute-start | bytes 417800 | tf_op jit(solution)/shard_map/ppermute | solution.py:35
  127.7 4.5 %collective-permute-start.27 = (f32[17,8,128]{2,1,0:T(8,128)}, f32[17,8,128]{2,1,0:T(8,128)S(1)}, u32[]{:S(2)}, u32[]{:S(2)}) collective-permute-start(f32[17,8,128]{2,1,0:T(8,128)} %get-tuple-element.59), channel_id=1, source_target_pairs={{0,4},{4,0},{8,12},{12,8},{16,20},{20,16},{24,28},{28,24},{1,5},{5... | collective-permute-start | bytes 208904 | tf_op jit(solution)/shard_map/ppermute | solution.py:35
  129.7 4.5 %collective-permute-start.25 = (f32[17,8,128]{2,1,0:T(8,128)}, f32[17,8,128]{2,1,0:T(8,128)S(1)}, u32[]{:S(2)}, u32[]{:S(2)}) collective-permute-start(f32[17,8,128]{2,1,0:T(8,128)} %get-tuple-element.58), channel_id=1, source_target_pairs={{0,8},{4,12},{8,0},{12,4},{16,24},{20,28},{24,16},{28,20},{1,9},{5... | collective-permute-start | bytes 208904 | tf_op jit(solution)/shard_map/ppermute | solution.py:35
  132.9 5.1 %collective-permute-start.28 = (f32[33,8,128]{2,1,0:T(8,128)S(1)}, f32[33,8,128]{2,1,0:T(8,128)S(1)}, u32[]{:S(2)}, u32[]{:S(2)}) collective-permute-start(f32[33,8,128]{2,1,0:T(8,128)S(1)} %pad_maximum_fusion.6.own_b), channel_id=1, source_target_pairs={{0,8},{4,12},{8,0},{12,4},{16,24},{20,28},{24,16},{28,20},{1,9},{5... | collective-permute-start | bytes 405512 | tf_op jit(solution)/shard_map/ppermute | solution.py:35
  134.9 5.1 %collective-permute-start.26 = (f32[33,8,128]{2,1,0:T(8,128)S(1)}, f32[33,8,128]{2,1,0:T(8,128)S(1)}, u32[]{:S(2)}, u32[]{:S(2)}) collective-permute-start(f32[33,8,128]{2,1,0:T(8,128)S(1)} %pad_maximum_fusion.5.own_a), channel_id=1, source_target_pairs={{0,4},{4,0},{8,12},{12,8},{16,20},{20,16},{24,28},{28,24},{1,5},{5... | collective-permute-start | bytes 405512 | tf_op jit(solution)/shard_map/ppermute | solution.py:35
  151.4 5.8 %collective-permute-start.30 = (f32[17,16,128]{2,1,0:T(8,128)S(1)}, f32[17,16,128]{2,1,0:T(8,128)S(1)}, u32[]{:S(2)}, u32[]{:S(2)}) collective-permute-start(f32[17,16,128]{2,1,0:T(8,128)S(1)} %pad_maximum_fusion.1.refs_0_), channel_id=1, source_target_pairs={{0,2},{1,3},{2,0},{3,1},{4,6},{5,7},{6,4},{7,5},{8,10},{9,11},{10,... | collective-permute-start | bytes 417800 | tf_op jit(solution)/shard_map/ppermute | solution.py:35
  168.3 5.9 %collective-permute-start.32 = (f32[33,8,128]{2,1,0:T(8,128)}, f32[33,8,128]{2,1,0:T(8,128)S(1)}, u32[]{:S(2)}, u32[]{:S(2)}) collective-permute-start(f32[33,8,128]{2,1,0:T(8,128)} %get-tuple-element.65), channel_id=1, source_target_pairs={{0,4},{4,0},{8,12},{12,8},{16,20},{20,16},{24,28},{28,24},{1,5},{5... | collective-permute-start | bytes 405512 | tf_op jit(solution)/shard_map/ppermute | solution.py:35
  170.0 6.6 %collective-permute-start.34 = (f32[33,8,128]{2,1,0:T(8,128)}, f32[33,8,128]{2,1,0:T(8,128)S(1)}, u32[]{:S(2)}, u32[]{:S(2)}) collective-permute-start(f32[33,8,128]{2,1,0:T(8,128)} %get-tuple-element.67), channel_id=1, source_target_pairs={{0,8},{4,12},{8,0},{12,4},{16,24},{20,28},{24,16},{28,20},{1,9},{5... | collective-permute-start | bytes 405512 | tf_op jit(solution)/shard_map/ppermute | solution.py:35
  182.7 7.5 %collective-permute-start.36 = (f32[17,16,128]{2,1,0:T(8,128)S(1)}, f32[17,16,128]{2,1,0:T(8,128)S(1)}, u32[]{:S(2)}, u32[]{:S(2)}) collective-permute-start(f32[17,16,128]{2,1,0:T(8,128)S(1)} %maximum_maximum_fusion.3.refs_0_), channel_id=1, source_target_pairs={{0,16},{4,20},{8,24},{12,28},{16,0},{20,4},{24,8},{28,12},{1,17},{... | collective-permute-start | bytes 417800 | tf_op jit(solution)/shard_map/ppermute | solution.py:35
  192.8 4.5 %collective-permute-start.39 = (f32[17,8,128]{2,1,0:T(8,128)}, f32[17,8,128]{2,1,0:T(8,128)S(1)}, u32[]{:S(2)}, u32[]{:S(2)}) collective-permute-start(f32[17,8,128]{2,1,0:T(8,128)} %get-tuple-element.72), channel_id=1, source_target_pairs={{0,4},{4,0},{8,12},{12,8},{16,20},{20,16},{24,28},{28,24},{1,5},{5... | collective-permute-start | bytes 208904 | tf_op jit(solution)/shard_map/ppermute | solution.py:35
  195.9 4.5 %collective-permute-start.37 = (f32[17,8,128]{2,1,0:T(8,128)}, f32[17,8,128]{2,1,0:T(8,128)S(1)}, u32[]{:S(2)}, u32[]{:S(2)}) collective-permute-start(f32[17,8,128]{2,1,0:T(8,128)} %get-tuple-element.71), channel_id=1, source_target_pairs={{0,8},{4,12},{8,0},{12,4},{16,24},{20,28},{24,16},{28,20},{1,9},{5... | collective-permute-start | bytes 208904 | tf_op jit(solution)/shard_map/ppermute | solution.py:35
  198.0 5.1 %collective-permute-start.40 = (f32[33,8,128]{2,1,0:T(8,128)S(1)}, f32[33,8,128]{2,1,0:T(8,128)S(1)}, u32[]{:S(2)}, u32[]{:S(2)}) collective-permute-start(f32[33,8,128]{2,1,0:T(8,128)S(1)} %pad_maximum_fusion.8.own_b), channel_id=1, source_target_pairs={{0,8},{4,12},{8,0},{12,4},{16,24},{20,28},{24,16},{28,20},{1,9},{5... | collective-permute-start | bytes 405512 | tf_op jit(solution)/shard_map/ppermute | solution.py:35
  201.1 5.1 %collective-permute-start.38 = (f32[33,8,128]{2,1,0:T(8,128)S(1)}, f32[33,8,128]{2,1,0:T(8,128)S(1)}, u32[]{:S(2)}, u32[]{:S(2)}) collective-permute-start(f32[33,8,128]{2,1,0:T(8,128)S(1)} %pad_maximum_fusion.7.own_a), channel_id=1, source_target_pairs={{0,4},{4,0},{8,12},{12,8},{16,20},{20,16},{24,28},{28,24},{1,5},{5... | collective-permute-start | bytes 405512 | tf_op jit(solution)/shard_map/ppermute | solution.py:35
  217.6 5.8 %collective-permute-start.42 = (f32[17,16,128]{2,1,0:T(8,128)S(1)}, f32[17,16,128]{2,1,0:T(8,128)S(1)}, u32[]{:S(2)}, u32[]{:S(2)}) collective-permute-start(f32[17,16,128]{2,1,0:T(8,128)S(1)} %pad_maximum_fusion.2.refs_0_), channel_id=1, source_target_pairs={{0,2},{1,3},{2,0},{3,1},{4,6},{5,7},{6,4},{7,5},{8,10},{9,11},{10,... | collective-permute-start | bytes 417800 | tf_op jit(solution)/shard_map/ppermute | solution.py:35
  235.7 4.5 %collective-permute-start.46 = (f32[16,128]{1,0:T(8,128)S(1)}, f32[16,128]{1,0:T(8,128)S(1)}, u32[]{:S(2)}, u32[]{:S(2)}) collective-permute-start(f32[16,128]{1,0:T(8,128)S(1)} %add.215), channel_id=1, source_target_pairs={{0,16},{4,20},{8,24},{12,28},{16,0},{20,4},{24,8},{28,12},{1,17},{... | collective-permute-start | bytes 24584 | tf_op jit(solution)/shard_map/ppermute | solution.py:35
  (54 other events, 409.8 us)

commit v2 on v0

v2 whole, which is shorter than its diff:
```python
import jax
import jax.numpy as jnp
from jax import lax
from jax.experimental import pallas as pl
from jax.experimental.pallas import tpu as pltpu
from jax.sharding import PartitionSpec as P

ITERS = 3
LEAD_MAX = 4
GROUP = 32
PIECE = 16

step_scale = 0.45
return_share = 0.6
epsilon = 1e-06
F32 = jnp.float32
BF16 = jnp.bfloat16


def bit_count(count):
    bits = count.bit_length() - 1
    assert count == 1 << bits and bits >= 2
    return bits


def bit_position(relative, order):
    bits = len(order)
    place = 0
    for step, bit in enumerate(order):
        place = place + (((relative >> bit) & 1) << (bits - 1 - step))
    return place


def exchanged(value, axis, mask):
    count = lax.axis_size(axis)
    return lax.ppermute(value, axis, [(source, source ^ mask) for source in range(count)])


def passed_along(value, axis, steps):
    count = lax.axis_size(axis)
    return lax.ppermute(value, axis, [(source, (source + steps) % count) for source in range(count)])


def halves(value):
    high = value.astype(BF16)
    low = (value - high.astype(F32)).astype(BF16)
    return high, low


def stacked(value):
    high, low = halves(value)
    return jnp.concatenate(
        [jnp.concatenate([high, high], 1), jnp.concatenate([low, low], 1)], 0
    )


def call_once(body, inputs, outputs):
    return pl.pallas_call(
        body, out_shape=[jax.ShapeDtypeStruct(shape, F32) for shape in outputs]
    )(*inputs)


def unit_of(ref, k, tile):
    return ref[:, k * tile : (k + 1) * tile] if len(ref.shape) == 2 else ref[k]


def tile_products(index, parts, matrix_tiles, transposed, operand_units, total_units, sub, finish, extra, outputs):
    count, tile, _ = matrix_tiles.shape
    scen = parts[0].shape[-2]
    group = min(GROUP, count)
    piece = min(PIECE, group)
    pieces = count // piece

    def body(index_ref, tiles_ref, *refs):
        part_refs = refs[: len(parts)]
        extra_refs = refs[len(parts) : len(parts) + len(extra)]
        out_refs = refs[len(parts) + len(extra) : -4]
        held, total, operand, arrived = refs[-4:]

        def copy_of(which):
            where = pl.ds(which * piece, piece)
            return pltpu.make_async_copy(tiles_ref.at[where], held.at[where], arrived.at[which])

        for which in range(pieces):
            copy_of(which).start()
        total[...] = jnp.zeros_like(total)
        per_part = operand_units // len(parts)
        for which, ref in enumerate(part_refs):
            for k in range(per_part):
                operand[which * per_part + k] = stacked(unit_of(ref, k, tile))

        def one_group(step, carry):
            for k in range(group):
                if k % piece == 0:
                    copy_of(step * (group // piece) + k // piece).wait()
                t = step * group + k
                row = index_ref[t]
                column = index_ref[count + t]
                high, low = halves(held[t])
                if transposed:
                    operand_at, weights, sides, total_at = (
                        row,
                        jnp.concatenate([high, low], 0),
                        (((1,), (0,)), ((), ())),
                        column,
                    )
                else:
                    operand_at, weights, sides, total_at = (
                        column,
                        jnp.concatenate([high, low], 1),
                        (((1,), (1,)), ((), ())),
                        row,
                    )
                product = lax.dot_general(
                    operand[operand_at], weights, sides, preferred_element_type=F32
                )
                total[total_at] += product[:scen] + product[scen:]
            return carry

        lax.fori_loop(0, count // group, one_group, 0)
        finish(part_refs, extra_refs, total, out_refs)

    in_vmem = pl.BlockSpec(memory_space=pltpu.VMEM)
    return pl.pallas_call(
        body,
        out_shape=[jax.ShapeDtypeStruct(shape, F32) for shape in outputs],
        in_specs=[
            pl.BlockSpec(memory_space=pltpu.SMEM),
            pl.BlockSpec(memory_space=pl.ANY),
        ]
        + [in_vmem] * (len(parts) + len(extra)),
        out_specs=[in_vmem] * len(outputs),
        scratch_shapes=[
            pltpu.VMEM((count, tile, tile), F32),
            pltpu.VMEM((total_units, scen, tile), F32),
            pltpu.VMEM((operand_units, 2 * scen, 2 * tile), BF16),
            pltpu.SemaphoreType.DMA((pieces,)),
        ],
    )(index, matrix_tiles, *parts, *extra)


def backward_product(index, parts, matrix_tiles, units_row, units_col, sub):
    scen, tile = parts[0].shape[-2], matrix_tiles.shape[-1]
    quarter = units_col // 4
    carried = len(parts) == 2

    def finish(part_refs, extra_refs, total, out_refs):
        for mask in range(4):
            for k in range(quarter):
                out_refs[mask][k] = total[mask * quarter + k]
        if carried:
            square = part_refs[0][units_row // 2] + part_refs[1][units_row // 2]
        else:
            square = jnp.zeros((scen, tile), F32)
        for mask in range(4):
            out_refs[mask][quarter] = square

    return tile_products(
        index, parts, matrix_tiles, True, units_row, units_col, sub, finish, [],
        [(quarter + 1, scen, tile)] * 4,
    )


def forward_product(index, parts, matrix_tiles, right_side, units_row, units_col, sub):
    _, scen, tile = parts[0].shape
    quarter = units_col // 4
    half = units_row // 2

    def finish(part_refs, extra_refs, total, out_refs):
        keep, send = out_refs
        for k in range(half):
            value = total[k]
            keep[k] = value - extra_refs[0][k] if k < sub else value
            send[k] = total[half + k]
        squares = [ref[quarter] for ref in part_refs]
        square = (squares[0] + squares[1]) + (squares[2] + squares[3])
        keep[half] = square
        send[half] = square

    return tile_products(
        index, parts, matrix_tiles, False, units_col, units_row, sub, finish, [right_side],
        [(half + 1, scen, tile)] * 2,
    )


def right_side_of(demand_rows, earlier, lead, tile):
    scen, rows = demand_rows.shape
    sub = rows // tile

    def body(demand_ref, *refs):
        lead_ref, out_ref = refs[-2:]
        for k in range(sub):
            lanes = slice(k * tile, (k + 1) * tile)
            wanted = lead_ref[k : k + 1, :]
            lagged = jnp.zeros((scen, tile), F32)
            for steps in range(1, LEAD_MAX + 1):
                lagged = jnp.where(wanted == steps, refs[steps - 1][:, lanes], lagged)
            out_ref[k] = demand_ref[:, lanes] - return_share * lagged

    return call_once(body, (demand_rows, *earlier, lead), ((sub, scen, tile),))[0]


def next_weight(weight, primal_square, dual_square):
    primal_sum = jnp.sum(primal_square, axis=-1, keepdims=True)
    dual_sum = jnp.sum(dual_square, axis=-1, keepdims=True)
    ratio = (primal_sum + epsilon) / (dual_sum + epsilon)
    return jnp.sqrt(weight * jnp.sqrt(ratio))


def primal_update(own, other, starts, primal, weight, primal_square, sub, last):
    _, scen, tile = own.shape
    first = primal is None

    def body(*refs):
        own_ref, other_ref = refs[:2]
        start_refs = refs[2:4]
        weight_ref = refs[4]
        rest = refs[5:]
        if not first:
            primal_ref, square_ref = rest[:2]
            rest = rest[2:]
        new_ref, message = rest[:2]
        rest = rest[2:]
        weight_now = weight_ref[...]
        if not first:
            weight_now = next_weight(
                weight_now, square_ref[...], own_ref[2 * sub] + other_ref[2 * sub]
            )
            rest[0][...] = weight_now
            rest = rest[1:]
        primal_step = step_scale / weight_now
        squares = []
        for chunk in range(2):
            square = jnp.zeros((scen, tile), F32)
            for k in range(sub):
                here = chunk * sub + k
                lanes = slice(k * tile, (k + 1) * tile)
                pull = own_ref[here] + other_ref[(1 - chunk) * sub + k]
                before = start_refs[chunk][:scen, lanes] if first else primal_ref[here]
                cost = start_refs[chunk][scen : scen + 1, lanes]
                after = jnp.maximum(before - primal_step * (cost - pull), 0.0)
                change = after - before
                square = square + change * change
                new_ref[here] = after
                message[here] = 2.0 * after - before
                if last and chunk == 0:
                    rest[0][:, lanes] = after
            squares.append(square)
        message[2 * sub] = squares[0] + squares[1]

    inputs = [own, other, *starts, weight]
    outputs = [(2 * sub, scen, tile), (2 * sub + 1, scen, tile)]
    if not first:
        inputs += [primal, primal_square]
        outputs.append((scen, tile))
    if last:
        outputs.append((scen, sub * tile))
    return call_once(body, inputs, outputs)


def dual_update(own, other, duals, weight, sub, last):
    _, scen, tile = own.shape

    def body(*refs):
        own_ref, other_ref, weight_ref = refs[:3]
        dual_refs = refs[3 : 3 + len(duals)]
        message, square_ref = refs[3 + len(duals) :][:2]
        square_ref[...] = own_ref[2 * sub] + other_ref[2 * sub]
        dual_step = step_scale * weight_ref[...]
        squares = []
        for chunk in range(2):
            square = jnp.zeros((scen, tile), F32)
            for k in range(sub):
                here = chunk * sub + k
                excess = own_ref[here] + other_ref[(1 - chunk) * sub + k]
                if len(duals) == 2:
                    before = unit_of(dual_refs[chunk], k, tile)
                else:
                    before = dual_refs[0][here]
                after = before - dual_step * excess
                change = after - before
                square = square + change * change
                if not last:
                    message[here] = after
                elif chunk == 0:
                    message[:, k * tile : (k + 1) * tile] = after
            squares.append(square)
        square = squares[0] + squares[1]
        if last:
            refs[-1][...] = square
        else:
            message[2 * sub] = square

    if last:
        outputs = [(scen, sub * tile), (scen, tile), (scen, tile)]
    else:
        outputs = [(2 * sub + 1, scen, tile), (scen, tile)]
    return call_once(body, [own, other, weight, *duals], outputs)


def summed(own, axis, others):
    got = [exchanged(value, axis, mask) for mask, value in enumerate(others, 1)]
    return (own + got[0]) + (got[1] + got[2])


def on_device(
    demand, lead_periods, matrix_tiles, tile_pos, cost_vector, primal_init, dual_init, weight_init
):
    band_bits = bit_count(lax.axis_size("band"))
    assert bit_count(lax.axis_size("col")) == 2 and band_bits >= 3
    matrix_tiles = matrix_tiles.reshape(matrix_tiles.shape[2:])
    positions = tile_pos.reshape(-1)
    tile = matrix_tiles.shape[-1]
    block_rows, scen = demand.shape
    sub = block_rows // tile
    units_col = sub << band_bits
    units_row = 4 * sub
    order = tuple(range(2, band_bits))

    row_unit, column_unit = positions // units_col, positions % units_col
    apart = (row_unit // sub) ^ lax.axis_index("col")
    row_place = ((apart & 1) * 2 + (apart >> 1)) * sub + row_unit % sub
    apart = (column_unit // sub) ^ lax.axis_index("band")
    column_place = (
        (apart & 3) * (units_col // 4) + bit_position(apart, order) * sub + column_unit % sub
    )
    index = jnp.concatenate([row_place, column_place])

    with jax.named_scope("dual_x"):
        dual_own = dual_init.T
        dual_beside = exchanged(dual_own, "col", 2)
        duals = [dual_own, dual_beside]
        parts = duals + [exchanged(value, "col", 1) for value in duals]
    demand_rows = demand.T
    earlier = []
    for steps in range(1, LEAD_MAX + 1):
        with jax.named_scope(f"lag_{steps}"):
            earlier.append(passed_along(demand_rows, "band", steps))
    right_side = right_side_of(demand_rows, earlier, lead_periods.reshape(sub, tile), tile)
    with jax.named_scope("start"):
        start_own = jnp.concatenate([primal_init.T, cost_vector[None, :]])
        starts = [start_own, exchanged(start_own, "band", 1 << order[-1])]
    weight = jnp.broadcast_to(weight_init[:, None], (scen, tile))
    primal = None
    primal_square = None
    for iteration in range(ITERS):
        last = iteration == ITERS - 1
        with jax.named_scope(f"back_{iteration}"):
            pieces = backward_product(index, parts, matrix_tiles, units_row, units_col, sub)
        total = summed(pieces[0], "band", pieces[1:])
        for bit in order[:-1]:
            half = total.shape[0] // 2
            send = jnp.concatenate([total[half:-1], total[-1:]])
            total = jnp.concatenate([total[:half], total[-1:]]) + exchanged(send, "band", 1 << bit)
        with jax.named_scope(f"pair_{iteration}"):
            other = exchanged(total, "band", 1 << order[-1])
        results = primal_update(total, other, starts, primal, weight, primal_square, sub, last)
        primal, ahead = results[:2]
        if iteration:
            weight = results[2]
        if last:
            primal_rows = results[-1]
        for bit in order[-2::-1]:
            got = exchanged(ahead, "band", 1 << bit)
            ahead = jnp.concatenate([ahead[:-1], got[:-1], ahead[-1:] + got[-1:]])
        with jax.named_scope(f"spread_{iteration}"):
            ahead = [ahead] + [exchanged(ahead, "band", mask) for mask in range(1, 4)]
        with jax.named_scope(f"fore_{iteration}"):
            keep, send = forward_product(
                index, ahead, matrix_tiles, right_side, units_row, units_col, sub
            )
        total = keep + exchanged(send, "col", 1)
        results = dual_update(total, exchanged(total, "col", 2), duals, weight, sub, last)
        primal_square = results[1]
        if last:
            dual_rows, _, square = results
        else:
            duals = [results[0]]
            parts = [results[0], exchanged(results[0], "col", 1)]
    square = square + exchanged(square, "col", 1)
    square = summed(square, "band", [square] * 3)
    for bit in order:
        square = square + exchanged(square, "band", 1 << bit)
    weight = next_weight(weight, primal_square, square)[:, 0]
    return (primal_rows.T, dual_rows.T, weight)


def solution(mesh):
    in_specs = (
        P(("band", "col"), None),
        P(("band", "col")),
        P("band", "col", None, None, None),
        P("band", "col", None),
        P(("band", "col")),
        P(("band", "col"), None),
        P(("band", "col"), None),
        P(),
    )
    out_specs = (P(("band", "col"), None), P(("band", "col"), None), P())
    return jax.shard_map(
        on_device, mesh=mesh, in_specs=in_specs, out_specs=out_specs, check_vma=False
    )
```

time: 481 us -> 215 us (0.45)
  blocking collectives: 199 us -> 0 us
  matrix products: 76.6 us -> 0 us
  Pallas kernels: 0 us -> 50.2 us
  starting transfers between devices: 1.03 us -> 43.5 us
  waiting for transfers between devices: 140 us -> 101 us
  other arithmetic: 29.2 us -> 9.24 us
  between operations: 14.8 us -> 0.96 us
  local copies, waits for them, and re-layouts: 15.5 us -> 9.76 us
    psum x3 -> x0, blocking collectives: 116 us -> none  [on_device(): dual_square = lax.psum(dual_local, ('band', 'col'))]
    all_gather x5 -> x0, blocking collectives: 82.6 us -> none  [the longest x1 31.7 us: on_device(): lax.all_gather(primal_init, 'band', axis=0, tiled=True)]
    dot_general x9 -> x0, matrix products: 76.6 us -> none  [the longest x3 46.1 us: forward_part(): jnp.einsum('tij,tjs->tis', matrix_tiles, picked, precision=highest)]
    psum x3 -> x0, waiting for transfers between devices: 76.1 us -> none  [on_device(): pull_terms = lax.psum(partial_value, 'band')]
    ppermute x4 -> x42, waiting for transfers between devices: 27.1 us -> 101 us  [the longest x38 90.1 us: exchanged(): lax.ppermute(value, axis, [(source, source ^ mask) for source in range(co...]
    pallas_call x0 -> x13, Pallas kernels: none -> 50.2 us  [the longest x6 37.5 us: tile_products(): pl.pallas_call(body, out_shape=[jax.ShapeDtypeStruct(shape, F32) for shap...]
    ppermute x4 -> x42, starting transfers between devices: 0.79 us -> 43.5 us  [the longest x38 35.8 us: exchanged(): lax.ppermute(value, axis, [(source, source ^ mask) for source in range(co...]
    reduce_scatter x3 -> x0, waiting for transfers between devices: 37.1 us -> none  [on_device(): lax.psum_scatter(push_part, 'col', scatter_dimension=0, tiled=True)]
  transfers between devices with their start and end apart: 10 -> 42, of which waited for: 9 -> 36; matrix products, arithmetic and copies ran while one was open for 1% -> 1% of each run, Pallas kernels for 0% -> 1%
where the time goes in v2:
time: 215 us; the launch traced here: 214 us
  waiting for transfers between devices  101 us (47%)
  Pallas kernels  50.2 us (23%)
  starting transfers between devices  43.5 us (20%)
  local copies, waits for them, and re-layouts  9.76 us (5%)
  other arithmetic  9.24 us (4%)
    ppermute x38, waiting for transfers between devices, exchanged(): lax.ppermute(value, axis, [(source, source ^ mask) for source in range(co...  90.1 us
    pallas_call x6, Pallas kernels, tile_products(): pl.pallas_call(body, out_shape=[jax.ShapeDtypeStruct(shape, F32) for shap...  37.5 us
    ppermute x38, starting transfers between devices, exchanged(): lax.ppermute(value, axis, [(source, source ^ mask) for source in range(co...  35.8 us
    pallas_call x7, Pallas kernels, call_once(): pl.pallas_call(body, out_shape=[jax.ShapeDtypeStruct(shape, F32) for shap...  12.6 us
    ppermute x4, waiting for transfers between devices, passed_along(): lax.ppermute(value, axis, [(source, (source + steps) % count) for source...  10.6 us
    unnamed x74, local copies, waits for them, and re-layouts  9.1 us
    ppermute x4, starting transfers between devices, passed_along(): lax.ppermute(value, axis, [(source, (source + steps) % count) for source...  7.7 us
  transfers between devices with their start and end apart: 42, of which 36 were waited for; matrix products, arithmetic and copies ran while one was open for 1% of the time, Pallas kernels for 1%

profile of v2, /device:TPU:0, one launch (start us, length us, event | category | flops | bytes accessed | tf_op | source)
XLA Modules:
  0.0 214.3 jit_solution(13349134463552999835)
XLA Ops:
  1.2 2.6 %collective-permute-start = (f32[16,1024]{1,0:T(8,128)}, f32[16,1024]{1,0:T(8,128)S(1)}, u32[]{:S(2)}, u32[]{:S(2)}) collective-permute-start(f32[16,1024]{1,0:T(8,128)} %bitcast.32), channel_id=1, source_target_pairs={{0,2},{1,3},{2,0},{3,1},{4,6},{5,7},{6,4},{7,5},{8,10},{9,11},{10,... | collective-permute-start | bytes 196616 | tf_op jit(solution)/shard_map/dual_x/ppermute | solution.py:36
  4.5 2.2 %collective-permute-done.refs_1_.refs_4_ = f32[16,1024]{1,0:T(8,128)S(1)} collective-permute-done((f32[16,1024]{1,0:T(8,128)}, f32[16,1024]{1,0:T(8,128)S(1)}, u32[]{:S(2)}, u32[]{:S(2)}) %collective-permute-start) | collective-permute-done | bytes 65568 | tf_op jit(solution)/shard_map/dual_x/ppermute | solution.py:36
  8.6 5.5 %back_0.1 = (f32[17,16,128]{2,1,0:T(8,128)}, f32[17,16,128]{2,1,0:T(8,128)}, f32[17,16,128]{2,1,0:T(8,128)}, f32[17,16,128]{2,1,0:T(8,128)}) custom-call(s32[256]{0:T(256)} %pad_add_fusion.index_ref, f32[128,128,128]{2,1,0:T(8,128)} %bitcast.25, f32[16,1024]{1,0:T(8,128)} %bitcast.33, f32[16,1024]{1,0:T(8,128)} %copy-done.8, f32[16,1024]{1,0:T(8,128)} %copy-done.26, ...), custom_call_target="tpu_custom_call" | custom-call | tf_op jit(solution)/shard_map/back_0/pallas_call | solution.py:124
  17.7 2.5 %collective-permute-done.3 = f32[17,16,128]{2,1,0:T(8,128)S(1)} collective-permute-done((f32[17,16,128]{2,1,0:T(8,128)}, f32[17,16,128]{2,1,0:T(8,128)S(1)}, u32[]{:S(2)}, u32[]{:S(2)}) %collective-permute-start.3) | collective-permute-done | bytes 139296 | tf_op jit(solution)/shard_map/ppermute | solution.py:36
  20.2 2.6 %collective-permute-done.4 = f32[17,16,128]{2,1,0:T(8,128)S(1)} collective-permute-done((f32[17,16,128]{2,1,0:T(8,128)}, f32[17,16,128]{2,1,0:T(8,128)S(1)}, u32[]{:S(2)}, u32[]{:S(2)}) %collective-permute-start.4) | collective-permute-done | bytes 139296 | tf_op jit(solution)/shard_map/ppermute | solution.py:36
  25.3 2.8 %collective-permute-start.6 = (f32[17,16,128]{2,1,0:T(8,128)S(1)}, f32[17,16,128]{2,1,0:T(8,128)S(1)}, u32[]{:S(2)}, u32[]{:S(2)}) collective-permute-start(f32[17,16,128]{2,1,0:T(8,128)S(1)} %add_add_fusion.2.refs_0_), channel_id=1, source_target_pairs={{0,16},{4,20},{8,24},{12,28},{16,0},{20,4},{24,8},{28,12},{1,17},{... | collective-permute-start | bytes 417800 | tf_op jit(solution)/shard_map/pair_0/ppermute | solution.py:36
  28.4 10.1 %collective-permute-done.7.refs_3_ = f32[17,1024]{1,0:T(8,128)S(1)} collective-permute-done((f32[17,1024]{1,0:T(8,128)S(1)}, f32[17,1024]{1,0:T(8,128)S(1)}, u32[]{:S(2)}, u32[]{:S(2)}) %collective-permute-start.7) | collective-permute-done | bytes 69664 | tf_op jit(solution)/shard_map/start/ppermute | solution.py:36
  46.4 2.9 %collective-permute-start.13 = (f32[16,1024]{1,0:T(8,128)S(1)}, f32[16,1024]{1,0:T(8,128)S(1)}, u32[]{:S(2)}, u32[]{:S(2)}) collective-permute-start(f32[16,1024]{1,0:T(8,128)S(1)} %bitcast.37), channel_id=1, source_target_pairs={{0,12},{4,16},{8,20},{12,24},{16,28},{20,0},{24,4},{28,8},{1,13},{... | collective-permute-start | bytes 196616 | tf_op jit(solution)/shard_map/lag_3/ppermute | solution.py:41
  50.8 3.0 %collective-permute-start.12 = (f32[16,1024]{1,0:T(8,128)S(1)}, f32[16,1024]{1,0:T(8,128)S(1)}, u32[]{:S(2)}, u32[]{:S(2)}) collective-permute-start(f32[16,1024]{1,0:T(8,128)S(1)} %bitcast.38), channel_id=1, source_target_pairs={{0,8},{4,12},{8,16},{12,20},{16,24},{20,28},{24,0},{28,4},{1,9},{5... | collective-permute-start | bytes 196616 | tf_op jit(solution)/shard_map/lag_2/ppermute | solution.py:41
  53.8 2.1 collective-permute-done.13.refs_2_
  56.9 6.0 %collective-permute-done.11.refs_0_ = f32[16,1024]{1,0:T(8,128)S(1)} collective-permute-done((f32[16,1024]{1,0:T(8,128)S(1)}, f32[16,1024]{1,0:T(8,128)S(1)}, u32[]{:S(2)}, u32[]{:S(2)}) %collective-permute-start.11) | collective-permute-done | bytes 65568 | tf_op jit(solution)/shard_map/lag_1/ppermute | solution.py:41
  66.5 7.0 %fore_0.1 = (f32[17,16,128]{2,1,0:T(8,128)}, f32[17,16,128]{2,1,0:T(8,128)}) custom-call(s32[256]{0:T(256)} %pad_add_fusion.index_ref, f32[128,128,128]{2,1,0:T(8,128)} %bitcast.26, f32[17,16,128]{2,1,0:T(8,128)} %get-tuple-element.40.refs_0_, f32[17,16,128]{2,1,0:T(8,128)} %copy-done.11, f32[17,16,128]{2,1,0:T(8,128)} %copy-done.10, ...), custom_call_target="tpu_custom_call" | custom-call | tf_op jit(solution)/shard_map/fore_0/pallas_call | solution.py:124
  77.6 4.2 %collective-permute-done.16.refs_1_ = f32[17,16,128]{2,1,0:T(8,128)S(1)} collective-permute-done((f32[17,16,128]{2,1,0:T(8,128)S(1)}, f32[17,16,128]{2,1,0:T(8,128)S(1)}, u32[]{:S(2)}, u32[]{:S(2)}) %collective-permute-start.16) | collective-permute-done | bytes 139296 | tf_op jit(solution)/shard_map/ppermute | solution.py:36
  86.5 5.6 %back_1.1 = (f32[17,16,128]{2,1,0:T(8,128)}, f32[17,16,128]{2,1,0:T(8,128)}, f32[17,16,128]{2,1,0:T(8,128)}, f32[17,16,128]{2,1,0:T(8,128)}) custom-call(s32[256]{0:T(256)} %pad_add_fusion.index_ref, f32[128,128,128]{2,1,0:T(8,128)} %bitcast.27, f32[17,16,128]{2,1,0:T(8,128)} %get-tuple-element.43.refs_0_.refs_3_, f32[17,16,128]{2,1,0:T(8,128)} %copy-done.18), custom_call_target="tpu_custom_call" | custom-call | tf_op jit(solution)/shard_map/back_1/pallas_call | solution.py:124
  92.2 3.4 %collective-permute-start.20 = (f32[17,16,128]{2,1,0:T(8,128)}, f32[17,16,128]{2,1,0:T(8,128)S(1)}, u32[]{:S(2)}, u32[]{:S(2)}) collective-permute-start(f32[17,16,128]{2,1,0:T(8,128)} %get-tuple-element.47), channel_id=1, source_target_pairs={{0,12},{4,8},{8,4},{12,0},{16,28},{20,24},{24,20},{28,16},{1,13},{... | collective-permute-start | bytes 417800 | tf_op jit(solution)/shard_map/ppermute | solution.py:36
  95.6 2.4 %collective-permute-done.18 = f32[17,16,128]{2,1,0:T(8,128)S(1)} collective-permute-done((f32[17,16,128]{2,1,0:T(8,128)}, f32[17,16,128]{2,1,0:T(8,128)S(1)}, u32[]{:S(2)}, u32[]{:S(2)}) %collective-permute-start.18) | collective-permute-done | bytes 139296 | tf_op jit(solution)/shard_map/ppermute | solution.py:36
  98.9 3.3 %collective-permute-done.20 = f32[17,16,128]{2,1,0:T(8,128)S(1)} collective-permute-done((f32[17,16,128]{2,1,0:T(8,128)}, f32[17,16,128]{2,1,0:T(8,128)S(1)}, u32[]{:S(2)}, u32[]{:S(2)}) %collective-permute-start.20) | collective-permute-done | bytes 139296 | tf_op jit(solution)/shard_map/ppermute | solution.py:36
  103.2 8.5 %collective-permute-done.21.refs_1_ = f32[17,16,128]{2,1,0:T(8,128)S(1)} collective-permute-done((f32[17,16,128]{2,1,0:T(8,128)S(1)}, f32[17,16,128]{2,1,0:T(8,128)S(1)}, u32[]{:S(2)}, u32[]{:S(2)}) %collective-permute-start.21) | collective-permute-done | bytes 139296 | tf_op jit(solution)/shard_map/pair_1/ppermute | solution.py:36
  117.8 4.2 %collective-permute-done.24.refs_3_ = f32[17,16,128]{2,1,0:T(8,128)S(1)} collective-permute-done((f32[17,16,128]{2,1,0:T(8,128)}, f32[17,16,128]{2,1,0:T(8,128)S(1)}, u32[]{:S(2)}, u32[]{:S(2)}) %collective-permute-start.24) | collective-permute-done | bytes 139296 | tf_op jit(solution)/shard_map/spread_1/ppermute | solution.py:36
  124.6 7.0 %fore_1.1 = (f32[17,16,128]{2,1,0:T(8,128)}, f32[17,16,128]{2,1,0:T(8,128)}) custom-call(s32[256]{0:T(256)} %pad_add_fusion.index_ref, f32[128,128,128]{2,1,0:T(8,128)} %bitcast.28, f32[17,16,128]{2,1,0:T(8,128)} %get-tuple-element.50.refs_0_, f32[17,16,128]{2,1,0:T(8,128)} %copy-done.17, f32[17,16,128]{2,1,0:T(8,128)} %copy-done.15, ...), custom_call_target="tpu_custom_call" | custom-call | tf_op jit(solution)/shard_map/fore_1/pallas_call | solution.py:124
  135.7 4.2 %collective-permute-done.26.refs_1_ = f32[17,16,128]{2,1,0:T(8,128)S(1)} collective-permute-done((f32[17,16,128]{2,1,0:T(8,128)S(1)}, f32[17,16,128]{2,1,0:T(8,128)S(1)}, u32[]{:S(2)}, u32[]{:S(2)}) %collective-permute-start.26) | collective-permute-done | bytes 139296 | tf_op jit(solution)/shard_map/ppermute | solution.py:36
  144.6 5.6 %back_2.1 = (f32[17,16,128]{2,1,0:T(8,128)}, f32[17,16,128]{2,1,0:T(8,128)}, f32[17,16,128]{2,1,0:T(8,128)}, f32[17,16,128]{2,1,0:T(8,128)}) custom-call(s32[256]{0:T(256)} %pad_add_fusion.index_ref, f32[128,128,128]{2,1,0:T(8,128)} %bitcast.29, f32[17,16,128]{2,1,0:T(8,128)} %get-tuple-element.54.refs_0_.refs_3_, f32[17,16,128]{2,1,0:T(8,128)} %copy-done.19), custom_call_target="tpu_custom_call" | custom-call | tf_op jit(solution)/shard_map/back_2/pallas_call | solution.py:124
  151.5 2.2 %collective-permute-start.30 = (f32[17,16,128]{2,1,0:T(8,128)}, f32[17,16,128]{2,1,0:T(8,128)S(1)}, u32[]{:S(2)}, u32[]{:S(2)}) collective-permute-start(f32[17,16,128]{2,1,0:T(8,128)} %get-tuple-element.58), channel_id=1, source_target_pairs={{0,12},{4,8},{8,4},{12,0},{16,28},{20,24},{24,20},{28,16},{1,13},{... | collective-permute-start | bytes 417800 | tf_op jit(solution)/shard_map/ppermute | solution.py:36
  153.7 2.4 %collective-permute-done.28 = f32[17,16,128]{2,1,0:T(8,128)S(1)} collective-permute-done((f32[17,16,128]{2,1,0:T(8,128)}, f32[17,16,128]{2,1,0:T(8,128)S(1)}, u32[]{:S(2)}, u32[]{:S(2)}) %collective-permute-start.28) | collective-permute-done | bytes 139296 | tf_op jit(solution)/shard_map/ppermute | solution.py:36
  156.2 2.1 collective-permute-done.29
  158.2 2.1 collective-permute-done.30
  161.4 8.4 %collective-permute-done.31.refs_1_ = f32[17,16,128]{2,1,0:T(8,128)S(1)} collective-permute-done((f32[17,16,128]{2,1,0:T(8,128)S(1)}, f32[17,16,128]{2,1,0:T(8,128)S(1)}, u32[]{:S(2)}, u32[]{:S(2)}) %collective-permute-start.31) | collective-permute-done | bytes 139296 | tf_op jit(solution)/shard_map/pair_2/ppermute | solution.py:36
  172.5 2.7 %collective-permute-start.33 = (f32[17,16,128]{2,1,0:T(8,128)}, f32[17,16,128]{2,1,0:T(8,128)S(1)}, u32[]{:S(2)}, u32[]{:S(2)}) collective-permute-start(f32[17,16,128]{2,1,0:T(8,128)} %get-tuple-element.62.refs_0_), channel_id=1, source_target_pairs={{0,8},{4,12},{8,0},{12,4},{16,24},{20,28},{24,16},{28,20},{1,9},{5... | collective-permute-start | bytes 417800 | tf_op jit(solution)/shard_map/spread_2/ppermute | solution.py:36
  176.0 4.2 %collective-permute-done.34.refs_3_ = f32[17,16,128]{2,1,0:T(8,128)S(1)} collective-permute-done((f32[17,16,128]{2,1,0:T(8,128)}, f32[17,16,128]{2,1,0:T(8,128)S(1)}, u32[]{:S(2)}, u32[]{:S(2)}) %collective-permute-start.34) | collective-permute-done | bytes 139296 | tf_op jit(solution)/shard_map/spread_2/ppermute | solution.py:36
  183.2 7.0 %fore_2.1 = (f32[17,16,128]{2,1,0:T(8,128)}, f32[17,16,128]{2,1,0:T(8,128)}) custom-call(s32[256]{0:T(256)} %pad_add_fusion.index_ref, f32[128,128,128]{2,1,0:T(8,128)} %bitcast.30, f32[17,16,128]{2,1,0:T(8,128)} %get-tuple-element.62.refs_0_, f32[17,16,128]{2,1,0:T(8,128)} %copy-done.16, f32[17,16,128]{2,1,0:T(8,128)} %copy-done.14, ...), custom_call_target="tpu_custom_call" | custom-call | tf_op jit(solution)/shard_map/fore_2/pallas_call | solution.py:124
  194.3 4.2 %collective-permute-done.36.refs_1_ = f32[17,16,128]{2,1,0:T(8,128)S(1)} collective-permute-done((f32[17,16,128]{2,1,0:T(8,128)S(1)}, f32[17,16,128]{2,1,0:T(8,128)S(1)}, u32[]{:S(2)}, u32[]{:S(2)}) %collective-permute-start.36) | collective-permute-done | bytes 139296 | tf_op jit(solution)/shard_map/ppermute | solution.py:36
  209.7 3.7 %collective-permute-done.41 = f32[16,128]{1,0:T(8,128)S(1)} collective-permute-done((f32[16,128]{1,0:T(8,128)S(1)}, f32[16,128]{1,0:T(8,128)S(1)}, u32[]{:S(2)}, u32[]{:S(2)}) %collective-permute-start.41) | collective-permute-done | bytes 8224 | tf_op jit(solution)/shard_map/ppermute | solution.py:36
  (155 shorter events, 76.8 us)
Async XLA Ops:
  0.7 6.6 %collective-permute-start.1 = (f32[16,1024]{1,0:T(8,128)}, f32[16,1024]{1,0:T(8,128)S(1)}, u32[]{:S(2)}, u32[]{:S(2)}) collective-permute-start(f32[16,1024]{1,0:T(8,128)} %bitcast.31), channel_id=1, source_target_pairs={{0,1},{1,0},{2,3},{3,2},{4,5},{5,4},{6,7},{7,6},{8,9},{9,8},{10,11... | collective-permute-start | bytes 196616 | tf_op jit(solution)/shard_map/dual_x/ppermute | solution.py:36
  1.2 5.4 %collective-permute-start = (f32[16,1024]{1,0:T(8,128)}, f32[16,1024]{1,0:T(8,128)S(1)}, u32[]{:S(2)}, u32[]{:S(2)}) collective-permute-start(f32[16,1024]{1,0:T(8,128)} %bitcast.32), channel_id=1, source_target_pairs={{0,2},{1,3},{2,0},{3,1},{4,6},{5,7},{6,4},{7,5},{8,10},{9,11},{10,... | collective-permute-start | bytes 196616 | tf_op jit(solution)/shard_map/dual_x/ppermute | solution.py:36
  14.1 6.0 %collective-permute-start.3 = (f32[17,16,128]{2,1,0:T(8,128)}, f32[17,16,128]{2,1,0:T(8,128)S(1)}, u32[]{:S(2)}, u32[]{:S(2)}) collective-permute-start(f32[17,16,128]{2,1,0:T(8,128)} %get-tuple-element.37), channel_id=1, source_target_pairs={{0,4},{4,0},{8,12},{12,8},{16,20},{20,16},{24,28},{28,24},{1,5},{5... | collective-permute-start | bytes 417800 | tf_op jit(solution)/shard_map/ppermute | solution.py:36
  15.9 6.8 %collective-permute-start.4 = (f32[17,16,128]{2,1,0:T(8,128)}, f32[17,16,128]{2,1,0:T(8,128)S(1)}, u32[]{:S(2)}, u32[]{:S(2)}) collective-permute-start(f32[17,16,128]{2,1,0:T(8,128)} %get-tuple-element.38), channel_id=1, source_target_pairs={{0,8},{4,12},{8,0},{12,4},{16,24},{20,28},{24,16},{28,20},{1,9},{5... | collective-permute-start | bytes 417800 | tf_op jit(solution)/shard_map/ppermute | solution.py:36
  17.5 6.9 %collective-permute-start.5 = (f32[17,16,128]{2,1,0:T(8,128)}, f32[17,16,128]{2,1,0:T(8,128)S(1)}, u32[]{:S(2)}, u32[]{:S(2)}) collective-permute-start(f32[17,16,128]{2,1,0:T(8,128)} %get-tuple-element.39), channel_id=1, source_target_pairs={{0,12},{4,8},{8,4},{12,0},{16,28},{20,24},{24,20},{28,16},{1,13},{... | collective-permute-start | bytes 417800 | tf_op jit(solution)/shard_map/ppermute | solution.py:36
  25.3 13.2 %collective-permute-start.6 = (f32[17,16,128]{2,1,0:T(8,128)S(1)}, f32[17,16,128]{2,1,0:T(8,128)S(1)}, u32[]{:S(2)}, u32[]{:S(2)}) collective-permute-start(f32[17,16,128]{2,1,0:T(8,128)S(1)} %add_add_fusion.2.refs_0_), channel_id=1, source_target_pairs={{0,16},{4,20},{8,24},{12,28},{16,0},{20,4},{24,8},{28,12},{1,17},{... | collective-permute-start | bytes 417800 | tf_op jit(solution)/shard_map/pair_0/ppermute | solution.py:36
  28.2 10.4 %collective-permute-start.7 = (f32[17,1024]{1,0:T(8,128)S(1)}, f32[17,1024]{1,0:T(8,128)S(1)}, u32[]{:S(2)}, u32[]{:S(2)}) collective-permute-start(f32[17,1024]{1,0:T(8,128)S(1)} %pad_maximum_fusion.refs_2_), channel_id=1, source_target_pairs={{0,16},{4,20},{8,24},{12,28},{16,0},{20,4},{24,8},{28,12},{1,17},{... | collective-permute-start | bytes 208904 | tf_op jit(solution)/shard_map/start/ppermute | solution.py:36
  41.1 24.0 %collective-permute-start.10 = (f32[17,16,128]{2,1,0:T(8,128)}, f32[17,16,128]{2,1,0:T(8,128)S(1)}, u32[]{:S(2)}, u32[]{:S(2)}) collective-permute-start(f32[17,16,128]{2,1,0:T(8,128)} %get-tuple-element.40.refs_0_), channel_id=1, source_target_pairs={{0,12},{4,8},{8,4},{12,0},{16,28},{20,24},{24,20},{28,16},{1,13},{... | collective-permute-start | bytes 417800 | tf_op jit(solution)/shard_map/spread_0/ppermute | solution.py:36
  42.4 22.7 %collective-permute-start.9 = (f32[17,16,128]{2,1,0:T(8,128)}, f32[17,16,128]{2,1,0:T(8,128)S(1)}, u32[]{:S(2)}, u32[]{:S(2)}) collective-permute-start(f32[17,16,128]{2,1,0:T(8,128)} %get-tuple-element.40.refs_0_), channel_id=1, source_target_pairs={{0,8},{4,12},{8,0},{12,4},{16,24},{20,28},{24,16},{28,20},{1,9},{5... | collective-permute-start | bytes 417800 | tf_op jit(solution)/shard_map/spread_0/ppermute | solution.py:36
  43.8 21.4 %collective-permute-start.8 = (f32[17,16,128]{2,1,0:T(8,128)}, f32[17,16,128]{2,1,0:T(8,128)S(1)}, u32[]{:S(2)}, u32[]{:S(2)}) collective-permute-start(f32[17,16,128]{2,1,0:T(8,128)} %get-tuple-element.40.refs_0_), channel_id=1, source_target_pairs={{0,4},{4,0},{8,12},{12,8},{16,20},{20,16},{24,28},{28,24},{1,5},{5... | collective-permute-start | bytes 417800 | tf_op jit(solution)/shard_map/spread_0/ppermute | solution.py:36
  44.6 6.3 %collective-permute-start.14 = (f32[16,1024]{1,0:T(8,128)S(1)}, f32[16,1024]{1,0:T(8,128)S(1)}, u32[]{:S(2)}, u32[]{:S(2)}) collective-permute-start(f32[16,1024]{1,0:T(8,128)S(1)} %bitcast.36), channel_id=1, source_target_pairs={{0,16},{4,20},{8,24},{12,28},{16,0},{20,4},{24,8},{28,12},{1,17},{... | collective-permute-start | bytes 196616 | tf_op jit(solution)/shard_map/lag_4/ppermute | solution.py:41
  46.4 9.5 %collective-permute-start.13 = (f32[16,1024]{1,0:T(8,128)S(1)}, f32[16,1024]{1,0:T(8,128)S(1)}, u32[]{:S(2)}, u32[]{:S(2)}) collective-permute-start(f32[16,1024]{1,0:T(8,128)S(1)} %bitcast.37), channel_id=1, source_target_pairs={{0,12},{4,16},{8,20},{12,24},{16,28},{20,0},{24,4},{28,8},{1,13},{... | collective-permute-start | bytes 196616 | tf_op jit(solution)/shard_map/lag_3/ppermute | solution.py:41
  50.8 6.1 %collective-permute-start.12 = (f32[16,1024]{1,0:T(8,128)S(1)}, f32[16,1024]{1,0:T(8,128)S(1)}, u32[]{:S(2)}, u32[]{:S(2)}) collective-permute-start(f32[16,1024]{1,0:T(8,128)S(1)} %bitcast.38), channel_id=1, source_target_pairs={{0,8},{4,12},{8,16},{12,20},{16,24},{20,28},{24,0},{28,4},{1,9},{5... | collective-permute-start | bytes 196616 | tf_op jit(solution)/shard_map/lag_2/ppermute | solution.py:41
  55.9 7.0 %collective-permute-start.11 = (f32[16,1024]{1,0:T(8,128)S(1)}, f32[16,1024]{1,0:T(8,128)S(1)}, u32[]{:S(2)}, u32[]{:S(2)}) collective-permute-start(f32[16,1024]{1,0:T(8,128)S(1)} %bitcast.39), channel_id=1, source_target_pairs={{0,4},{4,8},{8,12},{12,16},{16,20},{20,24},{24,28},{28,0},{1,5},{5... | collective-permute-start | bytes 196616 | tf_op jit(solution)/shard_map/lag_1/ppermute | solution.py:41
  76.0 5.8 %collective-permute-start.16 = (f32[17,16,128]{2,1,0:T(8,128)S(1)}, f32[17,16,128]{2,1,0:T(8,128)S(1)}, u32[]{:S(2)}, u32[]{:S(2)}) collective-permute-start(f32[17,16,128]{2,1,0:T(8,128)S(1)} %add.106.refs_0_), channel_id=1, source_target_pairs={{0,2},{1,3},{2,0},{3,1},{4,6},{5,7},{6,4},{7,5},{8,10},{9,11},{10,... | collective-permute-start | bytes 417800 | tf_op jit(solution)/shard_map/ppermute | solution.py:36
  92.0 6.0 %collective-permute-start.18 = (f32[17,16,128]{2,1,0:T(8,128)}, f32[17,16,128]{2,1,0:T(8,128)S(1)}, u32[]{:S(2)}, u32[]{:S(2)}) collective-permute-start(f32[17,16,128]{2,1,0:T(8,128)} %get-tuple-element.45), channel_id=1, source_target_pairs={{0,4},{4,0},{8,12},{12,8},{16,20},{20,16},{24,28},{28,24},{1,5},{5... | collective-permute-start | bytes 417800 | tf_op jit(solution)/shard_map/ppermute | solution.py:36
  92.1 6.8 %collective-permute-start.19 = (f32[17,16,128]{2,1,0:T(8,128)}, f32[17,16,128]{2,1,0:T(8,128)S(1)}, u32[]{:S(2)}, u32[]{:S(2)}) collective-permute-start(f32[17,16,128]{2,1,0:T(8,128)} %get-tuple-element.46), channel_id=1, source_target_pairs={{0,8},{4,12},{8,0},{12,4},{16,24},{20,28},{24,16},{28,20},{1,9},{5... | collective-permute-start | bytes 417800 | tf_op jit(solution)/shard_map/ppermute | solution.py:36
  92.2 10.0 %collective-permute-start.20 = (f32[17,16,128]{2,1,0:T(8,128)}, f32[17,16,128]{2,1,0:T(8,128)S(1)}, u32[]{:S(2)}, u32[]{:S(2)}) collective-permute-start(f32[17,16,128]{2,1,0:T(8,128)} %get-tuple-element.47), channel_id=1, source_target_pairs={{0,12},{4,8},{8,4},{12,0},{16,28},{20,24},{24,20},{28,16},{1,13},{... | collective-permute-start | bytes 417800 | tf_op jit(solution)/shard_map/ppermute | solution.py:36
  103.2 8.5 %collective-permute-start.21 = (f32[17,16,128]{2,1,0:T(8,128)S(1)}, f32[17,16,128]{2,1,0:T(8,128)S(1)}, u32[]{:S(2)}, u32[]{:S(2)}) collective-permute-start(f32[17,16,128]{2,1,0:T(8,128)S(1)} %add_add_fusion.1.refs_0_), channel_id=1, source_target_pairs={{0,16},{4,20},{8,24},{12,28},{16,0},{20,4},{24,8},{28,12},{1,17},{... | collective-permute-start | bytes 417800 | tf_op jit(solution)/shard_map/pair_1/ppermute | solution.py:36
  114.4 7.7 %collective-permute-start.24 = (f32[17,16,128]{2,1,0:T(8,128)}, f32[17,16,128]{2,1,0:T(8,128)S(1)}, u32[]{:S(2)}, u32[]{:S(2)}) collective-permute-start(f32[17,16,128]{2,1,0:T(8,128)} %get-tuple-element.50.refs_0_), channel_id=1, source_target_pairs={{0,12},{4,8},{8,4},{12,0},{16,28},{20,24},{24,20},{28,16},{1,13},{... | collective-permute-start | bytes 417800 | tf_op jit(solution)/shard_map/spread_1/ppermute | solution.py:36
  114.4 8.2 %collective-permute-start.23 = (f32[17,16,128]{2,1,0:T(8,128)}, f32[17,16,128]{2,1,0:T(8,128)S(1)}, u32[]{:S(2)}, u32[]{:S(2)}) collective-permute-start(f32[17,16,128]{2,1,0:T(8,128)} %get-tuple-element.50.refs_0_), channel_id=1, source_target_pairs={{0,8},{4,12},{8,0},{12,4},{16,24},{20,28},{24,16},{28,20},{1,9},{5... | collective-permute-start | bytes 417800 | tf_op jit(solution)/shard_map/spread_1/ppermute | solution.py:36
  116.0 7.9 %collective-permute-start.22 = (f32[17,16,128]{2,1,0:T(8,128)}, f32[17,16,128]{2,1,0:T(8,128)S(1)}, u32[]{:S(2)}, u32[]{:S(2)}) collective-permute-start(f32[17,16,128]{2,1,0:T(8,128)} %get-tuple-element.50.refs_0_), channel_id=1, source_target_pairs={{0,4},{4,0},{8,12},{12,8},{16,20},{20,16},{24,28},{28,24},{1,5},{5... | collective-permute-start | bytes 417800 | tf_op jit(solution)/shard_map/spread_1/ppermute | solution.py:36
  134.2 5.8 %collective-permute-start.26 = (f32[17,16,128]{2,1,0:T(8,128)S(1)}, f32[17,16,128]{2,1,0:T(8,128)S(1)}, u32[]{:S(2)}, u32[]{:S(2)}) collective-permute-start(f32[17,16,128]{2,1,0:T(8,128)S(1)} %add.110.refs_0_), channel_id=1, source_target_pairs={{0,2},{1,3},{2,0},{3,1},{4,6},{5,7},{6,4},{7,5},{8,10},{9,11},{10,... | collective-permute-start | bytes 417800 | tf_op jit(solution)/shard_map/ppermute | solution.py:36
  150.2 6.0 %collective-permute-start.28 = (f32[17,16,128]{2,1,0:T(8,128)}, f32[17,16,128]{2,1,0:T(8,128)S(1)}, u32[]{:S(2)}, u32[]{:S(2)}) collective-permute-start(f32[17,16,128]{2,1,0:T(8,128)} %get-tuple-element.56), channel_id=1, source_target_pairs={{0,4},{4,0},{8,12},{12,8},{16,20},{20,16},{24,28},{28,24},{1,5},{5... | collective-permute-start | bytes 417800 | tf_op jit(solution)/shard_map/ppermute | solution.py:36
  151.5 6.8 %collective-permute-start.29 = (f32[17,16,128]{2,1,0:T(8,128)}, f32[17,16,128]{2,1,0:T(8,128)S(1)}, u32[]{:S(2)}, u32[]{:S(2)}) collective-permute-start(f32[17,16,128]{2,1,0:T(8,128)} %get-tuple-element.57), channel_id=1, source_target_pairs={{0,8},{4,12},{8,0},{12,4},{16,24},{20,28},{24,16},{28,20},{1,9},{5... | collective-permute-start | bytes 417800 | tf_op jit(solution)/shard_map/ppermute | solution.py:36
  151.5 8.9 %collective-permute-start.30 = (f32[17,16,128]{2,1,0:T(8,128)}, f32[17,16,128]{2,1,0:T(8,128)S(1)}, u32[]{:S(2)}, u32[]{:S(2)}) collective-permute-start(f32[17,16,128]{2,1,0:T(8,128)} %get-tuple-element.58), channel_id=1, source_target_pairs={{0,12},{4,8},{8,4},{12,0},{16,28},{20,24},{24,20},{28,16},{1,13},{... | collective-permute-start | bytes 417800 | tf_op jit(solution)/shard_map/ppermute | solution.py:36
  161.3 8.5 %collective-permute-start.31 = (f32[17,16,128]{2,1,0:T(8,128)S(1)}, f32[17,16,128]{2,1,0:T(8,128)S(1)}, u32[]{:S(2)}, u32[]{:S(2)}) collective-permute-start(f32[17,16,128]{2,1,0:T(8,128)S(1)} %add_add_fusion.refs_0_), channel_id=1, source_target_pairs={{0,16},{4,20},{8,24},{12,28},{16,0},{20,4},{24,8},{28,12},{1,17},{... | collective-permute-start | bytes 417800 | tf_op jit(solution)/shard_map/pair_2/ppermute | solution.py:36
  172.5 7.7 %collective-permute-start.34 = (f32[17,16,128]{2,1,0:T(8,128)}, f32[17,16,128]{2,1,0:T(8,128)S(1)}, u32[]{:S(2)}, u32[]{:S(2)}) collective-permute-start(f32[17,16,128]{2,1,0:T(8,128)} %get-tuple-element.62.refs_0_), channel_id=1, source_target_pairs={{0,12},{4,8},{8,4},{12,0},{16,28},{20,24},{24,20},{28,16},{1,13},{... | collective-permute-start | bytes 417800 | tf_op jit(solution)/shard_map/spread_2/ppermute | solution.py:36
  172.5 9.4 %collective-permute-start.33 = (f32[17,16,128]{2,1,0:T(8,128)}, f32[17,16,128]{2,1,0:T(8,128)S(1)}, u32[]{:S(2)}, u32[]{:S(2)}) collective-permute-start(f32[17,16,128]{2,1,0:T(8,128)} %get-tuple-element.62.refs_0_), channel_id=1, source_target_pairs={{0,8},{4,12},{8,0},{12,4},{16,24},{20,28},{24,16},{28,20},{1,9},{5... | collective-permute-start | bytes 417800 | tf_op jit(solution)/shard_map/spread_2/ppermute | solution.py:36
  175.2 6.9 %collective-permute-start.32 = (f32[17,16,128]{2,1,0:T(8,128)}, f32[17,16,128]{2,1,0:T(8,128)S(1)}, u32[]{:S(2)}, u32[]{:S(2)}) collective-permute-start(f32[17,16,128]{2,1,0:T(8,128)} %get-tuple-element.62.refs_0_), channel_id=1, source_target_pairs={{0,4},{4,0},{8,12},{12,8},{16,20},{20,16},{24,28},{28,24},{1,5},{5... | collective-permute-start | bytes 417800 | tf_op jit(solution)/shard_map/spread_2/ppermute | solution.py:36
  192.7 5.8 %collective-permute-start.36 = (f32[17,16,128]{2,1,0:T(8,128)S(1)}, f32[17,16,128]{2,1,0:T(8,128)S(1)}, u32[]{:S(2)}, u32[]{:S(2)}) collective-permute-start(f32[17,16,128]{2,1,0:T(8,128)S(1)} %add.114.refs_0_), channel_id=1, source_target_pairs={{0,2},{1,3},{2,0},{3,1},{4,6},{5,7},{6,4},{7,5},{8,10},{9,11},{10,... | collective-permute-start | bytes 417800 | tf_op jit(solution)/shard_map/ppermute | solution.py:36
  203.0 4.6 %collective-permute-start.40 = (f32[16,128]{1,0:T(8,128)S(1)}, f32[16,128]{1,0:T(8,128)S(1)}, u32[]{:S(2)}, u32[]{:S(2)}) collective-permute-start(f32[16,128]{1,0:T(8,128)S(1)} %add.116), channel_id=1, source_target_pairs={{0,12},{4,8},{8,4},{12,0},{16,28},{20,24},{24,20},{28,16},{1,13},{... | collective-permute-start | bytes 24584 | tf_op jit(solution)/shard_map/ppermute | solution.py:36
  (47 other events, 304.1 us)

commit v3 on v2

--- a/solution.py
+++ b/solution.py
@@ -8,7 +8,8 @@
 ITERS = 3
 LEAD_MAX = 4
 GROUP = 32
-PIECE = 16
+PIECE = 8
+KERNEL_VMEM = 24 << 20
 
 step_scale = 0.45
 return_share = 0.6
@@ -54,35 +55,81 @@
     )
 
 
-def call_once(body, inputs, outputs):
+def in_vmem(array):
+    return pltpu.with_memory_space_constraint(array, pltpu.VMEM)
+
+
+def call_in_vmem(body, inputs, outputs, scratch=(), index=None):
+    spec = pl.BlockSpec(memory_space=pltpu.VMEM)
+    first = [] if index is None else [index]
     return pl.pallas_call(
-        body, out_shape=[jax.ShapeDtypeStruct(shape, F32) for shape in outputs]
-    )(*inputs)
+        body,
+        out_shape=[pltpu.VMEM(shape, F32) for shape in outputs],
+        in_specs=[pl.BlockSpec(memory_space=pltpu.SMEM)] * len(first) + [spec] * len(inputs),
+        out_specs=[spec] * len(outputs),
+        scratch_shapes=list(scratch),
+        compiler_params=pltpu.CompilerParams(vmem_limit_bytes=KERNEL_VMEM),
+    )(*first, *(in_vmem(array) for array in inputs))
 
 
 def unit_of(ref, k, tile):
     return ref[:, k * tile : (k + 1) * tile] if len(ref.shape) == 2 else ref[k]
 
 
-def tile_products(index, parts, matrix_tiles, transposed, operand_units, total_units, sub, finish, extra, outputs):
+def prepared_tiles(matrix_tiles):
     count, tile, _ = matrix_tiles.shape
+    piece = min(PIECE, count)
+    pieces = count // piece
+
+    def body(tiles_ref, plain_ref, turned_ref, held, arrived):
+        def copy_of(which):
+            return pltpu.make_async_copy(
+                tiles_ref.at[pl.ds(which * piece, piece)],
+                held.at[pl.ds(which * piece, piece)],
+                arrived.at[which],
+            )
+
+        for which in range(pieces):
+            copy_of(which).start()
+
+        def one_piece(which, carry):
+            copy_of(which).wait()
+            for k in range(piece):
+                t = which * piece + k
+                high, low = halves(held[t])
+                plain_ref[t, :tile] = high
+                plain_ref[t, tile:] = low
+                turned_ref[t, :tile] = high.T
+                turned_ref[t, tile:] = low.T
+            return carry
+
+        lax.fori_loop(0, pieces, one_piece, 0)
+
+    spec = pl.BlockSpec(memory_space=pltpu.VMEM)
+    return pl.pallas_call(
+        body,
+        out_shape=[pltpu.VMEM((count, 2 * tile, tile), BF16)] * 2,
+        in_specs=[pl.BlockSpec(memory_space=pl.ANY)],
+        out_specs=[spec] * 2,
+        scratch_shapes=[
+            pltpu.VMEM((count, tile, tile), F32),
+            pltpu.SemaphoreType.DMA((pieces,)),
+        ],
+        compiler_params=pltpu.CompilerParams(vmem_limit_bytes=KERNEL_VMEM),
+    )(matrix_tiles)
+
+
+def tile_products(index, parts, tiles, from_row, operand_units, total_units, finish, extra, outputs):
+    count, _, tile = tiles.shape
     scen = parts[0].shape[-2]
     group = min(GROUP, count)
-    piece = min(PIECE, group)
-    pieces = count // piece
+    given = len(parts) + len(extra)
 
     def body(index_ref, tiles_ref, *refs):
         part_refs = refs[: len(parts)]
-        extra_refs = refs[len(parts) : len(parts) + len(extra)]
-        out_refs = refs[len(parts) + len(extra) : -4]
-        held, total, operand, arrived = refs[-4:]
-
-        def copy_of(which):
-            where = pl.ds(which * piece, piece)
-            return pltpu.make_async_copy(tiles_ref.at[where], held.at[where], arrived.at[which])
-
-        for which in range(pieces):
-            copy_of(which).start()
+        extra_refs = refs[len(parts) : given]
+        out_refs = refs[given:-2]
+        total, operand = refs[-2:]
         total[...] = jnp.zeros_like(total)
         per_part = operand_units // len(parts)
         for which, ref in enumerate(part_refs):
@@ -91,56 +138,31 @@
 
         def one_group(step, carry):
             for k in range(group):
-                if k % piece == 0:
-                    copy_of(step * (group // piece) + k // piece).wait()
                 t = step * group + k
                 row = index_ref[t]
                 column = index_ref[count + t]
-                high, low = halves(held[t])
-                if transposed:
-                    operand_at, weights, sides, total_at = (
-                        row,
-                        jnp.concatenate([high, low], 0),
-                        (((1,), (0,)), ((), ())),
-                        column,
-                    )
-                else:
-                    operand_at, weights, sides, total_at = (
-                        column,
-                        jnp.concatenate([high, low], 1),
-                        (((1,), (1,)), ((), ())),
-                        row,
-                    )
-                product = lax.dot_general(
-                    operand[operand_at], weights, sides, preferred_element_type=F32
-                )
-                total[total_at] += product[:scen] + product[scen:]
+                source, target = (row, column) if from_row else (column, row)
+                product = jnp.dot(operand[source], tiles_ref[t], preferred_element_type=F32)
+                total[target] += product[:scen] + product[scen:]
             return carry
 
         lax.fori_loop(0, count // group, one_group, 0)
         finish(part_refs, extra_refs, total, out_refs)
 
-    in_vmem = pl.BlockSpec(memory_space=pltpu.VMEM)
-    return pl.pallas_call(
+    return call_in_vmem(
         body,
-        out_shape=[jax.ShapeDtypeStruct(shape, F32) for shape in outputs],
-        in_specs=[
-            pl.BlockSpec(memory_space=pltpu.SMEM),
-            pl.BlockSpec(memory_space=pl.ANY),
-        ]
-        + [in_vmem] * (len(parts) + len(extra)),
-        out_specs=[in_vmem] * len(outputs),
-        scratch_shapes=[
-            pltpu.VMEM((count, tile, tile), F32),
+        [tiles, *parts, *extra],
+        outputs,
+        [
             pltpu.VMEM((total_units, scen, tile), F32),
             pltpu.VMEM((operand_units, 2 * scen, 2 * tile), BF16),
-            pltpu.SemaphoreType.DMA((pieces,)),
         ],
-    )(index, matrix_tiles, *parts, *extra)
-
-
-def backward_product(index, parts, matrix_tiles, units_row, units_col, sub):
-    scen, tile = parts[0].shape[-2], matrix_tiles.shape[-1]
+        index,
+    )
+
+
+def backward_product(index, parts, tiles, units_row, units_col):
+    scen, tile = parts[0].shape[-2], tiles.shape[-1]
     quarter = units_col // 4
     carried = len(parts) == 2
 
@@ -156,12 +178,12 @@
             out_refs[mask][quarter] = square
 
     return tile_products(
-        index, parts, matrix_tiles, True, units_row, units_col, sub, finish, [],
+        index, parts, tiles, True, units_row, units_col, finish, [],
         [(quarter + 1, scen, tile)] * 4,
     )
 
 
-def forward_product(index, parts, matrix_tiles, right_side, units_row, units_col, sub):
+def forward_product(index, parts, tiles, right_side, units_row, units_col, sub):
     _, scen, tile = parts[0].shape
     quarter = units_col // 4
     half = units_row // 2
@@ -178,7 +200,7 @@
         send[half] = square
 
     return tile_products(
-        index, parts, matrix_tiles, False, units_col, units_row, sub, finish, [right_side],
+        index, parts, tiles, False, units_col, units_row, finish, [right_side],
         [(half + 1, scen, tile)] * 2,
     )
 
@@ -197,7 +219,7 @@
                 lagged = jnp.where(wanted == steps, refs[steps - 1][:, lanes], lagged)
             out_ref[k] = demand_ref[:, lanes] - return_share * lagged
 
-    return call_once(body, (demand_rows, *earlier, lead), ((sub, scen, tile),))[0]
+    return call_in_vmem(body, (demand_rows, *earlier, lead), ((sub, scen, tile),))[0]
 
 
 def next_weight(weight, primal_square, dual_square):
@@ -255,7 +277,7 @@
         outputs.append((scen, tile))
     if last:
         outputs.append((scen, sub * tile))
-    return call_once(body, inputs, outputs)
+    return call_in_vmem(body, inputs, outputs)
 
 
 def dual_update(own, other, duals, weight, sub, last):
@@ -295,7 +317,7 @@
         outputs = [(scen, sub * tile), (scen, tile), (scen, tile)]
     else:
         outputs = [(2 * sub + 1, scen, tile), (scen, tile)]
-    return call_once(body, [own, other, weight, *duals], outputs)
+    return call_in_vmem(body, [own, other, weight, *duals], outputs)
 
 
 def summed(own, axis, others):
@@ -331,6 +353,8 @@
         dual_beside = exchanged(dual_own, "col", 2)
         duals = [dual_own, dual_beside]
         parts = duals + [exchanged(value, "col", 1) for value in duals]
+    with jax.named_scope("tiles"):
+        plain_tiles, turned_tiles = prepared_tiles(matrix_tiles)
     demand_rows = demand.T
     earlier = []
     for steps in range(1, LEAD_MAX + 1):
@@ -346,7 +370,7 @@
     for iteration in range(ITERS):
         last = iteration == ITERS - 1
         with jax.named_scope(f"back_{iteration}"):
-            pieces = backward_product(index, parts, matrix_tiles, units_row, units_col, sub)
+            pieces = backward_product(index, parts, plain_tiles, units_row, units_col)
         total = summed(pieces[0], "band", pieces[1:])
         for bit in order[:-1]:
             half = total.shape[0] // 2
@@ -367,7 +391,7 @@
             ahead = [ahead] + [exchanged(ahead, "band", mask) for mask in range(1, 4)]
         with jax.named_scope(f"fore_{iteration}"):
             keep, send = forward_product(
-                index, ahead, matrix_tiles, right_side, units_row, units_col, sub
+                index, ahead, turned_tiles, right_side, units_row, units_col, sub
             )
         total = keep + exchanged(send, "col", 1)
         results = dual_update(total, exchanged(total, "col", 2), duals, weight, sub, last)

time: 215 us -> 167 us (0.78)
  Pallas kernels: 50.2 us -> 19.5 us
  other arithmetic: 9.24 us -> 1.83 us
  local copies, waits for them, and re-layouts: 9.76 us -> 4.73 us
  starting transfers between devices: 43.5 us -> 41 us
  waiting for transfers between devices: 101 us -> 98.6 us
    pallas_call x13 -> x14, Pallas kernels: 50.2 us -> 19.5 us  [the longest x13 15.6 us: call_in_vmem(): pl.pallas_call(body, out_shape=[pltpu.VMEM(shape, F32) for shape in outpu...]
    unnamed x74 -> x16, local copies, waits for them, and re-layouts: 9.1 us -> 4.67 us
    add x3, other arithmetic: 2.78 us -> 0.05 us  [on_device(): total = keep + exchanged(send, 'col', 1)]
    add x4, other arithmetic: 2.84 us -> 0.12 us  [summed(): return own + got[0] + (got[1] + got[2])]
    ppermute x38, starting transfers between devices: 35.8 us -> 33.3 us  [exchanged(): lax.ppermute(value, axis, [(source, source ^ mask) for source in range(co...]
  transfers between devices with their start and end apart: 42 -> 42, of which waited for: 36 -> 35; matrix products, arithmetic and copies ran while one was open for 1% -> 1% of each run, Pallas kernels for 1% -> 2%
where the time goes in v3:
time: 167 us
  waiting for transfers between devices  98.6 us (59%)
  starting transfers between devices  41 us (25%)
  Pallas kernels  19.5 us (12%)
  local copies, waits for them, and re-layouts  4.73 us (3%)
  other arithmetic  1.83 us (1%)
    ppermute x38, waiting for transfers between devices, exchanged(): lax.ppermute(value, axis, [(source, source ^ mask) for source in range(co...  88.1 us
    ppermute x38, starting transfers between devices, exchanged(): lax.ppermute(value, axis, [(source, source ^ mask) for source in range(co...  33.3 us
    pallas_call x13, Pallas kernels, call_in_vmem(): pl.pallas_call(body, out_shape=[pltpu.VMEM(shape, F32) for shape in outpu...  15.6 us
    ppermute x4, waiting for transfers between devices, passed_along(): lax.ppermute(value, axis, [(source, (source + steps) % count) for source...  10.5 us
    ppermute x4, starting transfers between devices, passed_along(): lax.ppermute(value, axis, [(source, (source + steps) % count) for source...  7.65 us
    unnamed x16, local copies, waits for them, and re-layouts  4.67 us
    pallas_call x1, Pallas kernels, prepared_tiles(): pl.pallas_call(body, out_shape=[pltpu.VMEM((count, 2 * tile, tile), BF16)...  3.86 us
  transfers between devices with their start and end apart: 42, of which 35 were waited for; matrix products, arithmetic and copies ran while one was open for 1% of the time, Pallas kernels for 2%

profile of v3, /device:TPU:0, one launch (start us, length us, event | category | flops | bytes accessed | tf_op | source)
XLA Modules:
  0.0 166.5 jit_solution(11265780508226444930)
XLA Ops:
  1.2 2.6 %collective-permute-start = (f32[16,1024]{1,0:T(8,128)}, f32[16,1024]{1,0:T(8,128)S(1)}, u32[]{:S(2)}, u32[]{:S(2)}) collective-permute-start(f32[16,1024]{1,0:T(8,128)} %bitcast.29), channel_id=1, source_target_pairs={{0,2},{1,3},{2,0},{3,1},{4,6},{5,7},{6,4},{7,5},{8,10},{9,11},{10,... | collective-permute-start | bytes 196616 | tf_op jit(solution)/shard_map/dual_x/ppermute | solution.py:37
  4.4 3.4 %copy-done = f32[1,1,128,128,128]{4,3,2,1,0:T(8,128)S(1)} copy-done((f32[1,1,128,128,128]{4,3,2,1,0:T(8,128)S(1)}, f32[1,1,128,128,128]{4,3,2,1,0:T(8,128)}, u32[]{:S(2)}) %copy-start) | copy-done | bytes 8388632
  7.8 3.9 %tiles.1 = (bf16[128,256,128]{2,1,0:T(8,128)(2,1)S(1)}, bf16[128,256,128]{2,1,0:T(8,128)(2,1)S(1)}) custom-call(f32[128,128,128]{2,1,0:T(8,128)S(1)} %bitcast.27), custom_call_target="tpu_custom_call" | custom-call | tf_op jit(solution)/shard_map/tiles/pallas_call | solution.py:109
  13.0 2.4 %back_0.1 = (f32[17,16,128]{2,1,0:T(8,128)S(1)}, f32[17,16,128]{2,1,0:T(8,128)S(1)}, f32[17,16,128]{2,1,0:T(8,128)S(1)}, f32[17,16,128]{2,1,0:T(8,128)S(1)}) custom-call(s32[256]{0:T(256)S(1)} %pad_add_fusion.index_ref, bf16[128,256,128]{2,1,0:T(8,128)(2,1)S(1)} %get-tuple-element.38.tiles_ref, f32[16,1024]{1,0:T(8,128)S(1)} %bitcast.30, ...), custom_call_target="tpu_custom_call" | custom-call | tf_op jit(solution)/shard_map/back_0/pallas_call | solution.py:65
  19.0 2.3 %collective-permute-done.3 = f32[17,16,128]{2,1,0:T(8,128)S(1)} collective-permute-done((f32[17,16,128]{2,1,0:T(8,128)S(1)}, f32[17,16,128]{2,1,0:T(8,128)S(1)}, u32[]{:S(2)}, u32[]{:S(2)}) %collective-permute-start.3) | collective-permute-done | bytes 139296 | tf_op jit(solution)/shard_map/ppermute | solution.py:37
  21.3 2.3 %collective-permute-done.4 = f32[17,16,128]{2,1,0:T(8,128)S(1)} collective-permute-done((f32[17,16,128]{2,1,0:T(8,128)S(1)}, f32[17,16,128]{2,1,0:T(8,128)S(1)}, u32[]{:S(2)}, u32[]{:S(2)}) %collective-permute-start.4) | collective-permute-done | bytes 139296 | tf_op jit(solution)/shard_map/ppermute | solution.py:37
  25.5 2.6 %collective-permute-start.6 = (f32[17,16,128]{2,1,0:T(8,128)S(1)}, f32[17,16,128]{2,1,0:T(8,128)S(1)}, u32[]{:S(2)}, u32[]{:S(2)}) collective-permute-start(f32[17,16,128]{2,1,0:T(8,128)S(1)} %add_add_fusion.2.refs_0_), channel_id=1, source_target_pairs={{0,16},{4,20},{8,24},{12,28},{16,0},{20,4},{24,8},{28,12},{1,17},{... | collective-permute-start | bytes 417800 | tf_op jit(solution)/shard_map/pair_0/ppermute | solution.py:37
  28.6 10.0 %collective-permute-done.7.refs_3_ = f32[17,1024]{1,0:T(8,128)S(1)} collective-permute-done((f32[17,1024]{1,0:T(8,128)S(1)}, f32[17,1024]{1,0:T(8,128)S(1)}, u32[]{:S(2)}, u32[]{:S(2)}) %collective-permute-start.7) | collective-permute-done | bytes 69664 | tf_op jit(solution)/shard_map/start/ppermute | solution.py:37
  44.1 2.8 %collective-permute-start.13 = (f32[16,1024]{1,0:T(8,128)S(1)}, f32[16,1024]{1,0:T(8,128)S(1)}, u32[]{:S(2)}, u32[]{:S(2)}) collective-permute-start(f32[16,1024]{1,0:T(8,128)S(1)} %bitcast.33), channel_id=1, source_target_pairs={{0,12},{4,16},{8,20},{12,24},{16,28},{20,0},{24,4},{28,8},{1,13},{... | collective-permute-start | bytes 196616 | tf_op jit(solution)/shard_map/lag_3/ppermute | solution.py:42
  48.3 3.0 %collective-permute-start.12 = (f32[16,1024]{1,0:T(8,128)S(1)}, f32[16,1024]{1,0:T(8,128)S(1)}, u32[]{:S(2)}, u32[]{:S(2)}) collective-permute-start(f32[16,1024]{1,0:T(8,128)S(1)} %bitcast.34), channel_id=1, source_target_pairs={{0,8},{4,12},{8,16},{12,20},{16,24},{20,28},{24,0},{28,4},{1,9},{5... | collective-permute-start | bytes 196616 | tf_op jit(solution)/shard_map/lag_2/ppermute | solution.py:42
  51.3 2.2 %collective-permute-done.13.refs_2_ = f32[16,1024]{1,0:T(8,128)S(1)} collective-permute-done((f32[16,1024]{1,0:T(8,128)S(1)}, f32[16,1024]{1,0:T(8,128)S(1)}, u32[]{:S(2)}, u32[]{:S(2)}) %collective-permute-start.13) | collective-permute-done | bytes 65568 | tf_op jit(solution)/shard_map/lag_3/ppermute | solution.py:42
  54.4 6.1 %collective-permute-done.11.refs_0_ = f32[16,1024]{1,0:T(8,128)S(1)} collective-permute-done((f32[16,1024]{1,0:T(8,128)S(1)}, f32[16,1024]{1,0:T(8,128)S(1)}, u32[]{:S(2)}, u32[]{:S(2)}) %collective-permute-start.11) | collective-permute-done | bytes 65568 | tf_op jit(solution)/shard_map/lag_1/ppermute | solution.py:42
  60.5 2.4 %fore_0.1 = (f32[17,16,128]{2,1,0:T(8,128)S(1)}, f32[17,16,128]{2,1,0:T(8,128)S(1)}) custom-call(s32[256]{0:T(256)S(1)} %pad_add_fusion.index_ref, bf16[128,256,128]{2,1,0:T(8,128)(2,1)S(1)} %get-tuple-element.39.tiles_ref, f32[17,16,128]{2,1,0:T(8,128)S(1)} %get-tuple-element.44.refs_0_, f32[17,16,128]{2,1,0:T(8,128)S(1)} %collective-permute-done.8.refs_1_, ...), custom_call_target="tpu_custom_call" | custom-call | tf_op jit(solution)/shard_map/fore_0/pallas_call | solution.py:65
  65.0 5.2 %collective-permute-done.16.refs_1_ = f32[17,16,128]{2,1,0:T(8,128)S(1)} collective-permute-done((f32[17,16,128]{2,1,0:T(8,128)S(1)}, f32[17,16,128]{2,1,0:T(8,128)S(1)}, u32[]{:S(2)}, u32[]{:S(2)}) %collective-permute-start.16) | collective-permute-done | bytes 139296 | tf_op jit(solution)/shard_map/ppermute | solution.py:37
  71.7 2.4 %back_1.1 = (f32[17,16,128]{2,1,0:T(8,128)S(1)}, f32[17,16,128]{2,1,0:T(8,128)S(1)}, f32[17,16,128]{2,1,0:T(8,128)S(1)}, f32[17,16,128]{2,1,0:T(8,128)S(1)}) custom-call(s32[256]{0:T(256)S(1)} %pad_add_fusion.index_ref, bf16[128,256,128]{2,1,0:T(8,128)(2,1)S(1)} %get-tuple-element.38.tiles_ref, f32[17,16,128]{2,1,0:T(8,128)S(1)} %get-tuple-element.47.refs_0_.refs_3_, ...), custom_call_target="tpu_custom_call" | custom-call | tf_op jit(solution)/shard_map/back_1/pallas_call | solution.py:65
  74.2 3.4 %collective-permute-start.20 = (f32[17,16,128]{2,1,0:T(8,128)S(1)}, f32[17,16,128]{2,1,0:T(8,128)S(1)}, u32[]{:S(2)}, u32[]{:S(2)}) collective-permute-start(f32[17,16,128]{2,1,0:T(8,128)S(1)} %get-tuple-element.51), channel_id=1, source_target_pairs={{0,12},{4,8},{8,4},{12,0},{16,28},{20,24},{24,20},{28,16},{1,13},{... | collective-permute-start | bytes 417800 | tf_op jit(solution)/shard_map/ppermute | solution.py:37
  77.6 2.2 %collective-permute-done.18 = f32[17,16,128]{2,1,0:T(8,128)S(1)} collective-permute-done((f32[17,16,128]{2,1,0:T(8,128)S(1)}, f32[17,16,128]{2,1,0:T(8,128)S(1)}, u32[]{:S(2)}, u32[]{:S(2)}) %collective-permute-start.18) | collective-permute-done | bytes 139296 | tf_op jit(solution)/shard_map/ppermute | solution.py:37
  80.7 3.3 %collective-permute-done.20 = f32[17,16,128]{2,1,0:T(8,128)S(1)} collective-permute-done((f32[17,16,128]{2,1,0:T(8,128)S(1)}, f32[17,16,128]{2,1,0:T(8,128)S(1)}, u32[]{:S(2)}, u32[]{:S(2)}) %collective-permute-start.20) | collective-permute-done | bytes 139296 | tf_op jit(solution)/shard_map/ppermute | solution.py:37
  84.1 8.5 %collective-permute-done.21.refs_1_ = f32[17,16,128]{2,1,0:T(8,128)S(1)} collective-permute-done((f32[17,16,128]{2,1,0:T(8,128)S(1)}, f32[17,16,128]{2,1,0:T(8,128)S(1)}, u32[]{:S(2)}, u32[]{:S(2)}) %collective-permute-start.21) | collective-permute-done | bytes 139296 | tf_op jit(solution)/shard_map/pair_1/ppermute | solution.py:37
  96.3 4.0 %collective-permute-done.24.refs_3_ = f32[17,16,128]{2,1,0:T(8,128)S(1)} collective-permute-done((f32[17,16,128]{2,1,0:T(8,128)S(1)}, f32[17,16,128]{2,1,0:T(8,128)S(1)}, u32[]{:S(2)}, u32[]{:S(2)}) %collective-permute-start.24) | collective-permute-done | bytes 139296 | tf_op jit(solution)/shard_map/spread_1/ppermute | solution.py:37
  102.2 2.4 %fore_1.1 = (f32[17,16,128]{2,1,0:T(8,128)S(1)}, f32[17,16,128]{2,1,0:T(8,128)S(1)}) custom-call(s32[256]{0:T(256)S(1)} %pad_add_fusion.index_ref, bf16[128,256,128]{2,1,0:T(8,128)(2,1)S(1)} %get-tuple-element.39.tiles_ref, f32[17,16,128]{2,1,0:T(8,128)S(1)} %get-tuple-element.54.refs_0_, f32[17,16,128]{2,1,0:T(8,128)S(1)} %collective-permute-done.22.refs_1_, ...), custom_call_target="tpu_custom_call" | custom-call | tf_op jit(solution)/shard_map/fore_1/pallas_call | solution.py:65
  106.6 5.2 %collective-permute-done.26.refs_1_ = f32[17,16,128]{2,1,0:T(8,128)S(1)} collective-permute-done((f32[17,16,128]{2,1,0:T(8,128)S(1)}, f32[17,16,128]{2,1,0:T(8,128)S(1)}, u32[]{:S(2)}, u32[]{:S(2)}) %collective-permute-start.26) | collective-permute-done | bytes 139296 | tf_op jit(solution)/shard_map/ppermute | solution.py:37
  113.3 2.4 %back_2.1 = (f32[17,16,128]{2,1,0:T(8,128)S(1)}, f32[17,16,128]{2,1,0:T(8,128)S(1)}, f32[17,16,128]{2,1,0:T(8,128)S(1)}, f32[17,16,128]{2,1,0:T(8,128)S(1)}) custom-call(s32[256]{0:T(256)S(1)} %pad_add_fusion.index_ref, bf16[128,256,128]{2,1,0:T(8,128)(2,1)S(1)} %get-tuple-element.38.tiles_ref, f32[17,16,128]{2,1,0:T(8,128)S(1)} %get-tuple-element.58.refs_0_.refs_3_, ...), custom_call_target="tpu_custom_call" | custom-call | tf_op jit(solution)/shard_map/back_2/pallas_call | solution.py:65
  116.7 2.6 %collective-permute-start.30 = (f32[17,16,128]{2,1,0:T(8,128)S(1)}, f32[17,16,128]{2,1,0:T(8,128)S(1)}, u32[]{:S(2)}, u32[]{:S(2)}) collective-permute-start(f32[17,16,128]{2,1,0:T(8,128)S(1)} %get-tuple-element.62), channel_id=1, source_target_pairs={{0,12},{4,8},{8,4},{12,0},{16,28},{20,24},{24,20},{28,16},{1,13},{... | collective-permute-start | bytes 417800 | tf_op jit(solution)/shard_map/ppermute | solution.py:37
  119.3 2.2 %collective-permute-done.28 = f32[17,16,128]{2,1,0:T(8,128)S(1)} collective-permute-done((f32[17,16,128]{2,1,0:T(8,128)S(1)}, f32[17,16,128]{2,1,0:T(8,128)S(1)}, u32[]{:S(2)}, u32[]{:S(2)}) %collective-permute-start.28) | collective-permute-done | bytes 139296 | tf_op jit(solution)/shard_map/ppermute | solution.py:37
  123.0 2.8 %collective-permute-done.30 = f32[17,16,128]{2,1,0:T(8,128)S(1)} collective-permute-done((f32[17,16,128]{2,1,0:T(8,128)S(1)}, f32[17,16,128]{2,1,0:T(8,128)S(1)}, u32[]{:S(2)}, u32[]{:S(2)}) %collective-permute-start.30) | collective-permute-done | bytes 139296 | tf_op jit(solution)/shard_map/ppermute | solution.py:37
  125.8 8.5 %collective-permute-done.31.refs_1_ = f32[17,16,128]{2,1,0:T(8,128)S(1)} collective-permute-done((f32[17,16,128]{2,1,0:T(8,128)S(1)}, f32[17,16,128]{2,1,0:T(8,128)S(1)}, u32[]{:S(2)}, u32[]{:S(2)}) %collective-permute-start.31) | collective-permute-done | bytes 139296 | tf_op jit(solution)/shard_map/pair_2/ppermute | solution.py:37
  135.1 2.0 %collective-permute-start.33 = (f32[17,16,128]{2,1,0:T(8,128)S(1)}, f32[17,16,128]{2,1,0:T(8,128)S(1)}, u32[]{:S(2)}, u32[]{:S(2)}) collective-permute-start(f32[17,16,128]{2,1,0:T(8,128)S(1)} %get-tuple-element.66.refs_0_), channel_id=1, source_target_pairs={{0,8},{4,12},{8,0},{12,4},{16,24},{20,28},{24,16},{28,20},{1,9},{5... | collective-permute-start | bytes 417800 | tf_op jit(solution)/shard_map/spread_2/ppermute | solution.py:37
  138.6 4.0 %collective-permute-done.34.refs_3_ = f32[17,16,128]{2,1,0:T(8,128)S(1)} collective-permute-done((f32[17,16,128]{2,1,0:T(8,128)S(1)}, f32[17,16,128]{2,1,0:T(8,128)S(1)}, u32[]{:S(2)}, u32[]{:S(2)}) %collective-permute-start.34) | collective-permute-done | bytes 139296 | tf_op jit(solution)/shard_map/spread_2/ppermute | solution.py:37
  144.5 2.4 %fore_2.1 = (f32[17,16,128]{2,1,0:T(8,128)S(1)}, f32[17,16,128]{2,1,0:T(8,128)S(1)}) custom-call(s32[256]{0:T(256)S(1)} %pad_add_fusion.index_ref, bf16[128,256,128]{2,1,0:T(8,128)(2,1)S(1)} %get-tuple-element.39.tiles_ref, f32[17,16,128]{2,1,0:T(8,128)S(1)} %get-tuple-element.66.refs_0_, f32[17,16,128]{2,1,0:T(8,128)S(1)} %collective-permute-done.32.refs_1_, ...), custom_call_target="tpu_custom_call" | custom-call | tf_op jit(solution)/shard_map/fore_2/pallas_call | solution.py:65
  148.9 5.3 %collective-permute-done.36.refs_1_ = f32[17,16,128]{2,1,0:T(8,128)S(1)} collective-permute-done((f32[17,16,128]{2,1,0:T(8,128)S(1)}, f32[17,16,128]{2,1,0:T(8,128)S(1)}, u32[]{:S(2)}, u32[]{:S(2)}) %collective-permute-start.36) | collective-permute-done | bytes 139296 | tf_op jit(solution)/shard_map/ppermute | solution.py:37
  162.5 3.2 %collective-permute-done.41 = f32[16,128]{1,0:T(8,128)S(1)} collective-permute-done((f32[16,128]{1,0:T(8,128)S(1)}, f32[16,128]{1,0:T(8,128)S(1)}, u32[]{:S(2)}, u32[]{:S(2)}) %collective-permute-start.41) | collective-permute-done | bytes 8224 | tf_op jit(solution)/shard_map/ppermute | solution.py:37
  (98 shorter events, 47.7 us)
Async XLA Ops:
  0.6 11.3 %collective-permute-start.1 = (f32[16,1024]{1,0:T(8,128)}, f32[16,1024]{1,0:T(8,128)S(1)}, u32[]{:S(2)}, u32[]{:S(2)}) collective-permute-start(f32[16,1024]{1,0:T(8,128)} %bitcast.28), channel_id=1, source_target_pairs={{0,1},{1,0},{2,3},{3,2},{4,5},{5,4},{6,7},{7,6},{8,9},{9,8},{10,11... | collective-permute-start | bytes 196616 | tf_op jit(solution)/shard_map/dual_x/ppermute | solution.py:37
  1.2 10.5 %collective-permute-start = (f32[16,1024]{1,0:T(8,128)}, f32[16,1024]{1,0:T(8,128)S(1)}, u32[]{:S(2)}, u32[]{:S(2)}) collective-permute-start(f32[16,1024]{1,0:T(8,128)} %bitcast.29), channel_id=1, source_target_pairs={{0,2},{1,3},{2,0},{3,1},{4,6},{5,7},{6,4},{7,5},{8,10},{9,11},{10,... | collective-permute-start | bytes 196616 | tf_op jit(solution)/shard_map/dual_x/ppermute | solution.py:37
  15.5 5.8 %collective-permute-start.3 = (f32[17,16,128]{2,1,0:T(8,128)S(1)}, f32[17,16,128]{2,1,0:T(8,128)S(1)}, u32[]{:S(2)}, u32[]{:S(2)}) collective-permute-start(f32[17,16,128]{2,1,0:T(8,128)S(1)} %get-tuple-element.41), channel_id=1, source_target_pairs={{0,4},{4,0},{8,12},{12,8},{16,20},{20,16},{24,28},{28,24},{1,5},{5... | collective-permute-start | bytes 417800 | tf_op jit(solution)/shard_map/ppermute | solution.py:37
  17.0 6.5 %collective-permute-start.4 = (f32[17,16,128]{2,1,0:T(8,128)S(1)}, f32[17,16,128]{2,1,0:T(8,128)S(1)}, u32[]{:S(2)}, u32[]{:S(2)}) collective-permute-start(f32[17,16,128]{2,1,0:T(8,128)S(1)} %get-tuple-element.42), channel_id=1, source_target_pairs={{0,8},{4,12},{8,0},{12,4},{16,24},{20,28},{24,16},{28,20},{1,9},{5... | collective-permute-start | bytes 417800 | tf_op jit(solution)/shard_map/ppermute | solution.py:37
  18.6 6.8 %collective-permute-start.5 = (f32[17,16,128]{2,1,0:T(8,128)S(1)}, f32[17,16,128]{2,1,0:T(8,128)S(1)}, u32[]{:S(2)}, u32[]{:S(2)}) collective-permute-start(f32[17,16,128]{2,1,0:T(8,128)S(1)} %get-tuple-element.43), channel_id=1, source_target_pairs={{0,12},{4,8},{8,4},{12,0},{16,28},{20,24},{24,20},{28,16},{1,13},{... | collective-permute-start | bytes 417800 | tf_op jit(solution)/shard_map/ppermute | solution.py:37
  25.5 13.1 %collective-permute-start.6 = (f32[17,16,128]{2,1,0:T(8,128)S(1)}, f32[17,16,128]{2,1,0:T(8,128)S(1)}, u32[]{:S(2)}, u32[]{:S(2)}) collective-permute-start(f32[17,16,128]{2,1,0:T(8,128)S(1)} %add_add_fusion.2.refs_0_), channel_id=1, source_target_pairs={{0,16},{4,20},{8,24},{12,28},{16,0},{20,4},{24,8},{28,12},{1,17},{... | collective-permute-start | bytes 417800 | tf_op jit(solution)/shard_map/pair_0/ppermute | solution.py:37
  28.1 10.4 %collective-permute-start.7 = (f32[17,1024]{1,0:T(8,128)S(1)}, f32[17,1024]{1,0:T(8,128)S(1)}, u32[]{:S(2)}, u32[]{:S(2)}) collective-permute-start(f32[17,1024]{1,0:T(8,128)S(1)} %pad_maximum_fusion.refs_2_), channel_id=1, source_target_pairs={{0,16},{4,20},{8,24},{12,28},{16,0},{20,4},{24,8},{28,12},{1,17},{... | collective-permute-start | bytes 208904 | tf_op jit(solution)/shard_map/start/ppermute | solution.py:37
  38.7 21.8 %collective-permute-start.10 = (f32[17,16,128]{2,1,0:T(8,128)S(1)}, f32[17,16,128]{2,1,0:T(8,128)S(1)}, u32[]{:S(2)}, u32[]{:S(2)}) collective-permute-start(f32[17,16,128]{2,1,0:T(8,128)S(1)} %get-tuple-element.44.refs_0_), channel_id=1, source_target_pairs={{0,12},{4,8},{8,4},{12,0},{16,28},{20,24},{24,20},{28,16},{1,13},{... | collective-permute-start | bytes 417800 | tf_op jit(solution)/shard_map/spread_0/ppermute | solution.py:37
  40.1 20.4 %collective-permute-start.9 = (f32[17,16,128]{2,1,0:T(8,128)S(1)}, f32[17,16,128]{2,1,0:T(8,128)S(1)}, u32[]{:S(2)}, u32[]{:S(2)}) collective-permute-start(f32[17,16,128]{2,1,0:T(8,128)S(1)} %get-tuple-element.44.refs_0_), channel_id=1, source_target_pairs={{0,8},{4,12},{8,0},{12,4},{16,24},{20,28},{24,16},{28,20},{1,9},{5... | collective-permute-start | bytes 417800 | tf_op jit(solution)/shard_map/spread_0/ppermute | solution.py:37
  41.4 19.1 %collective-permute-start.8 = (f32[17,16,128]{2,1,0:T(8,128)S(1)}, f32[17,16,128]{2,1,0:T(8,128)S(1)}, u32[]{:S(2)}, u32[]{:S(2)}) collective-permute-start(f32[17,16,128]{2,1,0:T(8,128)S(1)} %get-tuple-element.44.refs_0_), channel_id=1, source_target_pairs={{0,4},{4,0},{8,12},{12,8},{16,20},{20,16},{24,28},{28,24},{1,5},{5... | collective-permute-start | bytes 417800 | tf_op jit(solution)/shard_map/spread_0/ppermute | solution.py:37
  42.3 6.0 %collective-permute-start.14 = (f32[16,1024]{1,0:T(8,128)S(1)}, f32[16,1024]{1,0:T(8,128)S(1)}, u32[]{:S(2)}, u32[]{:S(2)}) collective-permute-start(f32[16,1024]{1,0:T(8,128)S(1)} %bitcast.32), channel_id=1, source_target_pairs={{0,16},{4,20},{8,24},{12,28},{16,0},{20,4},{24,8},{28,12},{1,17},{... | collective-permute-start | bytes 196616 | tf_op jit(solution)/shard_map/lag_4/ppermute | solution.py:42
  44.1 9.4 %collective-permute-start.13 = (f32[16,1024]{1,0:T(8,128)S(1)}, f32[16,1024]{1,0:T(8,128)S(1)}, u32[]{:S(2)}, u32[]{:S(2)}) collective-permute-start(f32[16,1024]{1,0:T(8,128)S(1)} %bitcast.33), channel_id=1, source_target_pairs={{0,12},{4,16},{8,20},{12,24},{16,28},{20,0},{24,4},{28,8},{1,13},{... | collective-permute-start | bytes 196616 | tf_op jit(solution)/shard_map/lag_3/ppermute | solution.py:42
  48.3 6.1 %collective-permute-start.12 = (f32[16,1024]{1,0:T(8,128)S(1)}, f32[16,1024]{1,0:T(8,128)S(1)}, u32[]{:S(2)}, u32[]{:S(2)}) collective-permute-start(f32[16,1024]{1,0:T(8,128)S(1)} %bitcast.34), channel_id=1, source_target_pairs={{0,8},{4,12},{8,16},{12,20},{16,24},{20,28},{24,0},{28,4},{1,9},{5... | collective-permute-start | bytes 196616 | tf_op jit(solution)/shard_map/lag_2/ppermute | solution.py:42
  53.5 7.0 %collective-permute-start.11 = (f32[16,1024]{1,0:T(8,128)S(1)}, f32[16,1024]{1,0:T(8,128)S(1)}, u32[]{:S(2)}, u32[]{:S(2)}) collective-permute-start(f32[16,1024]{1,0:T(8,128)S(1)} %bitcast.35), channel_id=1, source_target_pairs={{0,4},{4,8},{8,12},{12,16},{16,20},{20,24},{24,28},{28,0},{1,5},{5... | collective-permute-start | bytes 196616 | tf_op jit(solution)/shard_map/lag_1/ppermute | solution.py:42
  64.4 5.8 %collective-permute-start.16 = (f32[17,16,128]{2,1,0:T(8,128)S(1)}, f32[17,16,128]{2,1,0:T(8,128)S(1)}, u32[]{:S(2)}, u32[]{:S(2)}) collective-permute-start(f32[17,16,128]{2,1,0:T(8,128)S(1)} %add.106.refs_0_), channel_id=1, source_target_pairs={{0,2},{1,3},{2,0},{3,1},{4,6},{5,7},{6,4},{7,5},{8,10},{9,11},{10,... | collective-permute-start | bytes 417800 | tf_op jit(solution)/shard_map/ppermute | solution.py:37
  74.1 5.8 %collective-permute-start.18 = (f32[17,16,128]{2,1,0:T(8,128)S(1)}, f32[17,16,128]{2,1,0:T(8,128)S(1)}, u32[]{:S(2)}, u32[]{:S(2)}) collective-permute-start(f32[17,16,128]{2,1,0:T(8,128)S(1)} %get-tuple-element.49), channel_id=1, source_target_pairs={{0,4},{4,0},{8,12},{12,8},{16,20},{20,16},{24,28},{28,24},{1,5},{5... | collective-permute-start | bytes 417800 | tf_op jit(solution)/shard_map/ppermute | solution.py:37
  74.1 6.6 %collective-permute-start.19 = (f32[17,16,128]{2,1,0:T(8,128)S(1)}, f32[17,16,128]{2,1,0:T(8,128)S(1)}, u32[]{:S(2)}, u32[]{:S(2)}) collective-permute-start(f32[17,16,128]{2,1,0:T(8,128)S(1)} %get-tuple-element.50), channel_id=1, source_target_pairs={{0,8},{4,12},{8,0},{12,4},{16,24},{20,28},{24,16},{28,20},{1,9},{5... | collective-permute-start | bytes 417800 | tf_op jit(solution)/shard_map/ppermute | solution.py:37
  74.2 9.8 %collective-permute-start.20 = (f32[17,16,128]{2,1,0:T(8,128)S(1)}, f32[17,16,128]{2,1,0:T(8,128)S(1)}, u32[]{:S(2)}, u32[]{:S(2)}) collective-permute-start(f32[17,16,128]{2,1,0:T(8,128)S(1)} %get-tuple-element.51), channel_id=1, source_target_pairs={{0,12},{4,8},{8,4},{12,0},{16,28},{20,24},{24,20},{28,16},{1,13},{... | collective-permute-start | bytes 417800 | tf_op jit(solution)/shard_map/ppermute | solution.py:37
  84.1 8.5 %collective-permute-start.21 = (f32[17,16,128]{2,1,0:T(8,128)S(1)}, f32[17,16,128]{2,1,0:T(8,128)S(1)}, u32[]{:S(2)}, u32[]{:S(2)}) collective-permute-start(f32[17,16,128]{2,1,0:T(8,128)S(1)} %add_add_fusion.1.refs_0_), channel_id=1, source_target_pairs={{0,16},{4,20},{8,24},{12,28},{16,0},{20,4},{24,8},{28,12},{1,17},{... | collective-permute-start | bytes 417800 | tf_op jit(solution)/shard_map/pair_1/ppermute | solution.py:37
  92.8 7.5 %collective-permute-start.24 = (f32[17,16,128]{2,1,0:T(8,128)S(1)}, f32[17,16,128]{2,1,0:T(8,128)S(1)}, u32[]{:S(2)}, u32[]{:S(2)}) collective-permute-start(f32[17,16,128]{2,1,0:T(8,128)S(1)} %get-tuple-element.54.refs_0_), channel_id=1, source_target_pairs={{0,12},{4,8},{8,4},{12,0},{16,28},{20,24},{24,20},{28,16},{1,13},{... | collective-permute-start | bytes 417800 | tf_op jit(solution)/shard_map/spread_1/ppermute | solution.py:37
  92.8 8.0 %collective-permute-start.23 = (f32[17,16,128]{2,1,0:T(8,128)S(1)}, f32[17,16,128]{2,1,0:T(8,128)S(1)}, u32[]{:S(2)}, u32[]{:S(2)}) collective-permute-start(f32[17,16,128]{2,1,0:T(8,128)S(1)} %get-tuple-element.54.refs_0_), channel_id=1, source_target_pairs={{0,8},{4,12},{8,0},{12,4},{16,24},{20,28},{24,16},{28,20},{1,9},{5... | collective-permute-start | bytes 417800 | tf_op jit(solution)/shard_map/spread_1/ppermute | solution.py:37
  94.5 7.7 %collective-permute-start.22 = (f32[17,16,128]{2,1,0:T(8,128)S(1)}, f32[17,16,128]{2,1,0:T(8,128)S(1)}, u32[]{:S(2)}, u32[]{:S(2)}) collective-permute-start(f32[17,16,128]{2,1,0:T(8,128)S(1)} %get-tuple-element.54.refs_0_), channel_id=1, source_target_pairs={{0,4},{4,0},{8,12},{12,8},{16,20},{20,16},{24,28},{28,24},{1,5},{5... | collective-permute-start | bytes 417800 | tf_op jit(solution)/shard_map/spread_1/ppermute | solution.py:37
  106.1 5.8 %collective-permute-start.26 = (f32[17,16,128]{2,1,0:T(8,128)S(1)}, f32[17,16,128]{2,1,0:T(8,128)S(1)}, u32[]{:S(2)}, u32[]{:S(2)}) collective-permute-start(f32[17,16,128]{2,1,0:T(8,128)S(1)} %add.110.refs_0_), channel_id=1, source_target_pairs={{0,2},{1,3},{2,0},{3,1},{4,6},{5,7},{6,4},{7,5},{8,10},{9,11},{10,... | collective-permute-start | bytes 417800 | tf_op jit(solution)/shard_map/ppermute | solution.py:37
  115.8 5.8 %collective-permute-start.28 = (f32[17,16,128]{2,1,0:T(8,128)S(1)}, f32[17,16,128]{2,1,0:T(8,128)S(1)}, u32[]{:S(2)}, u32[]{:S(2)}) collective-permute-start(f32[17,16,128]{2,1,0:T(8,128)S(1)} %get-tuple-element.60), channel_id=1, source_target_pairs={{0,4},{4,0},{8,12},{12,8},{16,20},{20,16},{24,28},{28,24},{1,5},{5... | collective-permute-start | bytes 417800 | tf_op jit(solution)/shard_map/ppermute | solution.py:37
  116.4 6.5 %collective-permute-start.29 = (f32[17,16,128]{2,1,0:T(8,128)S(1)}, f32[17,16,128]{2,1,0:T(8,128)S(1)}, u32[]{:S(2)}, u32[]{:S(2)}) collective-permute-start(f32[17,16,128]{2,1,0:T(8,128)S(1)} %get-tuple-element.61), channel_id=1, source_target_pairs={{0,8},{4,12},{8,0},{12,4},{16,24},{20,28},{24,16},{28,20},{1,9},{5... | collective-permute-start | bytes 417800 | tf_op jit(solution)/shard_map/ppermute | solution.py:37
  116.7 9.0 %collective-permute-start.30 = (f32[17,16,128]{2,1,0:T(8,128)S(1)}, f32[17,16,128]{2,1,0:T(8,128)S(1)}, u32[]{:S(2)}, u32[]{:S(2)}) collective-permute-start(f32[17,16,128]{2,1,0:T(8,128)S(1)} %get-tuple-element.62), channel_id=1, source_target_pairs={{0,12},{4,8},{8,4},{12,0},{16,28},{20,24},{24,20},{28,16},{1,13},{... | collective-permute-start | bytes 417800 | tf_op jit(solution)/shard_map/ppermute | solution.py:37
  125.8 8.5 %collective-permute-start.31 = (f32[17,16,128]{2,1,0:T(8,128)S(1)}, f32[17,16,128]{2,1,0:T(8,128)S(1)}, u32[]{:S(2)}, u32[]{:S(2)}) collective-permute-start(f32[17,16,128]{2,1,0:T(8,128)S(1)} %add_add_fusion.refs_0_), channel_id=1, source_target_pairs={{0,16},{4,20},{8,24},{12,28},{16,0},{20,4},{24,8},{28,12},{1,17},{... | collective-permute-start | bytes 417800 | tf_op jit(solution)/shard_map/pair_2/ppermute | solution.py:37
  135.1 7.4 %collective-permute-start.34 = (f32[17,16,128]{2,1,0:T(8,128)S(1)}, f32[17,16,128]{2,1,0:T(8,128)S(1)}, u32[]{:S(2)}, u32[]{:S(2)}) collective-permute-start(f32[17,16,128]{2,1,0:T(8,128)S(1)} %get-tuple-element.66.refs_0_), channel_id=1, source_target_pairs={{0,12},{4,8},{8,4},{12,0},{16,28},{20,24},{24,20},{28,16},{1,13},{... | collective-permute-start | bytes 417800 | tf_op jit(solution)/shard_map/spread_2/ppermute | solution.py:37
  135.1 8.5 %collective-permute-start.33 = (f32[17,16,128]{2,1,0:T(8,128)S(1)}, f32[17,16,128]{2,1,0:T(8,128)S(1)}, u32[]{:S(2)}, u32[]{:S(2)}) collective-permute-start(f32[17,16,128]{2,1,0:T(8,128)S(1)} %get-tuple-element.66.refs_0_), channel_id=1, source_target_pairs={{0,8},{4,12},{8,0},{12,4},{16,24},{20,28},{24,16},{28,20},{1,9},{5... | collective-permute-start | bytes 417800 | tf_op jit(solution)/shard_map/spread_2/ppermute | solution.py:37
  137.2 7.3 %collective-permute-start.32 = (f32[17,16,128]{2,1,0:T(8,128)S(1)}, f32[17,16,128]{2,1,0:T(8,128)S(1)}, u32[]{:S(2)}, u32[]{:S(2)}) collective-permute-start(f32[17,16,128]{2,1,0:T(8,128)S(1)} %get-tuple-element.66.refs_0_), channel_id=1, source_target_pairs={{0,4},{4,0},{8,12},{12,8},{16,20},{20,16},{24,28},{28,24},{1,5},{5... | collective-permute-start | bytes 417800 | tf_op jit(solution)/shard_map/spread_2/ppermute | solution.py:37
  148.4 5.8 %collective-permute-start.36 = (f32[17,16,128]{2,1,0:T(8,128)S(1)}, f32[17,16,128]{2,1,0:T(8,128)S(1)}, u32[]{:S(2)}, u32[]{:S(2)}) collective-permute-start(f32[17,16,128]{2,1,0:T(8,128)S(1)} %add.114.refs_0_), channel_id=1, source_target_pairs={{0,2},{1,3},{2,0},{3,1},{4,6},{5,7},{6,4},{7,5},{8,10},{9,11},{10,... | collective-permute-start | bytes 417800 | tf_op jit(solution)/shard_map/ppermute | solution.py:37
  155.4 4.5 %collective-permute-start.40 = (f32[16,128]{1,0:T(8,128)S(1)}, f32[16,128]{1,0:T(8,128)S(1)}, u32[]{:S(2)}, u32[]{:S(2)}) collective-permute-start(f32[16,128]{1,0:T(8,128)S(1)} %add.116), channel_id=1, source_target_pairs={{0,12},{4,8},{8,4},{12,0},{16,28},{20,24},{24,20},{28,16},{1,13},{... | collective-permute-start | bytes 24584 | tf_op jit(solution)/shard_map/ppermute | solution.py:37
  (17 other events, 189.3 us)

commit v4 on v3

--- a/solution.py
+++ b/solution.py
@@ -1,3 +1,5 @@
+import math
+
 import jax
 import jax.numpy as jnp
 from jax import lax
@@ -5,11 +7,13 @@
 from jax.experimental.pallas import tpu as pltpu
 from jax.sharding import PartitionSpec as P
 
+
 ITERS = 3
 LEAD_MAX = 4
 GROUP = 32
 PIECE = 8
-KERNEL_VMEM = 24 << 20
+STREAMS = 2
+KERNEL_VMEM = 1 << 20
 
 step_scale = 0.45
 return_share = 0.6
@@ -62,26 +66,28 @@
 def call_in_vmem(body, inputs, outputs, scratch=(), index=None):
     spec = pl.BlockSpec(memory_space=pltpu.VMEM)
     first = [] if index is None else [index]
+    room = KERNEL_VMEM + sum(math.prod(ref.shape) * ref.dtype.itemsize for ref in scratch)
     return pl.pallas_call(
         body,
         out_shape=[pltpu.VMEM(shape, F32) for shape in outputs],
         in_specs=[pl.BlockSpec(memory_space=pltpu.SMEM)] * len(first) + [spec] * len(inputs),
         out_specs=[spec] * len(outputs),
         scratch_shapes=list(scratch),
-        compiler_params=pltpu.CompilerParams(vmem_limit_bytes=KERNEL_VMEM),
+        compiler_params=pltpu.CompilerParams(vmem_limit_bytes=room),
     )(*first, *(in_vmem(array) for array in inputs))
 
 
-def unit_of(ref, k, tile):
-    return ref[:, k * tile : (k + 1) * tile] if len(ref.shape) == 2 else ref[k]
-
-
-def prepared_tiles(matrix_tiles):
+def unit_of(ref, k, tile, rows):
+    return ref[rows, k * tile : (k + 1) * tile] if len(ref.shape) == 2 else ref[k]
+
+
+def prepared(matrix_tiles, primal_rows, cost_row):
     count, tile, _ = matrix_tiles.shape
+    scen, rows = primal_rows.shape
     piece = min(PIECE, count)
     pieces = count // piece
 
-    def body(tiles_ref, plain_ref, turned_ref, held, arrived):
+    def body(tiles_ref, primal_ref, cost_ref, plain_ref, turned_ref, start_ref, held, arrived, small):
         def copy_of(which):
             return pltpu.make_async_copy(
                 tiles_ref.at[pl.ds(which * piece, piece)],
@@ -89,8 +95,12 @@
                 arrived.at[which],
             )
 
+        copy_primal = pltpu.make_async_copy(primal_ref, start_ref.at[pl.ds(0, scen)], small.at[0])
+        copy_cost = pltpu.make_async_copy(cost_ref, start_ref.at[pl.ds(scen, 1)], small.at[1])
         for which in range(pieces):
             copy_of(which).start()
+        copy_primal.start()
+        copy_cost.start()
 
         def one_piece(which, carry):
             copy_of(which).wait()
@@ -104,24 +114,38 @@
             return carry
 
         lax.fori_loop(0, pieces, one_piece, 0)
-
+        copy_primal.wait()
+        copy_cost.wait()
+
+    anywhere = pl.BlockSpec(memory_space=pl.ANY)
     spec = pl.BlockSpec(memory_space=pltpu.VMEM)
+    in_hbm = [
+        pltpu.with_memory_space_constraint(array, pltpu.HBM)
+        for array in (matrix_tiles, primal_rows, cost_row)
+    ]
     return pl.pallas_call(
         body,
-        out_shape=[pltpu.VMEM((count, 2 * tile, tile), BF16)] * 2,
-        in_specs=[pl.BlockSpec(memory_space=pl.ANY)],
-        out_specs=[spec] * 2,
+        out_shape=[
+            pltpu.VMEM((count, 2 * tile, tile), BF16),
+            pltpu.VMEM((count, 2 * tile, tile), BF16),
+            pltpu.VMEM((scen + 1, rows), F32),
+        ],
+        in_specs=[anywhere] * 3,
+        out_specs=[spec] * 3,
         scratch_shapes=[
             pltpu.VMEM((count, tile, tile), F32),
             pltpu.SemaphoreType.DMA((pieces,)),
+            pltpu.SemaphoreType.DMA((2,)),
         ],
-        compiler_params=pltpu.CompilerParams(vmem_limit_bytes=KERNEL_VMEM),
-    )(matrix_tiles)
-
-
-def tile_products(index, parts, tiles, from_row, operand_units, total_units, finish, extra, outputs):
+        compiler_params=pltpu.CompilerParams(
+            vmem_limit_bytes=KERNEL_VMEM + count * tile * tile * 4
+        ),
+    )(*in_hbm)
+
+
+def tile_products(index, parts, tiles, rows, from_row, operand_units, total_units, finish, extra, outputs):
     count, _, tile = tiles.shape
-    scen = parts[0].shape[-2]
+    scen = rows.stop - rows.start
     group = min(GROUP, count)
     given = len(parts) + len(extra)
 
@@ -134,7 +158,7 @@
         per_part = operand_units // len(parts)
         for which, ref in enumerate(part_refs):
             for k in range(per_part):
-                operand[which * per_part + k] = stacked(unit_of(ref, k, tile))
+                operand[which * per_part + k] = stacked(unit_of(ref, k, tile, rows))
 
         def one_group(step, carry):
             for k in range(group):
@@ -161,8 +185,8 @@
     )
 
 
-def backward_product(index, parts, tiles, units_row, units_col):
-    scen, tile = parts[0].shape[-2], tiles.shape[-1]
+def backward_product(index, parts, tiles, rows, units_row, units_col):
+    scen, tile = rows.stop - rows.start, tiles.shape[-1]
     quarter = units_col // 4
     carried = len(parts) == 2
 
@@ -178,12 +202,12 @@
             out_refs[mask][quarter] = square
 
     return tile_products(
-        index, parts, tiles, True, units_row, units_col, finish, [],
+        index, parts, tiles, rows, True, units_row, units_col, finish, [],
         [(quarter + 1, scen, tile)] * 4,
     )
 
 
-def forward_product(index, parts, tiles, right_side, units_row, units_col, sub):
+def forward_product(index, parts, tiles, rows, units_row, units_col):
     _, scen, tile = parts[0].shape
     quarter = units_col // 4
     half = units_row // 2
@@ -191,8 +215,7 @@
     def finish(part_refs, extra_refs, total, out_refs):
         keep, send = out_refs
         for k in range(half):
-            value = total[k]
-            keep[k] = value - extra_refs[0][k] if k < sub else value
+            keep[k] = total[k]
             send[k] = total[half + k]
         squares = [ref[quarter] for ref in part_refs]
         square = (squares[0] + squares[1]) + (squares[2] + squares[3])
@@ -200,26 +223,34 @@
         send[half] = square
 
     return tile_products(
-        index, parts, tiles, False, units_col, units_row, finish, [right_side],
+        index, parts, tiles, rows, False, units_col, units_row, finish, [],
         [(half + 1, scen, tile)] * 2,
     )
 
 
-def right_side_of(demand_rows, earlier, lead, tile):
+def right_sides_of(demand_rows, earlier, lead, tile, share):
     scen, rows = demand_rows.shape
     sub = rows // tile
 
     def body(demand_ref, *refs):
-        lead_ref, out_ref = refs[-2:]
-        for k in range(sub):
-            lanes = slice(k * tile, (k + 1) * tile)
-            wanted = lead_ref[k : k + 1, :]
-            lagged = jnp.zeros((scen, tile), F32)
-            for steps in range(1, LEAD_MAX + 1):
-                lagged = jnp.where(wanted == steps, refs[steps - 1][:, lanes], lagged)
-            out_ref[k] = demand_ref[:, lanes] - return_share * lagged
-
-    return call_in_vmem(body, (demand_rows, *earlier, lead), ((sub, scen, tile),))[0]
+        earlier_refs, lead_ref, out_refs = refs[:LEAD_MAX], refs[LEAD_MAX], refs[LEAD_MAX + 1 :]
+        for half, out_ref in enumerate(out_refs):
+            own = slice(half * share, (half + 1) * share)
+            for k in range(sub):
+                lanes = slice(k * tile, (k + 1) * tile)
+                wanted = lead_ref[k : k + 1, :]
+                lagged = jnp.zeros((share, tile), F32)
+                for steps in range(1, LEAD_MAX + 1):
+                    lagged = jnp.where(wanted == steps, earlier_refs[steps - 1][own, lanes], lagged)
+                out_ref[k] = demand_ref[own, lanes] - return_share * lagged
+            for k in range(sub, 2 * sub + 1):
+                out_ref[k] = jnp.zeros((share, tile), F32)
+
+    return call_in_vmem(
+        body,
+        (demand_rows, *earlier, lead),
+        [(2 * sub + 1, share, tile)] * (scen // share),
+    )
 
 
 def next_weight(weight, primal_square, dual_square):
@@ -229,8 +260,9 @@
     return jnp.sqrt(weight * jnp.sqrt(ratio))
 
 
-def primal_update(own, other, starts, primal, weight, primal_square, sub, last):
+def primal_update(own, other, starts, primal, weight, primal_square, rows, sub, last):
     _, scen, tile = own.shape
+    all_scen = starts[0].shape[0] - 1
     first = primal is None
 
     def body(*refs):
@@ -258,8 +290,8 @@
                 here = chunk * sub + k
                 lanes = slice(k * tile, (k + 1) * tile)
                 pull = own_ref[here] + other_ref[(1 - chunk) * sub + k]
-                before = start_refs[chunk][:scen, lanes] if first else primal_ref[here]
-                cost = start_refs[chunk][scen : scen + 1, lanes]
+                before = start_refs[chunk][rows, lanes] if first else primal_ref[here]
+                cost = start_refs[chunk][all_scen : all_scen + 1, lanes]
                 after = jnp.maximum(before - primal_step * (cost - pull), 0.0)
                 change = after - before
                 square = square + change * change
@@ -280,7 +312,7 @@
     return call_in_vmem(body, inputs, outputs)
 
 
-def dual_update(own, other, duals, weight, sub, last):
+def dual_update(own, other, duals, weight, rows, sub, last):
     _, scen, tile = own.shape
 
     def body(*refs):
@@ -296,7 +328,7 @@
                 here = chunk * sub + k
                 excess = own_ref[here] + other_ref[(1 - chunk) * sub + k]
                 if len(duals) == 2:
-                    before = unit_of(dual_refs[chunk], k, tile)
+                    before = unit_of(dual_refs[chunk], k, tile, rows)
                 else:
                     before = dual_refs[0][here]
                 after = before - dual_step * excess
@@ -325,7 +357,7 @@
     return (own + got[0]) + (got[1] + got[2])
 
 
-def on_device(
+def every_step(
     demand, lead_periods, matrix_tiles, tile_pos, cost_vector, primal_init, dual_init, weight_init
 ):
     band_bits = bit_count(lax.axis_size("band"))
@@ -348,65 +380,81 @@
     )
     index = jnp.concatenate([row_place, column_place])
 
-    with jax.named_scope("dual_x"):
-        dual_own = dual_init.T
-        dual_beside = exchanged(dual_own, "col", 2)
-        duals = [dual_own, dual_beside]
-        parts = duals + [exchanged(value, "col", 1) for value in duals]
-    with jax.named_scope("tiles"):
-        plain_tiles, turned_tiles = prepared_tiles(matrix_tiles)
-    demand_rows = demand.T
+    demand_rows, dual_rows, primal_rows = demand.T, dual_init.T, primal_init.T
+    dual_pair = [dual_rows, exchanged(dual_rows, "col", 2)]
     earlier = []
     for steps in range(1, LEAD_MAX + 1):
-        with jax.named_scope(f"lag_{steps}"):
-            earlier.append(passed_along(demand_rows, "band", steps))
-    right_side = right_side_of(demand_rows, earlier, lead_periods.reshape(sub, tile), tile)
-    with jax.named_scope("start"):
-        start_own = jnp.concatenate([primal_init.T, cost_vector[None, :]])
-        starts = [start_own, exchanged(start_own, "band", 1 << order[-1])]
-    weight = jnp.broadcast_to(weight_init[:, None], (scen, tile))
-    primal = None
-    primal_square = None
-    for iteration in range(ITERS):
+        earlier.append(passed_along(demand_rows, "band", steps))
+    plain_tiles, turned_tiles, start_rows = prepared(
+        matrix_tiles, primal_rows, cost_vector[None, :]
+    )
+    dual_pair += [exchanged(value, "col", 1) for value in dual_pair]
+    start_rows = [start_rows, exchanged(start_rows, "band", 1 << order[-1])]
+    share = scen // STREAMS
+    right_sides = right_sides_of(demand_rows, earlier, lead_periods.reshape(sub, tile), tile, share)
+    states = []
+    for stream in range(STREAMS):
+        rows = slice(stream * share, (stream + 1) * share)
+        states.append(
+            dict(
+                rows=rows,
+                parts=dual_pair,
+                duals=dual_pair[:2],
+                weight=jnp.broadcast_to(weight_init[rows, None], (share, tile)),
+                primal=None,
+                primal_square=None,
+                right_side=right_sides[stream],
+            )
+        )
+
+    def step_of(state, iteration):
         last = iteration == ITERS - 1
-        with jax.named_scope(f"back_{iteration}"):
-            pieces = backward_product(index, parts, plain_tiles, units_row, units_col)
+        rows = state["rows"]
+        pieces = backward_product(index, state["parts"], plain_tiles, rows, units_row, units_col)
         total = summed(pieces[0], "band", pieces[1:])
         for bit in order[:-1]:
             half = total.shape[0] // 2
             send = jnp.concatenate([total[half:-1], total[-1:]])
             total = jnp.concatenate([total[:half], total[-1:]]) + exchanged(send, "band", 1 << bit)
-        with jax.named_scope(f"pair_{iteration}"):
-            other = exchanged(total, "band", 1 << order[-1])
-        results = primal_update(total, other, starts, primal, weight, primal_square, sub, last)
-        primal, ahead = results[:2]
+        other = exchanged(total, "band", 1 << order[-1])
+        results = primal_update(
+            total, other, start_rows, state["primal"], state["weight"],
+            state["primal_square"], rows, sub, last,
+        )
+        state["primal"], ahead = results[:2]
         if iteration:
-            weight = results[2]
+            state["weight"] = results[2]
         if last:
-            primal_rows = results[-1]
+            state["primal_rows"] = results[-1]
         for bit in order[-2::-1]:
             got = exchanged(ahead, "band", 1 << bit)
             ahead = jnp.concatenate([ahead[:-1], got[:-1], ahead[-1:] + got[-1:]])
-        with jax.named_scope(f"spread_{iteration}"):
-            ahead = [ahead] + [exchanged(ahead, "band", mask) for mask in range(1, 4)]
-        with jax.named_scope(f"fore_{iteration}"):
-            keep, send = forward_product(
-                index, ahead, turned_tiles, right_side, units_row, units_col, sub
-            )
-        total = keep + exchanged(send, "col", 1)
-        results = dual_update(total, exchanged(total, "col", 2), duals, weight, sub, last)
-        primal_square = results[1]
+        ahead = [ahead] + [exchanged(ahead, "band", mask) for mask in range(1, 4)]
+        keep, send = forward_product(index, ahead, turned_tiles, rows, units_row, units_col)
+        total = (keep + exchanged(send, "col", 1)) - state["right_side"]
+        other = exchanged(total, "col", 2)
+        results = dual_update(total, other, state["duals"], state["weight"], rows, sub, last)
+        state["primal_square"] = results[1]
         if last:
-            dual_rows, _, square = results
+            state["dual_rows"], _, state["square"] = results
         else:
-            duals = [results[0]]
-            parts = [results[0], exchanged(results[0], "col", 1)]
+            state["duals"] = [results[0]]
+            state["parts"] = [results[0], exchanged(results[0], "col", 1)]
+
+    for iteration in range(ITERS):
+        for state in states:
+            step_of(state, iteration)
+
+    def joined(name):
+        return jnp.concatenate([state[name] for state in states])
+
+    square = joined("square")
     square = square + exchanged(square, "col", 1)
     square = summed(square, "band", [square] * 3)
     for bit in order:
         square = square + exchanged(square, "band", 1 << bit)
-    weight = next_weight(weight, primal_square, square)[:, 0]
-    return (primal_rows.T, dual_rows.T, weight)
+    weight = next_weight(joined("weight"), joined("primal_square"), square)[:, 0]
+    return (joined("primal_rows").T, joined("dual_rows").T, weight)
 
 
 def solution(mesh):
@@ -422,5 +470,5 @@
     )
     out_specs = (P(("band", "col"), None), P(("band", "col"), None), P())
     return jax.shard_map(
-        on_device, mesh=mesh, in_specs=in_specs, out_specs=out_specs, check_vma=False
-    )
+        every_step, mesh=mesh, in_specs=in_specs, out_specs=out_specs, check_vma=False
+    )

time: 167 us -> 152 us (0.910)
  waiting for transfers between devices: 98.6 us -> 40.2 us
  starting transfers between devices: 41 us -> 73.7 us
  Pallas kernels: 19.5 us -> 33 us
  local copies, waits for them, and re-layouts: 4.73 us -> 0.24 us
    ppermute x38 -> x67, waiting for transfers between devices: 88.1 us -> 35.8 us  [exchanged(): lax.ppermute(value, axis, [(source, source ^ mask) for source in range(co...]
    ppermute x38 -> x67, starting transfers between devices: 33.3 us -> 68.1 us  [exchanged(): lax.ppermute(value, axis, [(source, source ^ mask) for source in range(co...]
    pallas_call x13 -> x25, Pallas kernels: 15.6 us -> 28.6 us  [call_in_vmem(): pl.pallas_call(body, out_shape=[pltpu.VMEM(shape, F32) for shape in outpu...]
    ppermute x4, waiting for transfers between devices: 10.5 us -> 4.47 us  [passed_along(): lax.ppermute(value, axis, [(source, (source + steps) % count) for source...]
    unnamed x16 -> x9, local copies, waits for them, and re-layouts: 4.67 us -> 0.02 us
    ppermute x4, starting transfers between devices: 7.65 us -> 5.67 us  [passed_along(): lax.ppermute(value, axis, [(source, (source + steps) % count) for source...]
  transfers between devices with their start and end apart: 42 -> 71, of which waited for: 35 -> 30; matrix products, arithmetic and copies ran while one was open for 1% -> 2% of each run, Pallas kernels for 2% -> 20%
where the time goes in v4:
time: 152 us; the launch traced here: 151 us
  starting transfers between devices  73.7 us (48%)
  waiting for transfers between devices  40.2 us (26%)
  Pallas kernels  33 us (22%)
  other arithmetic  3.11 us (2%)
    ppermute x67, starting transfers between devices, exchanged(): lax.ppermute(value, axis, [(source, source ^ mask) for source in range(co...  68.1 us
    ppermute x67, waiting for transfers between devices, exchanged(): lax.ppermute(value, axis, [(source, source ^ mask) for source in range(co...  35.8 us
    pallas_call x25, Pallas kernels, call_in_vmem(): pl.pallas_call(body, out_shape=[pltpu.VMEM(shape, F32) for shape in outpu...  28.6 us
    ppermute x4, starting transfers between devices, passed_along(): lax.ppermute(value, axis, [(source, (source + steps) % count) for source...  5.67 us
    ppermute x4, waiting for transfers between devices, passed_along(): lax.ppermute(value, axis, [(source, (source + steps) % count) for source...  4.47 us
    pallas_call x1, Pallas kernels, prepared(): pl.pallas_call(body, out_shape=[pltpu.VMEM((count, 2 * tile, tile), BF16)...  4.37 us
  transfers between devices with their start and end apart: 71, of which 30 were waited for; matrix products, arithmetic and copies ran while one was open for 2% of the time, Pallas kernels for 20%

profile of v4, /device:TPU:0, one launch (start us, length us, event | category | flops | bytes accessed | tf_op | source)
XLA Modules:
  0.0 151.4 jit_solution(1256936790831246450)
XLA Ops:
  0.6 3.0 %collective-permute-start = (f32[16,1024]{1,0:T(8,128)}, f32[16,1024]{1,0:T(8,128)S(1)}, u32[]{:S(2)}, u32[]{:S(2)}) collective-permute-start(f32[16,1024]{1,0:T(8,128)} %bitcast.27), channel_id=1, source_target_pairs={{0,2},{1,3},{2,0},{3,1},{4,6},{5,7},{6,4},{7,5},{8,10},{9,11},{10,... | collective-permute-start | bytes 196616 | tf_op jit(solution)/shard_map/ppermute | solution.py:41
  4.4 4.4 %shard_map.103 = (bf16[128,256,128]{2,1,0:T(8,128)(2,1)S(1)}, bf16[128,256,128]{2,1,0:T(8,128)(2,1)S(1)}, f32[17,1024]{1,0:T(8,128)S(1)}) custom-call(f32[128,128,128]{2,1,0:T(8,128)} %bitcast.39, f32[16,1024]{1,0:T(8,128)} %bitcast.40, f32[1,1024]{1,0:T(1,128)} %bitcast.41), custom_call_target="tpu_custom_call" | custom-call | tf_op jit(solution)/shard_map/pallas_call | solution.py:126
  10.2 2.2 %shard_map.104 = (f32[17,8,128]{2,1,0:T(8,128)S(1)}, f32[17,8,128]{2,1,0:T(8,128)S(1)}, f32[17,8,128]{2,1,0:T(8,128)S(1)}, f32[17,8,128]{2,1,0:T(8,128)S(1)}) custom-call(s32[256]{0:T(256)S(1)} %pad_add_fusion.index_ref, bf16[128,256,128]{2,1,0:T(8,128)(2,1)S(1)} %get-tuple-element.74.tiles_ref, f32[16,1024]{1,0:T(8,128)S(1)} %bitcast.29, ...), custom_call_target="tpu_custom_call" | custom-call | tf_op jit(solution)/shard_map/pallas_call | solution.py:70
  16.0 2.6 %collective-permute-start.7 = (f32[17,1024]{1,0:T(8,128)S(1)}, f32[17,1024]{1,0:T(8,128)S(1)}, u32[]{:S(2)}, u32[]{:S(2)}) collective-permute-start(f32[17,1024]{1,0:T(8,128)S(1)} %get-tuple-element.80.refs_2_), channel_id=1, source_target_pairs={{0,16},{4,20},{8,24},{12,28},{16,0},{20,4},{24,8},{28,12},{1,17},{... | collective-permute-start | bytes 208904 | tf_op jit(solution)/shard_map/ppermute | solution.py:41
  20.1 2.2 %shard_map.115 = (f32[17,8,128]{2,1,0:T(8,128)S(1)}, f32[17,8,128]{2,1,0:T(8,128)S(1)}, f32[17,8,128]{2,1,0:T(8,128)S(1)}, f32[17,8,128]{2,1,0:T(8,128)S(1)}) custom-call(s32[256]{0:T(256)S(1)} %pad_add_fusion.index_ref, bf16[128,256,128]{2,1,0:T(8,128)(2,1)S(1)} %get-tuple-element.74.tiles_ref, f32[16,1024]{1,0:T(8,128)S(1)} %bitcast.30, ...), custom_call_target="tpu_custom_call" | custom-call | tf_op jit(solution)/shard_map/pallas_call | solution.py:70
  29.3 2.7 %collective-permute-start.35 = (f32[17,8,128]{2,1,0:T(8,128)S(1)}, f32[17,8,128]{2,1,0:T(8,128)S(1)}, u32[]{:S(2)}, u32[]{:S(2)}) collective-permute-start(f32[17,8,128]{2,1,0:T(8,128)S(1)} %add_add_fusion.2.refs_0_), channel_id=1, source_target_pairs={{0,16},{4,20},{8,24},{12,28},{16,0},{20,4},{24,8},{28,12},{1,17},{... | collective-permute-start | bytes 208904 | tf_op jit(solution)/shard_map/ppermute | solution.py:41
  33.8 2.4 %collective-permute-start.8 = (f32[17,8,128]{2,1,0:T(8,128)S(1)}, f32[17,8,128]{2,1,0:T(8,128)S(1)}, u32[]{:S(2)}, u32[]{:S(2)}) collective-permute-start(f32[17,8,128]{2,1,0:T(8,128)S(1)} %get-tuple-element.81.refs_0_), channel_id=1, source_target_pairs={{0,4},{4,0},{8,12},{12,8},{16,20},{20,16},{24,28},{28,24},{1,5},{5... | collective-permute-start | bytes 208904 | tf_op jit(solution)/shard_map/ppermute | solution.py:41
  43.9 2.2 %shard_map.106 = (f32[17,8,128]{2,1,0:T(8,128)S(1)}, f32[17,8,128]{2,1,0:T(8,128)S(1)}) custom-call(s32[256]{0:T(256)S(1)} %pad_add_fusion.index_ref, bf16[128,256,128]{2,1,0:T(8,128)(2,1)S(1)} %get-tuple-element.75.tiles_ref, f32[17,8,128]{2,1,0:T(8,128)S(1)} %get-tuple-element.81.refs_0_, f32[17,8,128]{2,1,0:T(8,128)S(1)} %collective-permute-done.8.refs_1_, ...), custom_call_target="tpu_custom_call" | custom-call | tf_op jit(solution)/shard_map/pallas_call | solution.py:70
  46.2 2.3 %collective-permute-start.15 = (f32[16,1024]{1,0:T(8,128)S(1)}, f32[16,1024]{1,0:T(8,128)S(1)}, u32[]{:S(2)}, u32[]{:S(2)}) collective-permute-start(f32[16,1024]{1,0:T(8,128)S(1)} %bitcast.36), channel_id=1, source_target_pairs={{0,16},{4,20},{8,24},{12,28},{16,0},{20,4},{24,8},{28,12},{1,17},{... | collective-permute-start | bytes 196616 | tf_op jit(solution)/shard_map/ppermute | solution.py:46
  48.6 4.5 %collective-permute-done.15.refs_3_ = f32[16,1024]{1,0:T(8,128)S(1)} collective-permute-done((f32[16,1024]{1,0:T(8,128)S(1)}, f32[16,1024]{1,0:T(8,128)S(1)}, u32[]{:S(2)}, u32[]{:S(2)}) %collective-permute-start.15) | collective-permute-done | bytes 65568 | tf_op jit(solution)/shard_map/ppermute | solution.py:46
  53.1 2.2 %shard_map.117 = (f32[17,8,128]{2,1,0:T(8,128)S(1)}, f32[17,8,128]{2,1,0:T(8,128)S(1)}) custom-call(s32[256]{0:T(256)S(1)} %pad_add_fusion.index_ref, bf16[128,256,128]{2,1,0:T(8,128)(2,1)S(1)} %get-tuple-element.75.tiles_ref, f32[17,8,128]{2,1,0:T(8,128)S(1)} %get-tuple-element.108.refs_0_, f32[17,8,128]{2,1,0:T(8,128)S(1)} %collective-permute-done.36.refs_1_, ...), custom_call_target="tpu_custom_call" | custom-call | tf_op jit(solution)/shard_map/pallas_call | solution.py:70
  57.6 2.9 %collective-permute-done.16.refs_1_ = f32[17,8,128]{2,1,0:T(8,128)S(1)} collective-permute-done((f32[17,8,128]{2,1,0:T(8,128)S(1)}, f32[17,8,128]{2,1,0:T(8,128)S(1)}, u32[]{:S(2)}, u32[]{:S(2)}) %collective-permute-start.16) | collective-permute-done | bytes 69664 | tf_op jit(solution)/shard_map/ppermute | solution.py:41
  61.9 2.2 %shard_map.109 = (f32[17,8,128]{2,1,0:T(8,128)S(1)}, f32[17,8,128]{2,1,0:T(8,128)S(1)}, f32[17,8,128]{2,1,0:T(8,128)S(1)}, f32[17,8,128]{2,1,0:T(8,128)S(1)}) custom-call(s32[256]{0:T(256)S(1)} %pad_add_fusion.index_ref, bf16[128,256,128]{2,1,0:T(8,128)(2,1)S(1)} %get-tuple-element.74.tiles_ref, f32[17,8,128]{2,1,0:T(8,128)S(1)} %get-tuple-element.85.refs_0_.refs_3_, ...), custom_call_target="tpu_custom_call" | custom-call | tf_op jit(solution)/shard_map/pallas_call | solution.py:70
  65.9 1.8 %collective-permute-start.20 = (f32[17,8,128]{2,1,0:T(8,128)S(1)}, f32[17,8,128]{2,1,0:T(8,128)S(1)}, u32[]{:S(2)}, u32[]{:S(2)}) collective-permute-start(f32[17,8,128]{2,1,0:T(8,128)S(1)} %get-tuple-element.89), channel_id=1, source_target_pairs={{0,12},{4,8},{8,4},{12,0},{16,28},{20,24},{24,20},{28,16},{1,13},{... | collective-permute-start | bytes 208904 | tf_op jit(solution)/shard_map/ppermute | solution.py:41
  67.7 2.2 %shard_map.119 = (f32[17,8,128]{2,1,0:T(8,128)S(1)}, f32[17,8,128]{2,1,0:T(8,128)S(1)}, f32[17,8,128]{2,1,0:T(8,128)S(1)}, f32[17,8,128]{2,1,0:T(8,128)S(1)}) custom-call(s32[256]{0:T(256)S(1)} %pad_add_fusion.index_ref, bf16[128,256,128]{2,1,0:T(8,128)(2,1)S(1)} %get-tuple-element.74.tiles_ref, f32[17,8,128]{2,1,0:T(8,128)S(1)} %get-tuple-element.112.refs_0_.refs_3_, ...), custom_call_target="tpu_custom_call" | custom-call | tf_op jit(solution)/shard_map/pallas_call | solution.py:70
  71.6 1.8 %collective-permute-start.44 = (f32[17,8,128]{2,1,0:T(8,128)S(1)}, f32[17,8,128]{2,1,0:T(8,128)S(1)}, u32[]{:S(2)}, u32[]{:S(2)}) collective-permute-start(f32[17,8,128]{2,1,0:T(8,128)S(1)} %get-tuple-element.116), channel_id=1, source_target_pairs={{0,12},{4,8},{8,4},{12,0},{16,28},{20,24},{24,20},{28,16},{1,13},{... | collective-permute-start | bytes 208904 | tf_op jit(solution)/shard_map/ppermute | solution.py:41
  75.4 1.8 %collective-permute-done.44 = f32[17,8,128]{2,1,0:T(8,128)S(1)} collective-permute-done((f32[17,8,128]{2,1,0:T(8,128)S(1)}, f32[17,8,128]{2,1,0:T(8,128)S(1)}, u32[]{:S(2)}, u32[]{:S(2)}) %collective-permute-start.44) | collective-permute-done | bytes 69664 | tf_op jit(solution)/shard_map/ppermute | solution.py:41
  78.6 2.0 %collective-permute-done.21.refs_1_ = f32[17,8,128]{2,1,0:T(8,128)S(1)} collective-permute-done((f32[17,8,128]{2,1,0:T(8,128)S(1)}, f32[17,8,128]{2,1,0:T(8,128)S(1)}, u32[]{:S(2)}, u32[]{:S(2)}) %collective-permute-start.21) | collective-permute-done | bytes 69664 | tf_op jit(solution)/shard_map/ppermute | solution.py:41
  82.3 2.1 %collective-permute-start.24 = (f32[17,8,128]{2,1,0:T(8,128)S(1)}, f32[17,8,128]{2,1,0:T(8,128)S(1)}, u32[]{:S(2)}, u32[]{:S(2)}) collective-permute-start(f32[17,8,128]{2,1,0:T(8,128)S(1)} %get-tuple-element.92.refs_0_), channel_id=1, source_target_pairs={{0,12},{4,8},{8,4},{12,0},{16,28},{20,24},{24,20},{28,16},{1,13},{... | collective-permute-start | bytes 208904 | tf_op jit(solution)/shard_map/ppermute | solution.py:41
  86.0 2.1 %collective-permute-start.48 = (f32[17,8,128]{2,1,0:T(8,128)S(1)}, f32[17,8,128]{2,1,0:T(8,128)S(1)}, u32[]{:S(2)}, u32[]{:S(2)}) collective-permute-start(f32[17,8,128]{2,1,0:T(8,128)S(1)} %get-tuple-element.119.refs_0_), channel_id=1, source_target_pairs={{0,12},{4,8},{8,4},{12,0},{16,28},{20,24},{24,20},{28,16},{1,13},{... | collective-permute-start | bytes 208904 | tf_op jit(solution)/shard_map/ppermute | solution.py:41
  88.1 2.2 %shard_map.111 = (f32[17,8,128]{2,1,0:T(8,128)S(1)}, f32[17,8,128]{2,1,0:T(8,128)S(1)}) custom-call(s32[256]{0:T(256)S(1)} %pad_add_fusion.index_ref, bf16[128,256,128]{2,1,0:T(8,128)(2,1)S(1)} %get-tuple-element.75.tiles_ref, f32[17,8,128]{2,1,0:T(8,128)S(1)} %get-tuple-element.92.refs_0_, f32[17,8,128]{2,1,0:T(8,128)S(1)} %collective-permute-done.22.refs_1_, ...), custom_call_target="tpu_custom_call" | custom-call | tf_op jit(solution)/shard_map/pallas_call | solution.py:70
  91.2 2.2 %shard_map.121 = (f32[17,8,128]{2,1,0:T(8,128)S(1)}, f32[17,8,128]{2,1,0:T(8,128)S(1)}) custom-call(s32[256]{0:T(256)S(1)} %pad_add_fusion.index_ref, bf16[128,256,128]{2,1,0:T(8,128)(2,1)S(1)} %get-tuple-element.75.tiles_ref, f32[17,8,128]{2,1,0:T(8,128)S(1)} %get-tuple-element.119.refs_0_, f32[17,8,128]{2,1,0:T(8,128)S(1)} %collective-permute-done.46.refs_1_, ...), custom_call_target="tpu_custom_call" | custom-call | tf_op jit(solution)/shard_map/pallas_call | solution.py:70
  95.8 2.9 %collective-permute-done.26.refs_1_ = f32[17,8,128]{2,1,0:T(8,128)S(1)} collective-permute-done((f32[17,8,128]{2,1,0:T(8,128)S(1)}, f32[17,8,128]{2,1,0:T(8,128)S(1)}, u32[]{:S(2)}, u32[]{:S(2)}) %collective-permute-start.26) | collective-permute-done | bytes 69664 | tf_op jit(solution)/shard_map/ppermute | solution.py:41
  100.0 2.2 %shard_map.113 = (f32[17,8,128]{2,1,0:T(8,128)S(1)}, f32[17,8,128]{2,1,0:T(8,128)S(1)}, f32[17,8,128]{2,1,0:T(8,128)S(1)}, f32[17,8,128]{2,1,0:T(8,128)S(1)}) custom-call(s32[256]{0:T(256)S(1)} %pad_add_fusion.index_ref, bf16[128,256,128]{2,1,0:T(8,128)(2,1)S(1)} %get-tuple-element.74.tiles_ref, f32[17,8,128]{2,1,0:T(8,128)S(1)} %get-tuple-element.96.refs_0_.refs_3_, ...), custom_call_target="tpu_custom_call" | custom-call | tf_op jit(solution)/shard_map/pallas_call | solution.py:70
  105.8 2.2 %shard_map.123 = (f32[17,8,128]{2,1,0:T(8,128)S(1)}, f32[17,8,128]{2,1,0:T(8,128)S(1)}, f32[17,8,128]{2,1,0:T(8,128)S(1)}, f32[17,8,128]{2,1,0:T(8,128)S(1)}) custom-call(s32[256]{0:T(256)S(1)} %pad_add_fusion.index_ref, bf16[128,256,128]{2,1,0:T(8,128)(2,1)S(1)} %get-tuple-element.74.tiles_ref, f32[17,8,128]{2,1,0:T(8,128)S(1)} %get-tuple-element.123.refs_0_.refs_3_, ...), custom_call_target="tpu_custom_call" | custom-call | tf_op jit(solution)/shard_map/pallas_call | solution.py:70
  111.6 2.0 %collective-permute-start.31 = (f32[17,8,128]{2,1,0:T(8,128)S(1)}, f32[17,8,128]{2,1,0:T(8,128)S(1)}, u32[]{:S(2)}, u32[]{:S(2)}) collective-permute-start(f32[17,8,128]{2,1,0:T(8,128)S(1)} %add_add_fusion.3.refs_0_), channel_id=1, source_target_pairs={{0,16},{4,20},{8,24},{12,28},{16,0},{20,4},{24,8},{28,12},{1,17},{... | collective-permute-start | bytes 208904 | tf_op jit(solution)/shard_map/ppermute | solution.py:41
  126.5 2.2 %shard_map.125 = (f32[17,8,128]{2,1,0:T(8,128)S(1)}, f32[17,8,128]{2,1,0:T(8,128)S(1)}) custom-call(s32[256]{0:T(256)S(1)} %pad_add_fusion.index_ref, bf16[128,256,128]{2,1,0:T(8,128)(2,1)S(1)} %get-tuple-element.75.tiles_ref, f32[17,8,128]{2,1,0:T(8,128)S(1)} %get-tuple-element.131.refs_0_, f32[17,8,128]{2,1,0:T(8,128)S(1)} %collective-permute-done.56.refs_1_, ...), custom_call_target="tpu_custom_call" | custom-call | tf_op jit(solution)/shard_map/pallas_call | solution.py:70
  130.2 2.2 %shard_map.127 = (f32[17,8,128]{2,1,0:T(8,128)S(1)}, f32[17,8,128]{2,1,0:T(8,128)S(1)}) custom-call(s32[256]{0:T(256)S(1)} %pad_add_fusion.index_ref, bf16[128,256,128]{2,1,0:T(8,128)(2,1)S(1)} %get-tuple-element.75.tiles_ref, f32[17,8,128]{2,1,0:T(8,128)S(1)} %get-tuple-element.136.refs_0_, f32[17,8,128]{2,1,0:T(8,128)S(1)} %collective-permute-done.61.refs_1_, ...), custom_call_target="tpu_custom_call" | custom-call | tf_op jit(solution)/shard_map/pallas_call | solution.py:70
  134.7 2.9 %collective-permute-done.60.refs_1_ = f32[17,8,128]{2,1,0:T(8,128)S(1)} collective-permute-done((f32[17,8,128]{2,1,0:T(8,128)S(1)}, f32[17,8,128]{2,1,0:T(8,128)S(1)}, u32[]{:S(2)}, u32[]{:S(2)}) %collective-permute-start.60) | collective-permute-done | bytes 69664 | tf_op jit(solution)/shard_map/ppermute | solution.py:41
  141.4 2.0 %collective-permute-start.69 = (f32[16,128]{1,0:T(8,128)S(1)}, f32[16,128]{1,0:T(8,128)S(1)}, u32[]{:S(2)}, u32[]{:S(2)}) collective-permute-start(f32[16,128]{1,0:T(8,128)S(1)} %add.164), channel_id=1, source_target_pairs={{0,12},{4,8},{8,4},{12,0},{16,28},{20,24},{24,20},{28,16},{1,13},{... | collective-permute-start | bytes 24584 | tf_op jit(solution)/shard_map/ppermute | solution.py:41
  146.0 2.0 %collective-permute-start.70 = (f32[16,128]{1,0:T(8,128)S(1)}, f32[16,128]{1,0:T(8,128)S(1)}, u32[]{:S(2)}, u32[]{:S(2)}) collective-permute-start(f32[16,128]{1,0:T(8,128)S(1)} %add_add_fusion.6), channel_id=1, source_target_pairs={{0,16},{4,20},{8,24},{12,28},{16,0},{20,4},{24,8},{28,12},{1,17},{... | collective-permute-start | bytes 24584 | tf_op jit(solution)/shard_map/ppermute | solution.py:41
  148.7 1.8 %collective-permute-done.70 = f32[16,128]{1,0:T(8,128)S(1)} collective-permute-done((f32[16,128]{1,0:T(8,128)S(1)}, f32[16,128]{1,0:T(8,128)S(1)}, u32[]{:S(2)}, u32[]{:S(2)}) %collective-permute-start.70) | collective-permute-done | bytes 8224 | tf_op jit(solution)/shard_map/ppermute | solution.py:41
  (171 shorter events, 73.5 us)
Async XLA Ops:
  0.6 8.1 %collective-permute-start = (f32[16,1024]{1,0:T(8,128)}, f32[16,1024]{1,0:T(8,128)S(1)}, u32[]{:S(2)}, u32[]{:S(2)}) collective-permute-start(f32[16,1024]{1,0:T(8,128)} %bitcast.27), channel_id=1, source_target_pairs={{0,2},{1,3},{2,0},{3,1},{4,6},{5,7},{6,4},{7,5},{8,10},{9,11},{10,... | collective-permute-start | bytes 196616 | tf_op jit(solution)/shard_map/ppermute | solution.py:41
  12.4 9.9 %collective-permute-start.3 = (f32[17,8,128]{2,1,0:T(8,128)S(1)}, f32[17,8,128]{2,1,0:T(8,128)S(1)}, u32[]{:S(2)}, u32[]{:S(2)}) collective-permute-start(f32[17,8,128]{2,1,0:T(8,128)S(1)} %get-tuple-element.77), channel_id=1, source_target_pairs={{0,4},{4,0},{8,12},{12,8},{16,20},{20,16},{24,28},{28,24},{1,5},{5... | collective-permute-start | bytes 208904 | tf_op jit(solution)/shard_map/ppermute | solution.py:41
  14.0 9.9 %collective-permute-start.4 = (f32[17,8,128]{2,1,0:T(8,128)S(1)}, f32[17,8,128]{2,1,0:T(8,128)S(1)}, u32[]{:S(2)}, u32[]{:S(2)}) collective-permute-start(f32[17,8,128]{2,1,0:T(8,128)S(1)} %get-tuple-element.78), channel_id=1, source_target_pairs={{0,8},{4,12},{8,0},{12,4},{16,24},{20,28},{24,16},{28,20},{1,9},{5... | collective-permute-start | bytes 208904 | tf_op jit(solution)/shard_map/ppermute | solution.py:41
  15.6 8.4 %collective-permute-start.5 = (f32[17,8,128]{2,1,0:T(8,128)S(1)}, f32[17,8,128]{2,1,0:T(8,128)S(1)}, u32[]{:S(2)}, u32[]{:S(2)}) collective-permute-start(f32[17,8,128]{2,1,0:T(8,128)S(1)} %get-tuple-element.79), channel_id=1, source_target_pairs={{0,12},{4,8},{8,4},{12,0},{16,28},{20,24},{24,20},{28,16},{1,13},{... | collective-permute-start | bytes 208904 | tf_op jit(solution)/shard_map/ppermute | solution.py:41
  16.0 16.1 %collective-permute-start.7 = (f32[17,1024]{1,0:T(8,128)S(1)}, f32[17,1024]{1,0:T(8,128)S(1)}, u32[]{:S(2)}, u32[]{:S(2)}) collective-permute-start(f32[17,1024]{1,0:T(8,128)S(1)} %get-tuple-element.80.refs_2_), channel_id=1, source_target_pairs={{0,16},{4,20},{8,24},{12,28},{16,0},{20,4},{24,8},{28,12},{1,17},{... | collective-permute-start | bytes 208904 | tf_op jit(solution)/shard_map/ppermute | solution.py:41
  18.6 18.7 %collective-permute-start.12 = (f32[16,1024]{1,0:T(8,128)S(1)}, f32[16,1024]{1,0:T(8,128)S(1)}, u32[]{:S(2)}, u32[]{:S(2)}) collective-permute-start(f32[16,1024]{1,0:T(8,128)S(1)} %bitcast.33), channel_id=1, source_target_pairs={{0,4},{4,8},{8,12},{12,16},{16,20},{20,24},{24,28},{28,0},{1,5},{5... | collective-permute-start | bytes 196616 | tf_op jit(solution)/shard_map/ppermute | solution.py:46
  27.6 6.0 %collective-permute-start.6 = (f32[17,8,128]{2,1,0:T(8,128)S(1)}, f32[17,8,128]{2,1,0:T(8,128)S(1)}, u32[]{:S(2)}, u32[]{:S(2)}) collective-permute-start(f32[17,8,128]{2,1,0:T(8,128)S(1)} %add_add_fusion.5.refs_0_), channel_id=1, source_target_pairs={{0,16},{4,20},{8,24},{12,28},{16,0},{20,4},{24,8},{28,12},{1,17},{... | collective-permute-start | bytes 208904 | tf_op jit(solution)/shard_map/ppermute | solution.py:41
  29.3 9.0 %collective-permute-start.35 = (f32[17,8,128]{2,1,0:T(8,128)S(1)}, f32[17,8,128]{2,1,0:T(8,128)S(1)}, u32[]{:S(2)}, u32[]{:S(2)}) collective-permute-start(f32[17,8,128]{2,1,0:T(8,128)S(1)} %add_add_fusion.2.refs_0_), channel_id=1, source_target_pairs={{0,16},{4,20},{8,24},{12,28},{16,0},{20,4},{24,8},{28,12},{1,17},{... | collective-permute-start | bytes 208904 | tf_op jit(solution)/shard_map/ppermute | solution.py:41
  33.8 6.6 %collective-permute-start.10 = (f32[17,8,128]{2,1,0:T(8,128)S(1)}, f32[17,8,128]{2,1,0:T(8,128)S(1)}, u32[]{:S(2)}, u32[]{:S(2)}) collective-permute-start(f32[17,8,128]{2,1,0:T(8,128)S(1)} %get-tuple-element.81.refs_0_), channel_id=1, source_target_pairs={{0,12},{4,8},{8,4},{12,0},{16,28},{20,24},{24,20},{28,16},{1,13},{... | collective-permute-start | bytes 208904 | tf_op jit(solution)/shard_map/ppermute | solution.py:41
  33.8 7.7 %collective-permute-start.8 = (f32[17,8,128]{2,1,0:T(8,128)S(1)}, f32[17,8,128]{2,1,0:T(8,128)S(1)}, u32[]{:S(2)}, u32[]{:S(2)}) collective-permute-start(f32[17,8,128]{2,1,0:T(8,128)S(1)} %get-tuple-element.81.refs_0_), channel_id=1, source_target_pairs={{0,4},{4,0},{8,12},{12,8},{16,20},{20,16},{24,28},{28,24},{1,5},{5... | collective-permute-start | bytes 208904 | tf_op jit(solution)/shard_map/ppermute | solution.py:41
  36.3 7.1 %collective-permute-start.9 = (f32[17,8,128]{2,1,0:T(8,128)S(1)}, f32[17,8,128]{2,1,0:T(8,128)S(1)}, u32[]{:S(2)}, u32[]{:S(2)}) collective-permute-start(f32[17,8,128]{2,1,0:T(8,128)S(1)} %get-tuple-element.81.refs_0_), channel_id=1, source_target_pairs={{0,8},{4,12},{8,0},{12,4},{16,24},{20,28},{24,16},{28,20},{1,9},{5... | collective-permute-start | bytes 208904 | tf_op jit(solution)/shard_map/ppermute | solution.py:41
  37.3 8.8 %collective-permute-start.13 = (f32[16,1024]{1,0:T(8,128)S(1)}, f32[16,1024]{1,0:T(8,128)S(1)}, u32[]{:S(2)}, u32[]{:S(2)}) collective-permute-start(f32[16,1024]{1,0:T(8,128)S(1)} %bitcast.34), channel_id=1, source_target_pairs={{0,8},{4,12},{8,16},{12,20},{16,24},{20,28},{24,0},{28,4},{1,9},{5... | collective-permute-start | bytes 196616 | tf_op jit(solution)/shard_map/ppermute | solution.py:46
  38.3 7.9 %collective-permute-start.14 = (f32[16,1024]{1,0:T(8,128)S(1)}, f32[16,1024]{1,0:T(8,128)S(1)}, u32[]{:S(2)}, u32[]{:S(2)}) collective-permute-start(f32[16,1024]{1,0:T(8,128)S(1)} %bitcast.35), channel_id=1, source_target_pairs={{0,12},{4,16},{8,20},{12,24},{16,28},{20,0},{24,4},{28,8},{1,13},{... | collective-permute-start | bytes 196616 | tf_op jit(solution)/shard_map/ppermute | solution.py:46
  40.4 12.7 %collective-permute-start.36 = (f32[17,8,128]{2,1,0:T(8,128)S(1)}, f32[17,8,128]{2,1,0:T(8,128)S(1)}, u32[]{:S(2)}, u32[]{:S(2)}) collective-permute-start(f32[17,8,128]{2,1,0:T(8,128)S(1)} %get-tuple-element.108.refs_0_), channel_id=1, source_target_pairs={{0,4},{4,0},{8,12},{12,8},{16,20},{20,16},{24,28},{28,24},{1,5},{5... | collective-permute-start | bytes 208904 | tf_op jit(solution)/shard_map/ppermute | solution.py:41
  41.6 11.5 %collective-permute-start.37 = (f32[17,8,128]{2,1,0:T(8,128)S(1)}, f32[17,8,128]{2,1,0:T(8,128)S(1)}, u32[]{:S(2)}, u32[]{:S(2)}) collective-permute-start(f32[17,8,128]{2,1,0:T(8,128)S(1)} %get-tuple-element.108.refs_0_), channel_id=1, source_target_pairs={{0,8},{4,12},{8,0},{12,4},{16,24},{20,28},{24,16},{28,20},{1,9},{5... | collective-permute-start | bytes 208904 | tf_op jit(solution)/shard_map/ppermute | solution.py:41
  43.4 9.7 %collective-permute-start.38 = (f32[17,8,128]{2,1,0:T(8,128)S(1)}, f32[17,8,128]{2,1,0:T(8,128)S(1)}, u32[]{:S(2)}, u32[]{:S(2)}) collective-permute-start(f32[17,8,128]{2,1,0:T(8,128)S(1)} %get-tuple-element.108.refs_0_), channel_id=1, source_target_pairs={{0,12},{4,8},{8,4},{12,0},{16,28},{20,24},{24,20},{28,16},{1,13},{... | collective-permute-start | bytes 208904 | tf_op jit(solution)/shard_map/ppermute | solution.py:41
  46.2 9.3 %collective-permute-start.11 = (f32[17,8,128]{2,1,0:T(8,128)S(1)}, f32[17,8,128]{2,1,0:T(8,128)S(1)}, u32[]{:S(2)}, u32[]{:S(2)}) collective-permute-start(f32[17,8,128]{2,1,0:T(8,128)S(1)} %get-tuple-element.83), channel_id=1, source_target_pairs={{0,1},{1,0},{2,3},{3,2},{4,5},{5,4},{6,7},{7,6},{8,9},{9,8},{10,11... | collective-permute-start | bytes 208904 | tf_op jit(solution)/shard_map/ppermute | solution.py:41
  46.2 6.8 %collective-permute-start.15 = (f32[16,1024]{1,0:T(8,128)S(1)}, f32[16,1024]{1,0:T(8,128)S(1)}, u32[]{:S(2)}, u32[]{:S(2)}) collective-permute-start(f32[16,1024]{1,0:T(8,128)S(1)} %bitcast.36), channel_id=1, source_target_pairs={{0,16},{4,20},{8,24},{12,28},{16,0},{20,4},{24,8},{28,12},{1,17},{... | collective-permute-start | bytes 196616 | tf_op jit(solution)/shard_map/ppermute | solution.py:46
  61.6 6.1 %collective-permute-start.41 = (f32[17,8,128]{2,1,0:T(8,128)S(1)}, f32[17,8,128]{2,1,0:T(8,128)S(1)}, u32[]{:S(2)}, u32[]{:S(2)}) collective-permute-start(f32[17,8,128]{2,1,0:T(8,128)S(1)} %get-tuple-element.112.refs_0_.refs_3_), channel_id=1, source_target_pairs={{0,1},{1,0},{2,3},{3,2},{4,5},{5,4},{6,7},{7,6},{8,9},{9,8},{10,11... | collective-permute-start | bytes 208904 | tf_op jit(solution)/shard_map/ppermute | solution.py:41
  64.1 7.5 %collective-permute-start.18 = (f32[17,8,128]{2,1,0:T(8,128)S(1)}, f32[17,8,128]{2,1,0:T(8,128)S(1)}, u32[]{:S(2)}, u32[]{:S(2)}) collective-permute-start(f32[17,8,128]{2,1,0:T(8,128)S(1)} %get-tuple-element.87), channel_id=1, source_target_pairs={{0,4},{4,0},{8,12},{12,8},{16,20},{20,16},{24,28},{28,24},{1,5},{5... | collective-permute-start | bytes 208904 | tf_op jit(solution)/shard_map/ppermute | solution.py:41
  65.3 8.1 %collective-permute-start.19 = (f32[17,8,128]{2,1,0:T(8,128)S(1)}, f32[17,8,128]{2,1,0:T(8,128)S(1)}, u32[]{:S(2)}, u32[]{:S(2)}) collective-permute-start(f32[17,8,128]{2,1,0:T(8,128)S(1)} %get-tuple-element.88), channel_id=1, source_target_pairs={{0,8},{4,12},{8,0},{12,4},{16,24},{20,28},{24,16},{28,20},{1,9},{5... | collective-permute-start | bytes 208904 | tf_op jit(solution)/shard_map/ppermute | solution.py:41
  65.9 7.6 %collective-permute-start.20 = (f32[17,8,128]{2,1,0:T(8,128)S(1)}, f32[17,8,128]{2,1,0:T(8,128)S(1)}, u32[]{:S(2)}, u32[]{:S(2)}) collective-permute-start(f32[17,8,128]{2,1,0:T(8,128)S(1)} %get-tuple-element.89), channel_id=1, source_target_pairs={{0,12},{4,8},{8,4},{12,0},{16,28},{20,24},{24,20},{28,16},{1,13},{... | collective-permute-start | bytes 208904 | tf_op jit(solution)/shard_map/ppermute | solution.py:41
  73.5 7.2 %collective-permute-start.21 = (f32[17,8,128]{2,1,0:T(8,128)S(1)}, f32[17,8,128]{2,1,0:T(8,128)S(1)}, u32[]{:S(2)}, u32[]{:S(2)}) collective-permute-start(f32[17,8,128]{2,1,0:T(8,128)S(1)} %add_add_fusion.4.refs_0_), channel_id=1, source_target_pairs={{0,16},{4,20},{8,24},{12,28},{16,0},{20,4},{24,8},{28,12},{1,17},{... | collective-permute-start | bytes 208904 | tf_op jit(solution)/shard_map/ppermute | solution.py:41
  77.3 7.1 %collective-permute-start.45 = (f32[17,8,128]{2,1,0:T(8,128)S(1)}, f32[17,8,128]{2,1,0:T(8,128)S(1)}, u32[]{:S(2)}, u32[]{:S(2)}) collective-permute-start(f32[17,8,128]{2,1,0:T(8,128)S(1)} %add_add_fusion.1.refs_0_), channel_id=1, source_target_pairs={{0,16},{4,20},{8,24},{12,28},{16,0},{20,4},{24,8},{28,12},{1,17},{... | collective-permute-start | bytes 208904 | tf_op jit(solution)/shard_map/ppermute | solution.py:41
  84.5 5.9 %collective-permute-start.46 = (f32[17,8,128]{2,1,0:T(8,128)S(1)}, f32[17,8,128]{2,1,0:T(8,128)S(1)}, u32[]{:S(2)}, u32[]{:S(2)}) collective-permute-start(f32[17,8,128]{2,1,0:T(8,128)S(1)} %get-tuple-element.119.refs_0_), channel_id=1, source_target_pairs={{0,4},{4,0},{8,12},{12,8},{16,20},{20,16},{24,28},{28,24},{1,5},{5... | collective-permute-start | bytes 208904 | tf_op jit(solution)/shard_map/ppermute | solution.py:41
  99.7 6.1 %collective-permute-start.51 = (f32[17,8,128]{2,1,0:T(8,128)S(1)}, f32[17,8,128]{2,1,0:T(8,128)S(1)}, u32[]{:S(2)}, u32[]{:S(2)}) collective-permute-start(f32[17,8,128]{2,1,0:T(8,128)S(1)} %get-tuple-element.123.refs_0_.refs_3_), channel_id=1, source_target_pairs={{0,1},{1,0},{2,3},{3,2},{4,5},{5,4},{6,7},{7,6},{8,9},{9,8},{10,11... | collective-permute-start | bytes 208904 | tf_op jit(solution)/shard_map/ppermute | solution.py:41
  102.3 8.5 %collective-permute-start.28 = (f32[17,8,128]{2,1,0:T(8,128)S(1)}, f32[17,8,128]{2,1,0:T(8,128)S(1)}, u32[]{:S(2)}, u32[]{:S(2)}) collective-permute-start(f32[17,8,128]{2,1,0:T(8,128)S(1)} %get-tuple-element.98), channel_id=1, source_target_pairs={{0,4},{4,0},{8,12},{12,8},{16,20},{20,16},{24,28},{28,24},{1,5},{5... | collective-permute-start | bytes 208904 | tf_op jit(solution)/shard_map/ppermute | solution.py:41
  103.6 8.0 %collective-permute-start.29 = (f32[17,8,128]{2,1,0:T(8,128)S(1)}, f32[17,8,128]{2,1,0:T(8,128)S(1)}, u32[]{:S(2)}, u32[]{:S(2)}) collective-permute-start(f32[17,8,128]{2,1,0:T(8,128)S(1)} %get-tuple-element.99), channel_id=1, source_target_pairs={{0,8},{4,12},{8,0},{12,4},{16,24},{20,28},{24,16},{28,20},{1,9},{5... | collective-permute-start | bytes 208904 | tf_op jit(solution)/shard_map/ppermute | solution.py:41
  104.9 6.7 %collective-permute-start.30 = (f32[17,8,128]{2,1,0:T(8,128)S(1)}, f32[17,8,128]{2,1,0:T(8,128)S(1)}, u32[]{:S(2)}, u32[]{:S(2)}) collective-permute-start(f32[17,8,128]{2,1,0:T(8,128)S(1)} %get-tuple-element.100), channel_id=1, source_target_pairs={{0,12},{4,8},{8,4},{12,0},{16,28},{20,24},{24,20},{28,16},{1,13},{... | collective-permute-start | bytes 208904 | tf_op jit(solution)/shard_map/ppermute | solution.py:41
  118.2 6.8 %collective-permute-start.56 = (f32[17,8,128]{2,1,0:T(8,128)S(1)}, f32[17,8,128]{2,1,0:T(8,128)S(1)}, u32[]{:S(2)}, u32[]{:S(2)}) collective-permute-start(f32[17,8,128]{2,1,0:T(8,128)S(1)} %get-tuple-element.131.refs_0_), channel_id=1, source_target_pairs={{0,4},{4,0},{8,12},{12,8},{16,20},{20,16},{24,28},{28,24},{1,5},{5... | collective-permute-start | bytes 208904 | tf_op jit(solution)/shard_map/ppermute | solution.py:41
  119.6 6.3 %collective-permute-start.57 = (f32[17,8,128]{2,1,0:T(8,128)S(1)}, f32[17,8,128]{2,1,0:T(8,128)S(1)}, u32[]{:S(2)}, u32[]{:S(2)}) collective-permute-start(f32[17,8,128]{2,1,0:T(8,128)S(1)} %get-tuple-element.131.refs_0_), channel_id=1, source_target_pairs={{0,8},{4,12},{8,0},{12,4},{16,24},{20,28},{24,16},{28,20},{1,9},{5... | collective-permute-start | bytes 208904 | tf_op jit(solution)/shard_map/ppermute | solution.py:41
  122.4 6.4 %collective-permute-start.61 = (f32[17,8,128]{2,1,0:T(8,128)S(1)}, f32[17,8,128]{2,1,0:T(8,128)S(1)}, u32[]{:S(2)}, u32[]{:S(2)}) collective-permute-start(f32[17,8,128]{2,1,0:T(8,128)S(1)} %get-tuple-element.136.refs_0_), channel_id=1, source_target_pairs={{0,4},{4,0},{8,12},{12,8},{16,20},{20,16},{24,28},{28,24},{1,5},{5... | collective-permute-start | bytes 208904 | tf_op jit(solution)/shard_map/ppermute | solution.py:41
  (43 other events, 249.2 us)

commit v5 on v4

--- a/solution.py
+++ b/solution.py
@@ -10,8 +10,9 @@
 
 ITERS = 3
 LEAD_MAX = 4
-GROUP = 32
+GROUP = 128
 PIECE = 8
+AHEAD = 16
 STREAMS = 2
 KERNEL_VMEM = 1 << 20
 
@@ -81,13 +82,17 @@
     return ref[rows, k * tile : (k + 1) * tile] if len(ref.shape) == 2 else ref[k]
 
 
-def prepared(matrix_tiles, primal_rows, cost_row):
+def prepared(matrix_tiles, message_rows):
     count, tile, _ = matrix_tiles.shape
-    scen, rows = primal_rows.shape
+    heights = [array.shape[0] for array in message_rows]
     piece = min(PIECE, count)
     pieces = count // piece
-
-    def body(tiles_ref, primal_ref, cost_ref, plain_ref, turned_ref, start_ref, held, arrived, small):
+    ahead = min(AHEAD, pieces)
+
+    def body(tiles_ref, *refs):
+        row_refs = refs[: len(heights)]
+        plain_ref, turned_ref, start_ref, held, arrived, small = refs[len(heights) :]
+
         def copy_of(which):
             return pltpu.make_async_copy(
                 tiles_ref.at[pl.ds(which * piece, piece)],
@@ -95,14 +100,22 @@
                 arrived.at[which],
             )
 
-        copy_primal = pltpu.make_async_copy(primal_ref, start_ref.at[pl.ds(0, scen)], small.at[0])
-        copy_cost = pltpu.make_async_copy(cost_ref, start_ref.at[pl.ds(scen, 1)], small.at[1])
-        for which in range(pieces):
+        row_copies = [
+            pltpu.make_async_copy(
+                ref, start_ref.at[pl.ds(sum(heights[:which]), heights[which])], small.at[which]
+            )
+            for which, ref in enumerate(row_refs)
+        ]
+        for which in range(ahead):
             copy_of(which).start()
-        copy_primal.start()
-        copy_cost.start()
+        for copy in row_copies:
+            copy.start()
 
         def one_piece(which, carry):
+            @pl.when(which + ahead < pieces)
+            def _():
+                copy_of(which + ahead).start()
+
             copy_of(which).wait()
             for k in range(piece):
                 t = which * piece + k
@@ -114,28 +127,28 @@
             return carry
 
         lax.fori_loop(0, pieces, one_piece, 0)
-        copy_primal.wait()
-        copy_cost.wait()
+        for copy in row_copies:
+            copy.wait()
 
     anywhere = pl.BlockSpec(memory_space=pl.ANY)
     spec = pl.BlockSpec(memory_space=pltpu.VMEM)
     in_hbm = [
         pltpu.with_memory_space_constraint(array, pltpu.HBM)
-        for array in (matrix_tiles, primal_rows, cost_row)
+        for array in (matrix_tiles, *message_rows)
     ]
     return pl.pallas_call(
         body,
         out_shape=[
             pltpu.VMEM((count, 2 * tile, tile), BF16),
             pltpu.VMEM((count, 2 * tile, tile), BF16),
-            pltpu.VMEM((scen + 1, rows), F32),
+            pltpu.VMEM((sum(heights), message_rows[0].shape[1]), F32),
         ],
-        in_specs=[anywhere] * 3,
+        in_specs=[anywhere] * len(in_hbm),
         out_specs=[spec] * 3,
         scratch_shapes=[
             pltpu.VMEM((count, tile, tile), F32),
             pltpu.SemaphoreType.DMA((pieces,)),
-            pltpu.SemaphoreType.DMA((2,)),
+            pltpu.SemaphoreType.DMA((len(heights),)),
         ],
         compiler_params=pltpu.CompilerParams(
             vmem_limit_bytes=KERNEL_VMEM + count * tile * tile * 4
@@ -241,7 +254,10 @@
                 wanted = lead_ref[k : k + 1, :]
                 lagged = jnp.zeros((share, tile), F32)
                 for steps in range(1, LEAD_MAX + 1):
-                    lagged = jnp.where(wanted == steps, earlier_refs[steps - 1][own, lanes], lagged)
+                    earlier_ref = earlier_refs[steps - 1]
+                    first = scen if earlier_ref.shape[0] > scen else 0
+                    here = slice(first + own.start, first + own.stop)
+                    lagged = jnp.where(wanted == steps, earlier_ref[here, lanes], lagged)
                 out_ref[k] = demand_ref[own, lanes] - return_share * lagged
             for k in range(sub, 2 * sub + 1):
                 out_ref[k] = jnp.zeros((share, tile), F32)
@@ -262,7 +278,7 @@
 
 def primal_update(own, other, starts, primal, weight, primal_square, rows, sub, last):
     _, scen, tile = own.shape
-    all_scen = starts[0].shape[0] - 1
+    cost_row = starts[0].shape[0] - 1
     first = primal is None
 
     def body(*refs):
@@ -291,7 +307,7 @@
                 lanes = slice(k * tile, (k + 1) * tile)
                 pull = own_ref[here] + other_ref[(1 - chunk) * sub + k]
                 before = start_refs[chunk][rows, lanes] if first else primal_ref[here]
-                cost = start_refs[chunk][all_scen : all_scen + 1, lanes]
+                cost = start_refs[chunk][cost_row : cost_row + 1, lanes]
                 after = jnp.maximum(before - primal_step * (cost - pull), 0.0)
                 change = after - before
                 square = square + change * change
@@ -352,8 +368,10 @@
     return call_in_vmem(body, [own, other, weight, *duals], outputs)
 
 
-def summed(own, axis, others):
-    got = [exchanged(value, axis, mask) for mask, value in enumerate(others, 1)]
+def summed(own, axis, others, masks=(1, 2, 3)):
+    got = []
+    for mask, value in zip(masks, others):
+        got.append(exchanged(value, axis, mask))
     return (own + got[0]) + (got[1] + got[2])
 
 
@@ -382,14 +400,17 @@
 
     demand_rows, dual_rows, primal_rows = demand.T, dual_init.T, primal_init.T
     dual_pair = [dual_rows, exchanged(dual_rows, "col", 2)]
+    together = lax.axis_size("band") == 2 * LEAD_MAX and 1 << order[-1] == LEAD_MAX
     earlier = []
-    for steps in range(1, LEAD_MAX + 1):
+    for steps in range(1, LEAD_MAX + 1 - together):
         earlier.append(passed_along(demand_rows, "band", steps))
     plain_tiles, turned_tiles, start_rows = prepared(
-        matrix_tiles, primal_rows, cost_vector[None, :]
+        matrix_tiles, [primal_rows] + [demand_rows] * together + [cost_vector[None, :]]
     )
     dual_pair += [exchanged(value, "col", 1) for value in dual_pair]
     start_rows = [start_rows, exchanged(start_rows, "band", 1 << order[-1])]
+    if together:
+        earlier.append(start_rows[1])
     share = scen // STREAMS
     right_sides = right_sides_of(demand_rows, earlier, lead_periods.reshape(sub, tile), tile, share)
     states = []
@@ -429,7 +450,9 @@
         for bit in order[-2::-1]:
             got = exchanged(ahead, "band", 1 << bit)
             ahead = jnp.concatenate([ahead[:-1], got[:-1], ahead[-1:] + got[-1:]])
-        ahead = [ahead] + [exchanged(ahead, "band", mask) for mask in range(1, 4)]
+        ahead = [ahead]
+        for mask in range(1, 4):
+            ahead.append(exchanged(ahead[0], "band", mask))
         keep, send = forward_product(index, ahead, turned_tiles, rows, units_row, units_col)
         total = (keep + exchanged(send, "col", 1)) - state["right_side"]
         other = exchanged(total, "col", 2)
@@ -449,9 +472,9 @@
         return jnp.concatenate([state[name] for state in states])
 
     square = joined("square")
-    square = square + exchanged(square, "col", 1)
-    square = summed(square, "band", [square] * 3)
-    for bit in order:
+    cols = lax.axis_size("col")
+    square = summed(square, ("band", "col"), [square] * 3, (1, cols, cols + 1))
+    for bit in range(1, band_bits):
         square = square + exchanged(square, "band", 1 << bit)
     weight = next_weight(joined("weight"), joined("primal_square"), square)[:, 0]
     return (joined("primal_rows").T, joined("dual_rows").T, weight)

time: 152 us -> 146 us (0.961)
  Pallas kernels: 33 us -> 28.5 us
    pallas_call x25, Pallas kernels: 28.6 us -> 24.2 us  [call_in_vmem(): pl.pallas_call(body, out_shape=[pltpu.VMEM(shape, F32) for shape in outpu...]
    ppermute x4 -> x3, starting transfers between devices: 5.67 us -> 5.06 us  [passed_along(): lax.ppermute(value, axis, [(source, (source + steps) % count) for source...]
    ppermute x4 -> x3, waiting for transfers between devices: 4.47 us -> 4.52 us  [passed_along(): lax.ppermute(value, axis, [(source, (source + steps) % count) for source...]
  transfers between devices with their start and end apart: 71 -> 70, of which waited for: 30 -> 32; matrix products, arithmetic and copies ran while one was open for 2% -> 2% of each run, Pallas kernels for 20% -> 18%
where the time goes in v5:
time: 146 us
  starting transfers between devices  72.7 us (50%)
  waiting for transfers between devices  40.5 us (28%)
  Pallas kernels  28.5 us (20%)
  other arithmetic  3.12 us (2%)
    ppermute x67, starting transfers between devices, exchanged(): lax.ppermute(value, axis, [(source, source ^ mask) for source in range(co...  67.7 us
    ppermute x67, waiting for transfers between devices, exchanged(): lax.ppermute(value, axis, [(source, source ^ mask) for source in range(co...  36 us
    pallas_call x25, Pallas kernels, call_in_vmem(): pl.pallas_call(body, out_shape=[pltpu.VMEM(shape, F32) for shape in outpu...  24.2 us
    ppermute x3, starting transfers between devices, passed_along(): lax.ppermute(value, axis, [(source, (source + steps) % count) for source...  5.06 us
    ppermute x3, waiting for transfers between devices, passed_along(): lax.ppermute(value, axis, [(source, (source + steps) % count) for source...  4.52 us
    pallas_call x1, Pallas kernels, prepared(): pl.pallas_call(body, out_shape=[pltpu.VMEM((count, 2 * tile, tile), BF16)...  4.36 us
  transfers between devices with their start and end apart: 70, of which 32 were waited for; matrix products, arithmetic and copies ran while one was open for 2% of the time, Pallas kernels for 18%

profile of v5, /device:TPU:0, one launch (start us, length us, event | category | flops | bytes accessed | tf_op | source)
XLA Modules:
  0.0 146.2 jit_solution(11947475474163705419)
XLA Ops:
  0.6 3.0 %collective-permute-start = (f32[16,1024]{1,0:T(8,128)}, f32[16,1024]{1,0:T(8,128)S(1)}, u32[]{:S(2)}, u32[]{:S(2)}) collective-permute-start(f32[16,1024]{1,0:T(8,128)} %bitcast.27), channel_id=1, source_target_pairs={{0,2},{1,3},{2,0},{3,1},{4,6},{5,7},{6,4},{7,5},{8,10},{9,11},{10,... | collective-permute-start | bytes 196616 | tf_op jit(solution)/shard_map/ppermute | solution.py:42
  4.4 4.4 %shard_map.103 = (bf16[128,256,128]{2,1,0:T(8,128)(2,1)S(1)}, bf16[128,256,128]{2,1,0:T(8,128)(2,1)S(1)}, f32[33,1024]{1,0:T(8,128)S(1)}) custom-call(f32[128,128,128]{2,1,0:T(8,128)} %bitcast.39, f32[16,1024]{1,0:T(8,128)} %bitcast.40, f32[16,1024]{1,0:T(8,128)} %bitcast.33, f32[1,1024]{1,0:T(1,128)} %bitcast.41), custom_call_target="tpu_custom_call" | custom-call | tf_op jit(solution)/shard_map/pallas_call | solution.py:139
  15.6 2.6 %collective-permute-start.7 = (f32[33,1024]{1,0:T(8,128)S(1)}, f32[33,1024]{1,0:T(8,128)S(1)}, u32[]{:S(2)}, u32[]{:S(2)}) collective-permute-start(f32[33,1024]{1,0:T(8,128)S(1)} %get-tuple-element.80.refs_2_), channel_id=1, source_target_pairs={{0,16},{4,20},{8,24},{12,28},{16,0},{20,4},{24,8},{28,12},{1,17},{... | collective-permute-start | bytes 405512 | tf_op jit(solution)/shard_map/ppermute | solution.py:42
  24.4 2.8 %collective-permute-done.32 = f32[17,8,128]{2,1,0:T(8,128)S(1)} collective-permute-done((f32[17,8,128]{2,1,0:T(8,128)S(1)}, f32[17,8,128]{2,1,0:T(8,128)S(1)}, u32[]{:S(2)}, u32[]{:S(2)}) %collective-permute-start.32) | collective-permute-done | bytes 69664 | tf_op jit(solution)/shard_map/ppermute | solution.py:42
  30.1 2.8 %collective-permute-start.10 = (f32[17,8,128]{2,1,0:T(8,128)S(1)}, f32[17,8,128]{2,1,0:T(8,128)S(1)}, u32[]{:S(2)}, u32[]{:S(2)}) collective-permute-start(f32[17,8,128]{2,1,0:T(8,128)S(1)} %get-tuple-element.81.refs_0_), channel_id=1, source_target_pairs={{0,12},{4,8},{8,4},{12,0},{16,28},{20,24},{24,20},{28,16},{1,13},{... | collective-permute-start | bytes 208904 | tf_op jit(solution)/shard_map/ppermute | solution.py:42
  34.9 2.0 %collective-permute-start.13 = (f32[16,1024]{1,0:T(8,128)S(1)}, f32[16,1024]{1,0:T(8,128)S(1)}, u32[]{:S(2)}, u32[]{:S(2)}) collective-permute-start(f32[16,1024]{1,0:T(8,128)S(1)} %bitcast.35), channel_id=1, source_target_pairs={{0,8},{4,12},{8,16},{12,20},{16,24},{20,28},{24,0},{28,4},{1,9},{5... | collective-permute-start | bytes 196616 | tf_op jit(solution)/shard_map/ppermute | solution.py:47
  40.6 1.9 %shard_map.106 = (f32[17,8,128]{2,1,0:T(8,128)S(1)}, f32[17,8,128]{2,1,0:T(8,128)S(1)}) custom-call(s32[256]{0:T(256)S(1)} %pad_add_fusion.index_ref, bf16[128,256,128]{2,1,0:T(8,128)(2,1)S(1)} %get-tuple-element.75.tiles_ref, f32[17,8,128]{2,1,0:T(8,128)S(1)} %get-tuple-element.81.refs_0_, f32[17,8,128]{2,1,0:T(8,128)S(1)} %collective-permute-done.8.refs_1_, ...), custom_call_target="tpu_custom_call" | custom-call | tf_op jit(solution)/shard_map/pallas_call | solution.py:71
  44.4 4.5 %collective-permute-done.14.refs_2_ = f32[16,1024]{1,0:T(8,128)S(1)} collective-permute-done((f32[16,1024]{1,0:T(8,128)S(1)}, f32[16,1024]{1,0:T(8,128)S(1)}, u32[]{:S(2)}, u32[]{:S(2)}) %collective-permute-start.14) | collective-permute-done | bytes 65568 | tf_op jit(solution)/shard_map/ppermute | solution.py:47
  49.0 1.9 %shard_map.117 = (f32[17,8,128]{2,1,0:T(8,128)S(1)}, f32[17,8,128]{2,1,0:T(8,128)S(1)}) custom-call(s32[256]{0:T(256)S(1)} %pad_add_fusion.index_ref, bf16[128,256,128]{2,1,0:T(8,128)(2,1)S(1)} %get-tuple-element.75.tiles_ref, f32[17,8,128]{2,1,0:T(8,128)S(1)} %get-tuple-element.108.refs_0_, f32[17,8,128]{2,1,0:T(8,128)S(1)} %collective-permute-done.35.refs_1_, ...), custom_call_target="tpu_custom_call" | custom-call | tf_op jit(solution)/shard_map/pallas_call | solution.py:71
  53.1 2.9 %collective-permute-done.15.refs_1_ = f32[17,8,128]{2,1,0:T(8,128)S(1)} collective-permute-done((f32[17,8,128]{2,1,0:T(8,128)S(1)}, f32[17,8,128]{2,1,0:T(8,128)S(1)}, u32[]{:S(2)}, u32[]{:S(2)}) %collective-permute-start.15) | collective-permute-done | bytes 69664 | tf_op jit(solution)/shard_map/ppermute | solution.py:42
  57.4 1.8 %shard_map.109 = (f32[17,8,128]{2,1,0:T(8,128)S(1)}, f32[17,8,128]{2,1,0:T(8,128)S(1)}, f32[17,8,128]{2,1,0:T(8,128)S(1)}, f32[17,8,128]{2,1,0:T(8,128)S(1)}) custom-call(s32[256]{0:T(256)S(1)} %pad_add_fusion.index_ref, bf16[128,256,128]{2,1,0:T(8,128)(2,1)S(1)} %get-tuple-element.74.tiles_ref, f32[17,8,128]{2,1,0:T(8,128)S(1)} %get-tuple-element.85.refs_0_.refs_3_, ...), custom_call_target="tpu_custom_call" | custom-call | tf_op jit(solution)/shard_map/pallas_call | solution.py:71
  59.3 2.4 %collective-permute-start.17 = (f32[17,8,128]{2,1,0:T(8,128)S(1)}, f32[17,8,128]{2,1,0:T(8,128)S(1)}, u32[]{:S(2)}, u32[]{:S(2)}) collective-permute-start(f32[17,8,128]{2,1,0:T(8,128)S(1)} %get-tuple-element.87), channel_id=1, source_target_pairs={{0,4},{4,0},{8,12},{12,8},{16,20},{20,16},{24,28},{28,24},{1,5},{5... | collective-permute-start | bytes 208904 | tf_op jit(solution)/shard_map/ppermute | solution.py:42
  63.2 1.8 %shard_map.119 = (f32[17,8,128]{2,1,0:T(8,128)S(1)}, f32[17,8,128]{2,1,0:T(8,128)S(1)}, f32[17,8,128]{2,1,0:T(8,128)S(1)}, f32[17,8,128]{2,1,0:T(8,128)S(1)}) custom-call(s32[256]{0:T(256)S(1)} %pad_add_fusion.index_ref, bf16[128,256,128]{2,1,0:T(8,128)(2,1)S(1)} %get-tuple-element.74.tiles_ref, f32[17,8,128]{2,1,0:T(8,128)S(1)} %get-tuple-element.112.refs_0_.refs_3_, ...), custom_call_target="tpu_custom_call" | custom-call | tf_op jit(solution)/shard_map/pallas_call | solution.py:71
  65.1 2.0 %collective-permute-start.41 = (f32[17,8,128]{2,1,0:T(8,128)S(1)}, f32[17,8,128]{2,1,0:T(8,128)S(1)}, u32[]{:S(2)}, u32[]{:S(2)}) collective-permute-start(f32[17,8,128]{2,1,0:T(8,128)S(1)} %get-tuple-element.114), channel_id=1, source_target_pairs={{0,4},{4,0},{8,12},{12,8},{16,20},{20,16},{24,28},{28,24},{1,5},{5... | collective-permute-start | bytes 208904 | tf_op jit(solution)/shard_map/ppermute | solution.py:42
  70.3 2.0 %collective-permute-done.42 = f32[17,8,128]{2,1,0:T(8,128)S(1)} collective-permute-done((f32[17,8,128]{2,1,0:T(8,128)S(1)}, f32[17,8,128]{2,1,0:T(8,128)S(1)}, u32[]{:S(2)}, u32[]{:S(2)}) %collective-permute-start.42) | collective-permute-done | bytes 69664 | tf_op jit(solution)/shard_map/ppermute | solution.py:42
  72.7 1.8 %collective-permute-start.44 = (f32[17,8,128]{2,1,0:T(8,128)S(1)}, f32[17,8,128]{2,1,0:T(8,128)S(1)}, u32[]{:S(2)}, u32[]{:S(2)}) collective-permute-start(f32[17,8,128]{2,1,0:T(8,128)S(1)} %add_add_fusion.1.refs_0_), channel_id=1, source_target_pairs={{0,16},{4,20},{8,24},{12,28},{16,0},{20,4},{24,8},{28,12},{1,17},{... | collective-permute-start | bytes 208904 | tf_op jit(solution)/shard_map/ppermute | solution.py:42
  74.7 2.9 %collective-permute-start.21 = (f32[17,8,128]{2,1,0:T(8,128)S(1)}, f32[17,8,128]{2,1,0:T(8,128)S(1)}, u32[]{:S(2)}, u32[]{:S(2)}) collective-permute-start(f32[17,8,128]{2,1,0:T(8,128)S(1)} %get-tuple-element.92.refs_0_), channel_id=1, source_target_pairs={{0,4},{4,0},{8,12},{12,8},{16,20},{20,16},{24,28},{28,24},{1,5},{5... | collective-permute-start | bytes 208904 | tf_op jit(solution)/shard_map/ppermute | solution.py:42
  79.3 2.0 %collective-permute-start.45 = (f32[17,8,128]{2,1,0:T(8,128)S(1)}, f32[17,8,128]{2,1,0:T(8,128)S(1)}, u32[]{:S(2)}, u32[]{:S(2)}) collective-permute-start(f32[17,8,128]{2,1,0:T(8,128)S(1)} %get-tuple-element.119.refs_0_), channel_id=1, source_target_pairs={{0,4},{4,0},{8,12},{12,8},{16,20},{20,16},{24,28},{28,24},{1,5},{5... | collective-permute-start | bytes 208904 | tf_op jit(solution)/shard_map/ppermute | solution.py:42
  83.5 1.9 %shard_map.111 = (f32[17,8,128]{2,1,0:T(8,128)S(1)}, f32[17,8,128]{2,1,0:T(8,128)S(1)}) custom-call(s32[256]{0:T(256)S(1)} %pad_add_fusion.index_ref, bf16[128,256,128]{2,1,0:T(8,128)(2,1)S(1)} %get-tuple-element.75.tiles_ref, f32[17,8,128]{2,1,0:T(8,128)S(1)} %get-tuple-element.92.refs_0_, f32[17,8,128]{2,1,0:T(8,128)S(1)} %collective-permute-done.21.refs_1_, ...), custom_call_target="tpu_custom_call" | custom-call | tf_op jit(solution)/shard_map/pallas_call | solution.py:71
  86.5 1.9 %shard_map.121 = (f32[17,8,128]{2,1,0:T(8,128)S(1)}, f32[17,8,128]{2,1,0:T(8,128)S(1)}) custom-call(s32[256]{0:T(256)S(1)} %pad_add_fusion.index_ref, bf16[128,256,128]{2,1,0:T(8,128)(2,1)S(1)} %get-tuple-element.75.tiles_ref, f32[17,8,128]{2,1,0:T(8,128)S(1)} %get-tuple-element.119.refs_0_, f32[17,8,128]{2,1,0:T(8,128)S(1)} %collective-permute-done.45.refs_1_, ...), custom_call_target="tpu_custom_call" | custom-call | tf_op jit(solution)/shard_map/pallas_call | solution.py:71
  90.7 2.9 %collective-permute-done.25.refs_1_ = f32[17,8,128]{2,1,0:T(8,128)S(1)} collective-permute-done((f32[17,8,128]{2,1,0:T(8,128)S(1)}, f32[17,8,128]{2,1,0:T(8,128)S(1)}, u32[]{:S(2)}, u32[]{:S(2)}) %collective-permute-start.25) | collective-permute-done | bytes 69664 | tf_op jit(solution)/shard_map/ppermute | solution.py:42
  95.0 1.8 %shard_map.113 = (f32[17,8,128]{2,1,0:T(8,128)S(1)}, f32[17,8,128]{2,1,0:T(8,128)S(1)}, f32[17,8,128]{2,1,0:T(8,128)S(1)}, f32[17,8,128]{2,1,0:T(8,128)S(1)}) custom-call(s32[256]{0:T(256)S(1)} %pad_add_fusion.index_ref, bf16[128,256,128]{2,1,0:T(8,128)(2,1)S(1)} %get-tuple-element.74.tiles_ref, f32[17,8,128]{2,1,0:T(8,128)S(1)} %get-tuple-element.96.refs_0_.refs_3_, ...), custom_call_target="tpu_custom_call" | custom-call | tf_op jit(solution)/shard_map/pallas_call | solution.py:71
  100.4 1.8 %shard_map.123 = (f32[17,8,128]{2,1,0:T(8,128)S(1)}, f32[17,8,128]{2,1,0:T(8,128)S(1)}, f32[17,8,128]{2,1,0:T(8,128)S(1)}, f32[17,8,128]{2,1,0:T(8,128)S(1)}) custom-call(s32[256]{0:T(256)S(1)} %pad_add_fusion.index_ref, bf16[128,256,128]{2,1,0:T(8,128)(2,1)S(1)} %get-tuple-element.74.tiles_ref, f32[17,8,128]{2,1,0:T(8,128)S(1)} %get-tuple-element.123.refs_0_.refs_3_, ...), custom_call_target="tpu_custom_call" | custom-call | tf_op jit(solution)/shard_map/pallas_call | solution.py:71
  105.8 2.0 %collective-permute-start.30 = (f32[17,8,128]{2,1,0:T(8,128)S(1)}, f32[17,8,128]{2,1,0:T(8,128)S(1)}, u32[]{:S(2)}, u32[]{:S(2)}) collective-permute-start(f32[17,8,128]{2,1,0:T(8,128)S(1)} %add_add_fusion.3.refs_0_), channel_id=1, source_target_pairs={{0,16},{4,20},{8,24},{12,28},{16,0},{20,4},{24,8},{28,12},{1,17},{... | collective-permute-start | bytes 208904 | tf_op jit(solution)/shard_map/ppermute | solution.py:42
  112.6 2.0 %collective-permute-start.55 = (f32[17,8,128]{2,1,0:T(8,128)S(1)}, f32[17,8,128]{2,1,0:T(8,128)S(1)}, u32[]{:S(2)}, u32[]{:S(2)}) collective-permute-start(f32[17,8,128]{2,1,0:T(8,128)S(1)} %get-tuple-element.131.refs_0_), channel_id=1, source_target_pairs={{0,4},{4,0},{8,12},{12,8},{16,20},{20,16},{24,28},{28,24},{1,5},{5... | collective-permute-start | bytes 208904 | tf_op jit(solution)/shard_map/ppermute | solution.py:42
  117.0 1.9 %collective-permute-start.60 = (f32[17,8,128]{2,1,0:T(8,128)S(1)}, f32[17,8,128]{2,1,0:T(8,128)S(1)}, u32[]{:S(2)}, u32[]{:S(2)}) collective-permute-start(f32[17,8,128]{2,1,0:T(8,128)S(1)} %get-tuple-element.136.refs_0_), channel_id=1, source_target_pairs={{0,4},{4,0},{8,12},{12,8},{16,20},{20,16},{24,28},{28,24},{1,5},{5... | collective-permute-start | bytes 208904 | tf_op jit(solution)/shard_map/ppermute | solution.py:42
  120.7 1.9 %shard_map.125 = (f32[17,8,128]{2,1,0:T(8,128)S(1)}, f32[17,8,128]{2,1,0:T(8,128)S(1)}) custom-call(s32[256]{0:T(256)S(1)} %pad_add_fusion.index_ref, bf16[128,256,128]{2,1,0:T(8,128)(2,1)S(1)} %get-tuple-element.75.tiles_ref, f32[17,8,128]{2,1,0:T(8,128)S(1)} %get-tuple-element.131.refs_0_, f32[17,8,128]{2,1,0:T(8,128)S(1)} %collective-permute-done.55.refs_1_, ...), custom_call_target="tpu_custom_call" | custom-call | tf_op jit(solution)/shard_map/pallas_call | solution.py:71
  124.4 1.9 %shard_map.127 = (f32[17,8,128]{2,1,0:T(8,128)S(1)}, f32[17,8,128]{2,1,0:T(8,128)S(1)}) custom-call(s32[256]{0:T(256)S(1)} %pad_add_fusion.index_ref, bf16[128,256,128]{2,1,0:T(8,128)(2,1)S(1)} %get-tuple-element.75.tiles_ref, f32[17,8,128]{2,1,0:T(8,128)S(1)} %get-tuple-element.136.refs_0_, f32[17,8,128]{2,1,0:T(8,128)S(1)} %collective-permute-done.60.refs_1_, ...), custom_call_target="tpu_custom_call" | custom-call | tf_op jit(solution)/shard_map/pallas_call | solution.py:71
  128.5 2.9 %collective-permute-done.59.refs_1_ = f32[17,8,128]{2,1,0:T(8,128)S(1)} collective-permute-done((f32[17,8,128]{2,1,0:T(8,128)S(1)}, f32[17,8,128]{2,1,0:T(8,128)S(1)}, u32[]{:S(2)}, u32[]{:S(2)}) %collective-permute-start.59) | collective-permute-done | bytes 69664 | tf_op jit(solution)/shard_map/ppermute | solution.py:42
  134.4 1.9 %collective-permute-done.66 = f32[16,128]{1,0:T(8,128)S(1)} collective-permute-done((f32[16,128]{1,0:T(8,128)S(1)}, f32[16,128]{1,0:T(8,128)S(1)}, u32[]{:S(2)}, u32[]{:S(2)}) %collective-permute-start.66) | collective-permute-done | bytes 8224 | tf_op jit(solution)/shard_map/ppermute | solution.py:42
  138.7 2.1 %collective-permute-done.68 = f32[16,128]{1,0:T(8,128)S(1)} collective-permute-done((f32[16,128]{1,0:T(8,128)S(1)}, f32[16,128]{1,0:T(8,128)S(1)}, u32[]{:S(2)}, u32[]{:S(2)}) %collective-permute-start.68) | collective-permute-done | bytes 8224 | tf_op jit(solution)/shard_map/ppermute | solution.py:42
  140.8 2.2 %collective-permute-start.69 = (f32[16,128]{1,0:T(8,128)S(1)}, f32[16,128]{1,0:T(8,128)S(1)}, u32[]{:S(2)}, u32[]{:S(2)}) collective-permute-start(f32[16,128]{1,0:T(8,128)S(1)} %add.167), channel_id=1, source_target_pairs={{0,16},{4,20},{8,24},{12,28},{16,0},{20,4},{24,8},{28,12},{1,17},{... | collective-permute-start | bytes 24584 | tf_op jit(solution)/shard_map/ppermute | solution.py:42
  (169 shorter events, 70.5 us)
Async XLA Ops:
  0.6 8.1 %collective-permute-start = (f32[16,1024]{1,0:T(8,128)}, f32[16,1024]{1,0:T(8,128)S(1)}, u32[]{:S(2)}, u32[]{:S(2)}) collective-permute-start(f32[16,1024]{1,0:T(8,128)} %bitcast.27), channel_id=1, source_target_pairs={{0,2},{1,3},{2,0},{3,1},{4,6},{5,7},{6,4},{7,5},{8,10},{9,11},{10,... | collective-permute-start | bytes 196616 | tf_op jit(solution)/shard_map/ppermute | solution.py:42
  12.0 9.6 %collective-permute-start.3 = (f32[17,8,128]{2,1,0:T(8,128)S(1)}, f32[17,8,128]{2,1,0:T(8,128)S(1)}, u32[]{:S(2)}, u32[]{:S(2)}) collective-permute-start(f32[17,8,128]{2,1,0:T(8,128)S(1)} %get-tuple-element.77), channel_id=1, source_target_pairs={{0,4},{4,0},{8,12},{12,8},{16,20},{20,16},{24,28},{28,24},{1,5},{5... | collective-permute-start | bytes 208904 | tf_op jit(solution)/shard_map/ppermute | solution.py:42
  13.6 9.6 %collective-permute-start.4 = (f32[17,8,128]{2,1,0:T(8,128)S(1)}, f32[17,8,128]{2,1,0:T(8,128)S(1)}, u32[]{:S(2)}, u32[]{:S(2)}) collective-permute-start(f32[17,8,128]{2,1,0:T(8,128)S(1)} %get-tuple-element.78), channel_id=1, source_target_pairs={{0,8},{4,12},{8,0},{12,4},{16,24},{20,28},{24,16},{28,20},{1,9},{5... | collective-permute-start | bytes 208904 | tf_op jit(solution)/shard_map/ppermute | solution.py:42
  15.2 8.4 %collective-permute-start.5 = (f32[17,8,128]{2,1,0:T(8,128)S(1)}, f32[17,8,128]{2,1,0:T(8,128)S(1)}, u32[]{:S(2)}, u32[]{:S(2)}) collective-permute-start(f32[17,8,128]{2,1,0:T(8,128)S(1)} %get-tuple-element.79), channel_id=1, source_target_pairs={{0,12},{4,8},{8,4},{12,0},{16,28},{20,24},{24,20},{28,16},{1,13},{... | collective-permute-start | bytes 208904 | tf_op jit(solution)/shard_map/ppermute | solution.py:42
  15.6 14.4 %collective-permute-start.7 = (f32[33,1024]{1,0:T(8,128)S(1)}, f32[33,1024]{1,0:T(8,128)S(1)}, u32[]{:S(2)}, u32[]{:S(2)}) collective-permute-start(f32[33,1024]{1,0:T(8,128)S(1)} %get-tuple-element.80.refs_2_), channel_id=1, source_target_pairs={{0,16},{4,20},{8,24},{12,28},{16,0},{20,4},{24,8},{28,12},{1,17},{... | collective-permute-start | bytes 405512 | tf_op jit(solution)/shard_map/ppermute | solution.py:42
  23.6 6.4 %collective-permute-start.6 = (f32[17,8,128]{2,1,0:T(8,128)S(1)}, f32[17,8,128]{2,1,0:T(8,128)S(1)}, u32[]{:S(2)}, u32[]{:S(2)}) collective-permute-start(f32[17,8,128]{2,1,0:T(8,128)S(1)} %add_add_fusion.5.refs_0_), channel_id=1, source_target_pairs={{0,16},{4,20},{8,24},{12,28},{16,0},{20,4},{24,8},{28,12},{1,17},{... | collective-permute-start | bytes 208904 | tf_op jit(solution)/shard_map/ppermute | solution.py:42
  28.8 6.1 %collective-permute-start.34 = (f32[17,8,128]{2,1,0:T(8,128)S(1)}, f32[17,8,128]{2,1,0:T(8,128)S(1)}, u32[]{:S(2)}, u32[]{:S(2)}) collective-permute-start(f32[17,8,128]{2,1,0:T(8,128)S(1)} %add_add_fusion.2.refs_0_), channel_id=1, source_target_pairs={{0,16},{4,20},{8,24},{12,28},{16,0},{20,4},{24,8},{28,12},{1,17},{... | collective-permute-start | bytes 208904 | tf_op jit(solution)/shard_map/ppermute | solution.py:42
  30.1 7.0 %collective-permute-start.10 = (f32[17,8,128]{2,1,0:T(8,128)S(1)}, f32[17,8,128]{2,1,0:T(8,128)S(1)}, u32[]{:S(2)}, u32[]{:S(2)}) collective-permute-start(f32[17,8,128]{2,1,0:T(8,128)S(1)} %get-tuple-element.81.refs_0_), channel_id=1, source_target_pairs={{0,12},{4,8},{8,4},{12,0},{16,28},{20,24},{24,20},{28,16},{1,13},{... | collective-permute-start | bytes 208904 | tf_op jit(solution)/shard_map/ppermute | solution.py:42
  33.7 8.8 %collective-permute-start.12 = (f32[16,1024]{1,0:T(8,128)S(1)}, f32[16,1024]{1,0:T(8,128)S(1)}, u32[]{:S(2)}, u32[]{:S(2)}) collective-permute-start(f32[16,1024]{1,0:T(8,128)S(1)} %bitcast.34), channel_id=1, source_target_pairs={{0,4},{4,8},{8,12},{12,16},{16,20},{20,24},{24,28},{28,0},{1,5},{5... | collective-permute-start | bytes 196616 | tf_op jit(solution)/shard_map/ppermute | solution.py:47
  34.9 7.7 %collective-permute-start.13 = (f32[16,1024]{1,0:T(8,128)S(1)}, f32[16,1024]{1,0:T(8,128)S(1)}, u32[]{:S(2)}, u32[]{:S(2)}) collective-permute-start(f32[16,1024]{1,0:T(8,128)S(1)} %bitcast.35), channel_id=1, source_target_pairs={{0,8},{4,12},{8,16},{12,20},{16,24},{20,28},{24,0},{28,4},{1,9},{5... | collective-permute-start | bytes 196616 | tf_op jit(solution)/shard_map/ppermute | solution.py:47
  37.1 11.9 %collective-permute-start.35 = (f32[17,8,128]{2,1,0:T(8,128)S(1)}, f32[17,8,128]{2,1,0:T(8,128)S(1)}, u32[]{:S(2)}, u32[]{:S(2)}) collective-permute-start(f32[17,8,128]{2,1,0:T(8,128)S(1)} %get-tuple-element.108.refs_0_), channel_id=1, source_target_pairs={{0,4},{4,0},{8,12},{12,8},{16,20},{20,16},{24,28},{28,24},{1,5},{5... | collective-permute-start | bytes 208904 | tf_op jit(solution)/shard_map/ppermute | solution.py:42
  38.6 10.3 %collective-permute-start.36 = (f32[17,8,128]{2,1,0:T(8,128)S(1)}, f32[17,8,128]{2,1,0:T(8,128)S(1)}, u32[]{:S(2)}, u32[]{:S(2)}) collective-permute-start(f32[17,8,128]{2,1,0:T(8,128)S(1)} %get-tuple-element.108.refs_0_), channel_id=1, source_target_pairs={{0,8},{4,12},{8,0},{12,4},{16,24},{20,28},{24,16},{28,20},{1,9},{5... | collective-permute-start | bytes 208904 | tf_op jit(solution)/shard_map/ppermute | solution.py:42
  39.3 9.7 %collective-permute-start.37 = (f32[17,8,128]{2,1,0:T(8,128)S(1)}, f32[17,8,128]{2,1,0:T(8,128)S(1)}, u32[]{:S(2)}, u32[]{:S(2)}) collective-permute-start(f32[17,8,128]{2,1,0:T(8,128)S(1)} %get-tuple-element.108.refs_0_), channel_id=1, source_target_pairs={{0,12},{4,8},{8,4},{12,0},{16,28},{20,24},{24,20},{28,16},{1,13},{... | collective-permute-start | bytes 208904 | tf_op jit(solution)/shard_map/ppermute | solution.py:42
  42.5 8.4 %collective-permute-start.11 = (f32[17,8,128]{2,1,0:T(8,128)S(1)}, f32[17,8,128]{2,1,0:T(8,128)S(1)}, u32[]{:S(2)}, u32[]{:S(2)}) collective-permute-start(f32[17,8,128]{2,1,0:T(8,128)S(1)} %get-tuple-element.83), channel_id=1, source_target_pairs={{0,1},{1,0},{2,3},{3,2},{4,5},{5,4},{6,7},{7,6},{8,9},{9,8},{10,11... | collective-permute-start | bytes 208904 | tf_op jit(solution)/shard_map/ppermute | solution.py:42
  42.6 6.3 %collective-permute-start.14 = (f32[16,1024]{1,0:T(8,128)S(1)}, f32[16,1024]{1,0:T(8,128)S(1)}, u32[]{:S(2)}, u32[]{:S(2)}) collective-permute-start(f32[16,1024]{1,0:T(8,128)S(1)} %bitcast.36), channel_id=1, source_target_pairs={{0,12},{4,16},{8,20},{12,24},{16,28},{20,0},{24,4},{28,8},{1,13},{... | collective-permute-start | bytes 196616 | tf_op jit(solution)/shard_map/ppermute | solution.py:47
  57.1 6.1 %collective-permute-start.40 = (f32[17,8,128]{2,1,0:T(8,128)S(1)}, f32[17,8,128]{2,1,0:T(8,128)S(1)}, u32[]{:S(2)}, u32[]{:S(2)}) collective-permute-start(f32[17,8,128]{2,1,0:T(8,128)S(1)} %get-tuple-element.112.refs_0_.refs_3_), channel_id=1, source_target_pairs={{0,1},{1,0},{2,3},{3,2},{4,5},{5,4},{6,7},{7,6},{8,9},{9,8},{10,11... | collective-permute-start | bytes 208904 | tf_op jit(solution)/shard_map/ppermute | solution.py:42
  59.3 8.0 %collective-permute-start.17 = (f32[17,8,128]{2,1,0:T(8,128)S(1)}, f32[17,8,128]{2,1,0:T(8,128)S(1)}, u32[]{:S(2)}, u32[]{:S(2)}) collective-permute-start(f32[17,8,128]{2,1,0:T(8,128)S(1)} %get-tuple-element.87), channel_id=1, source_target_pairs={{0,4},{4,0},{8,12},{12,8},{16,20},{20,16},{24,28},{28,24},{1,5},{5... | collective-permute-start | bytes 208904 | tf_op jit(solution)/shard_map/ppermute | solution.py:42
  61.7 6.9 %collective-permute-start.18 = (f32[17,8,128]{2,1,0:T(8,128)S(1)}, f32[17,8,128]{2,1,0:T(8,128)S(1)}, u32[]{:S(2)}, u32[]{:S(2)}) collective-permute-start(f32[17,8,128]{2,1,0:T(8,128)S(1)} %get-tuple-element.88), channel_id=1, source_target_pairs={{0,8},{4,12},{8,0},{12,4},{16,24},{20,28},{24,16},{28,20},{1,9},{5... | collective-permute-start | bytes 208904 | tf_op jit(solution)/shard_map/ppermute | solution.py:42
  61.8 6.8 %collective-permute-start.19 = (f32[17,8,128]{2,1,0:T(8,128)S(1)}, f32[17,8,128]{2,1,0:T(8,128)S(1)}, u32[]{:S(2)}, u32[]{:S(2)}) collective-permute-start(f32[17,8,128]{2,1,0:T(8,128)S(1)} %get-tuple-element.89), channel_id=1, source_target_pairs={{0,12},{4,8},{8,4},{12,0},{16,28},{20,24},{24,20},{28,16},{1,13},{... | collective-permute-start | bytes 208904 | tf_op jit(solution)/shard_map/ppermute | solution.py:42
  68.7 5.9 %collective-permute-start.20 = (f32[17,8,128]{2,1,0:T(8,128)S(1)}, f32[17,8,128]{2,1,0:T(8,128)S(1)}, u32[]{:S(2)}, u32[]{:S(2)}) collective-permute-start(f32[17,8,128]{2,1,0:T(8,128)S(1)} %add_add_fusion.4.refs_0_), channel_id=1, source_target_pairs={{0,16},{4,20},{8,24},{12,28},{16,0},{20,4},{24,8},{28,12},{1,17},{... | collective-permute-start | bytes 208904 | tf_op jit(solution)/shard_map/ppermute | solution.py:42
  72.7 6.5 %collective-permute-start.44 = (f32[17,8,128]{2,1,0:T(8,128)S(1)}, f32[17,8,128]{2,1,0:T(8,128)S(1)}, u32[]{:S(2)}, u32[]{:S(2)}) collective-permute-start(f32[17,8,128]{2,1,0:T(8,128)S(1)} %add_add_fusion.1.refs_0_), channel_id=1, source_target_pairs={{0,16},{4,20},{8,24},{12,28},{16,0},{20,4},{24,8},{28,12},{1,17},{... | collective-permute-start | bytes 208904 | tf_op jit(solution)/shard_map/ppermute | solution.py:42
  74.7 6.6 %collective-permute-start.21 = (f32[17,8,128]{2,1,0:T(8,128)S(1)}, f32[17,8,128]{2,1,0:T(8,128)S(1)}, u32[]{:S(2)}, u32[]{:S(2)}) collective-permute-start(f32[17,8,128]{2,1,0:T(8,128)S(1)} %get-tuple-element.92.refs_0_), channel_id=1, source_target_pairs={{0,4},{4,0},{8,12},{12,8},{16,20},{20,16},{24,28},{28,24},{1,5},{5... | collective-permute-start | bytes 208904 | tf_op jit(solution)/shard_map/ppermute | solution.py:42
  77.6 5.9 %collective-permute-start.23 = (f32[17,8,128]{2,1,0:T(8,128)S(1)}, f32[17,8,128]{2,1,0:T(8,128)S(1)}, u32[]{:S(2)}, u32[]{:S(2)}) collective-permute-start(f32[17,8,128]{2,1,0:T(8,128)S(1)} %get-tuple-element.92.refs_0_), channel_id=1, source_target_pairs={{0,12},{4,8},{8,4},{12,0},{16,28},{20,24},{24,20},{28,16},{1,13},{... | collective-permute-start | bytes 208904 | tf_op jit(solution)/shard_map/ppermute | solution.py:42
  79.3 6.2 %collective-permute-start.45 = (f32[17,8,128]{2,1,0:T(8,128)S(1)}, f32[17,8,128]{2,1,0:T(8,128)S(1)}, u32[]{:S(2)}, u32[]{:S(2)}) collective-permute-start(f32[17,8,128]{2,1,0:T(8,128)S(1)} %get-tuple-element.119.refs_0_), channel_id=1, source_target_pairs={{0,4},{4,0},{8,12},{12,8},{16,20},{20,16},{24,28},{28,24},{1,5},{5... | collective-permute-start | bytes 208904 | tf_op jit(solution)/shard_map/ppermute | solution.py:42
  96.8 7.6 %collective-permute-start.27 = (f32[17,8,128]{2,1,0:T(8,128)S(1)}, f32[17,8,128]{2,1,0:T(8,128)S(1)}, u32[]{:S(2)}, u32[]{:S(2)}) collective-permute-start(f32[17,8,128]{2,1,0:T(8,128)S(1)} %get-tuple-element.98), channel_id=1, source_target_pairs={{0,4},{4,0},{8,12},{12,8},{16,20},{20,16},{24,28},{28,24},{1,5},{5... | collective-permute-start | bytes 208904 | tf_op jit(solution)/shard_map/ppermute | solution.py:42
  98.2 7.6 %collective-permute-start.28 = (f32[17,8,128]{2,1,0:T(8,128)S(1)}, f32[17,8,128]{2,1,0:T(8,128)S(1)}, u32[]{:S(2)}, u32[]{:S(2)}) collective-permute-start(f32[17,8,128]{2,1,0:T(8,128)S(1)} %get-tuple-element.99), channel_id=1, source_target_pairs={{0,8},{4,12},{8,0},{12,4},{16,24},{20,28},{24,16},{28,20},{1,9},{5... | collective-permute-start | bytes 208904 | tf_op jit(solution)/shard_map/ppermute | solution.py:42
  99.0 6.8 %collective-permute-start.29 = (f32[17,8,128]{2,1,0:T(8,128)S(1)}, f32[17,8,128]{2,1,0:T(8,128)S(1)}, u32[]{:S(2)}, u32[]{:S(2)}) collective-permute-start(f32[17,8,128]{2,1,0:T(8,128)S(1)} %get-tuple-element.100), channel_id=1, source_target_pairs={{0,12},{4,8},{8,4},{12,0},{16,28},{20,24},{24,20},{28,16},{1,13},{... | collective-permute-start | bytes 208904 | tf_op jit(solution)/shard_map/ppermute | solution.py:42
  105.8 6.1 %collective-permute-start.30 = (f32[17,8,128]{2,1,0:T(8,128)S(1)}, f32[17,8,128]{2,1,0:T(8,128)S(1)}, u32[]{:S(2)}, u32[]{:S(2)}) collective-permute-start(f32[17,8,128]{2,1,0:T(8,128)S(1)} %add_add_fusion.3.refs_0_), channel_id=1, source_target_pairs={{0,16},{4,20},{8,24},{12,28},{16,0},{20,4},{24,8},{28,12},{1,17},{... | collective-permute-start | bytes 208904 | tf_op jit(solution)/shard_map/ppermute | solution.py:42
  110.2 6.0 %collective-permute-start.54 = (f32[17,8,128]{2,1,0:T(8,128)S(1)}, f32[17,8,128]{2,1,0:T(8,128)S(1)}, u32[]{:S(2)}, u32[]{:S(2)}) collective-permute-start(f32[17,8,128]{2,1,0:T(8,128)S(1)} %add_add_fusion.refs_0_), channel_id=1, source_target_pairs={{0,16},{4,20},{8,24},{12,28},{16,0},{20,4},{24,8},{28,12},{1,17},{... | collective-permute-start | bytes 208904 | tf_op jit(solution)/shard_map/ppermute | solution.py:42
  112.6 6.5 %collective-permute-start.55 = (f32[17,8,128]{2,1,0:T(8,128)S(1)}, f32[17,8,128]{2,1,0:T(8,128)S(1)}, u32[]{:S(2)}, u32[]{:S(2)}) collective-permute-start(f32[17,8,128]{2,1,0:T(8,128)S(1)} %get-tuple-element.131.refs_0_), channel_id=1, source_target_pairs={{0,4},{4,0},{8,12},{12,8},{16,20},{20,16},{24,28},{28,24},{1,5},{5... | collective-permute-start | bytes 208904 | tf_op jit(solution)/shard_map/ppermute | solution.py:42
  114.6 5.9 %collective-permute-start.56 = (f32[17,8,128]{2,1,0:T(8,128)S(1)}, f32[17,8,128]{2,1,0:T(8,128)S(1)}, u32[]{:S(2)}, u32[]{:S(2)}) collective-permute-start(f32[17,8,128]{2,1,0:T(8,128)S(1)} %get-tuple-element.131.refs_0_), channel_id=1, source_target_pairs={{0,8},{4,12},{8,0},{12,4},{16,24},{20,28},{24,16},{28,20},{1,9},{5... | collective-permute-start | bytes 208904 | tf_op jit(solution)/shard_map/ppermute | solution.py:42
  114.9 5.8 %collective-permute-start.57 = (f32[17,8,128]{2,1,0:T(8,128)S(1)}, f32[17,8,128]{2,1,0:T(8,128)S(1)}, u32[]{:S(2)}, u32[]{:S(2)}) collective-permute-start(f32[17,8,128]{2,1,0:T(8,128)S(1)} %get-tuple-element.131.refs_0_), channel_id=1, source_target_pairs={{0,12},{4,8},{8,4},{12,0},{16,28},{20,24},{24,20},{28,16},{1,13},{... | collective-permute-start | bytes 208904 | tf_op jit(solution)/shard_map/ppermute | solution.py:42
  (42 other events, 249.2 us)

commit v6 on v5

--- a/solution.py
+++ b/solution.py
@@ -289,8 +289,8 @@
         if not first:
             primal_ref, square_ref = rest[:2]
             rest = rest[2:]
-        new_ref, message = rest[:2]
-        rest = rest[2:]
+        message = rest[0]
+        rest = rest[1:]
         weight_now = weight_ref[...]
         if not first:
             weight_now = next_weight(
@@ -311,20 +311,20 @@
                 after = jnp.maximum(before - primal_step * (cost - pull), 0.0)
                 change = after - before
                 square = square + change * change
-                new_ref[here] = after
                 message[here] = 2.0 * after - before
-                if last and chunk == 0:
+                if not last:
+                    rest[0][here] = after
+                elif chunk == 0:
                     rest[0][:, lanes] = after
             squares.append(square)
         message[2 * sub] = squares[0] + squares[1]
 
     inputs = [own, other, *starts, weight]
-    outputs = [(2 * sub, scen, tile), (2 * sub + 1, scen, tile)]
+    outputs = [(2 * sub + 1, scen, tile)]
     if not first:
         inputs += [primal, primal_square]
         outputs.append((scen, tile))
-    if last:
-        outputs.append((scen, sub * tile))
+    outputs.append((scen, sub * tile) if last else (2 * sub, scen, tile))
     return call_in_vmem(body, inputs, outputs)
 
 
@@ -442,11 +442,10 @@
             total, other, start_rows, state["primal"], state["weight"],
             state["primal_square"], rows, sub, last,
         )
-        state["primal"], ahead = results[:2]
+        ahead = results[0]
         if iteration:
-            state["weight"] = results[2]
-        if last:
-            state["primal_rows"] = results[-1]
+            state["weight"] = results[1]
+        state["primal_rows" if last else "primal"] = results[-1]
         for bit in order[-2::-1]:
             got = exchanged(ahead, "band", 1 << bit)
             ahead = jnp.concatenate([ahead[:-1], got[:-1], ahead[-1:] + got[-1:]])

time: 146 us -> 145 us (level)
  transfers between devices with their start and end apart: 70 -> 70, of which waited for: 32 -> 31; matrix products, arithmetic and copies ran while one was open for 2% -> 2% of each run, Pallas kernels for 18% -> 18%
where the time goes in v6:
time: 145 us
  starting transfers between devices  72.5 us (50%)
  waiting for transfers between devices  40.9 us (28%)
  Pallas kernels  27.3 us (19%)
  other arithmetic  3.12 us (2%)
    ppermute x67, starting transfers between devices, exchanged(): lax.ppermute(value, axis, [(source, source ^ mask) for source in range(co...  67.4 us
    ppermute x67, waiting for transfers between devices, exchanged(): lax.ppermute(value, axis, [(source, source ^ mask) for source in range(co...  36.4 us
    pallas_call x25, Pallas kernels, call_in_vmem(): pl.pallas_call(body, out_shape=[pltpu.VMEM(shape, F32) for shape in outpu...  22.9 us
    ppermute x3, starting transfers between devices, passed_along(): lax.ppermute(value, axis, [(source, (source + steps) % count) for source...  5.06 us
    ppermute x3, waiting for transfers between devices, passed_along(): lax.ppermute(value, axis, [(source, (source + steps) % count) for source...  4.52 us
    pallas_call x1, Pallas kernels, prepared(): pl.pallas_call(body, out_shape=[pltpu.VMEM((count, 2 * tile, tile), BF16)...  4.36 us
  transfers between devices with their start and end apart: 70, of which 31 were waited for; matrix products, arithmetic and copies ran while one was open for 2% of the time, Pallas kernels for 18%

profile of v6, /device:TPU:0, one launch (start us, length us, event | category | flops | bytes accessed | tf_op | source)
XLA Modules:
  0.0 145.2 jit_solution(12074779168524134323)
XLA Ops:
  0.6 3.0 %collective-permute-start = (f32[16,1024]{1,0:T(8,128)}, f32[16,1024]{1,0:T(8,128)S(1)}, u32[]{:S(2)}, u32[]{:S(2)}) collective-permute-start(f32[16,1024]{1,0:T(8,128)} %bitcast.27), channel_id=1, source_target_pairs={{0,2},{1,3},{2,0},{3,1},{4,6},{5,7},{6,4},{7,5},{8,10},{9,11},{10,... | collective-permute-start | bytes 196616 | tf_op jit(solution)/shard_map/ppermute | solution.py:42
  4.4 4.4 %shard_map.103 = (bf16[128,256,128]{2,1,0:T(8,128)(2,1)S(1)}, bf16[128,256,128]{2,1,0:T(8,128)(2,1)S(1)}, f32[33,1024]{1,0:T(8,128)S(1)}) custom-call(f32[128,128,128]{2,1,0:T(8,128)} %bitcast.39, f32[16,1024]{1,0:T(8,128)} %bitcast.40, f32[16,1024]{1,0:T(8,128)} %bitcast.33, f32[1,1024]{1,0:T(1,128)} %bitcast.41), custom_call_target="tpu_custom_call" | custom-call | tf_op jit(solution)/shard_map/pallas_call | solution.py:139
  10.2 1.8 %shard_map.104 = (f32[17,8,128]{2,1,0:T(8,128)S(1)}, f32[17,8,128]{2,1,0:T(8,128)S(1)}, f32[17,8,128]{2,1,0:T(8,128)S(1)}, f32[17,8,128]{2,1,0:T(8,128)S(1)}) custom-call(s32[256]{0:T(256)S(1)} %pad_add_fusion.index_ref, bf16[128,256,128]{2,1,0:T(8,128)(2,1)S(1)} %get-tuple-element.74.tiles_ref, f32[16,1024]{1,0:T(8,128)S(1)} %bitcast.29, ...), custom_call_target="tpu_custom_call" | custom-call | tf_op jit(solution)/shard_map/pallas_call | solution.py:71
  15.6 2.6 %collective-permute-start.7 = (f32[33,1024]{1,0:T(8,128)S(1)}, f32[33,1024]{1,0:T(8,128)S(1)}, u32[]{:S(2)}, u32[]{:S(2)}) collective-permute-start(f32[33,1024]{1,0:T(8,128)S(1)} %get-tuple-element.80.refs_2_), channel_id=1, source_target_pairs={{0,16},{4,20},{8,24},{12,28},{16,0},{20,4},{24,8},{28,12},{1,17},{... | collective-permute-start | bytes 405512 | tf_op jit(solution)/shard_map/ppermute | solution.py:42
  24.4 2.8 %collective-permute-done.32 = f32[17,8,128]{2,1,0:T(8,128)S(1)} collective-permute-done((f32[17,8,128]{2,1,0:T(8,128)S(1)}, f32[17,8,128]{2,1,0:T(8,128)S(1)}, u32[]{:S(2)}, u32[]{:S(2)}) %collective-permute-start.32) | collective-permute-done | bytes 69664 | tf_op jit(solution)/shard_map/ppermute | solution.py:42
  30.1 2.8 %collective-permute-start.10 = (f32[17,8,128]{2,1,0:T(8,128)S(1)}, f32[17,8,128]{2,1,0:T(8,128)S(1)}, u32[]{:S(2)}, u32[]{:S(2)}) collective-permute-start(f32[17,8,128]{2,1,0:T(8,128)S(1)} %get-tuple-element.81.refs_0_), channel_id=1, source_target_pairs={{0,12},{4,8},{8,4},{12,0},{16,28},{20,24},{24,20},{28,16},{1,13},{... | collective-permute-start | bytes 208904 | tf_op jit(solution)/shard_map/ppermute | solution.py:42
  34.9 2.0 %collective-permute-start.13 = (f32[16,1024]{1,0:T(8,128)S(1)}, f32[16,1024]{1,0:T(8,128)S(1)}, u32[]{:S(2)}, u32[]{:S(2)}) collective-permute-start(f32[16,1024]{1,0:T(8,128)S(1)} %bitcast.35), channel_id=1, source_target_pairs={{0,8},{4,12},{8,16},{12,20},{16,24},{20,28},{24,0},{28,4},{1,9},{5... | collective-permute-start | bytes 196616 | tf_op jit(solution)/shard_map/ppermute | solution.py:47
  40.6 1.9 %shard_map.106 = (f32[17,8,128]{2,1,0:T(8,128)S(1)}, f32[17,8,128]{2,1,0:T(8,128)S(1)}) custom-call(s32[256]{0:T(256)S(1)} %pad_add_fusion.index_ref, bf16[128,256,128]{2,1,0:T(8,128)(2,1)S(1)} %get-tuple-element.75.tiles_ref, f32[17,8,128]{2,1,0:T(8,128)S(1)} %get-tuple-element.81.refs_0_, f32[17,8,128]{2,1,0:T(8,128)S(1)} %collective-permute-done.8.refs_1_, ...), custom_call_target="tpu_custom_call" | custom-call | tf_op jit(solution)/shard_map/pallas_call | solution.py:71
  44.4 4.5 %collective-permute-done.14.refs_2_ = f32[16,1024]{1,0:T(8,128)S(1)} collective-permute-done((f32[16,1024]{1,0:T(8,128)S(1)}, f32[16,1024]{1,0:T(8,128)S(1)}, u32[]{:S(2)}, u32[]{:S(2)}) %collective-permute-start.14) | collective-permute-done | bytes 65568 | tf_op jit(solution)/shard_map/ppermute | solution.py:47
  49.0 1.9 %shard_map.117 = (f32[17,8,128]{2,1,0:T(8,128)S(1)}, f32[17,8,128]{2,1,0:T(8,128)S(1)}) custom-call(s32[256]{0:T(256)S(1)} %pad_add_fusion.index_ref, bf16[128,256,128]{2,1,0:T(8,128)(2,1)S(1)} %get-tuple-element.75.tiles_ref, f32[17,8,128]{2,1,0:T(8,128)S(1)} %get-tuple-element.108.refs_0_, f32[17,8,128]{2,1,0:T(8,128)S(1)} %collective-permute-done.35.refs_1_, ...), custom_call_target="tpu_custom_call" | custom-call | tf_op jit(solution)/shard_map/pallas_call | solution.py:71
  53.1 2.9 %collective-permute-done.15.refs_1_ = f32[17,8,128]{2,1,0:T(8,128)S(1)} collective-permute-done((f32[17,8,128]{2,1,0:T(8,128)S(1)}, f32[17,8,128]{2,1,0:T(8,128)S(1)}, u32[]{:S(2)}, u32[]{:S(2)}) %collective-permute-start.15) | collective-permute-done | bytes 69664 | tf_op jit(solution)/shard_map/ppermute | solution.py:42
  57.4 1.8 %shard_map.109 = (f32[17,8,128]{2,1,0:T(8,128)S(1)}, f32[17,8,128]{2,1,0:T(8,128)S(1)}, f32[17,8,128]{2,1,0:T(8,128)S(1)}, f32[17,8,128]{2,1,0:T(8,128)S(1)}) custom-call(s32[256]{0:T(256)S(1)} %pad_add_fusion.index_ref, bf16[128,256,128]{2,1,0:T(8,128)(2,1)S(1)} %get-tuple-element.74.tiles_ref, f32[17,8,128]{2,1,0:T(8,128)S(1)} %get-tuple-element.85.refs_0_.refs_3_, ...), custom_call_target="tpu_custom_call" | custom-call | tf_op jit(solution)/shard_map/pallas_call | solution.py:71
  59.3 2.4 %collective-permute-start.17 = (f32[17,8,128]{2,1,0:T(8,128)S(1)}, f32[17,8,128]{2,1,0:T(8,128)S(1)}, u32[]{:S(2)}, u32[]{:S(2)}) collective-permute-start(f32[17,8,128]{2,1,0:T(8,128)S(1)} %get-tuple-element.87), channel_id=1, source_target_pairs={{0,4},{4,0},{8,12},{12,8},{16,20},{20,16},{24,28},{28,24},{1,5},{5... | collective-permute-start | bytes 208904 | tf_op jit(solution)/shard_map/ppermute | solution.py:42
  63.2 1.8 %shard_map.119 = (f32[17,8,128]{2,1,0:T(8,128)S(1)}, f32[17,8,128]{2,1,0:T(8,128)S(1)}, f32[17,8,128]{2,1,0:T(8,128)S(1)}, f32[17,8,128]{2,1,0:T(8,128)S(1)}) custom-call(s32[256]{0:T(256)S(1)} %pad_add_fusion.index_ref, bf16[128,256,128]{2,1,0:T(8,128)(2,1)S(1)} %get-tuple-element.74.tiles_ref, f32[17,8,128]{2,1,0:T(8,128)S(1)} %get-tuple-element.112.refs_0_.refs_3_, ...), custom_call_target="tpu_custom_call" | custom-call | tf_op jit(solution)/shard_map/pallas_call | solution.py:71
  65.1 2.0 %collective-permute-start.41 = (f32[17,8,128]{2,1,0:T(8,128)S(1)}, f32[17,8,128]{2,1,0:T(8,128)S(1)}, u32[]{:S(2)}, u32[]{:S(2)}) collective-permute-start(f32[17,8,128]{2,1,0:T(8,128)S(1)} %get-tuple-element.114), channel_id=1, source_target_pairs={{0,4},{4,0},{8,12},{12,8},{16,20},{20,16},{24,28},{28,24},{1,5},{5... | collective-permute-start | bytes 208904 | tf_op jit(solution)/shard_map/ppermute | solution.py:42
  70.3 2.0 %collective-permute-done.42 = f32[17,8,128]{2,1,0:T(8,128)S(1)} collective-permute-done((f32[17,8,128]{2,1,0:T(8,128)S(1)}, f32[17,8,128]{2,1,0:T(8,128)S(1)}, u32[]{:S(2)}, u32[]{:S(2)}) %collective-permute-start.42) | collective-permute-done | bytes 69664 | tf_op jit(solution)/shard_map/ppermute | solution.py:42
  72.7 1.8 %collective-permute-start.44 = (f32[17,8,128]{2,1,0:T(8,128)S(1)}, f32[17,8,128]{2,1,0:T(8,128)S(1)}, u32[]{:S(2)}, u32[]{:S(2)}) collective-permute-start(f32[17,8,128]{2,1,0:T(8,128)S(1)} %add_add_fusion.1.refs_0_), channel_id=1, source_target_pairs={{0,16},{4,20},{8,24},{12,28},{16,0},{20,4},{24,8},{28,12},{1,17},{... | collective-permute-start | bytes 208904 | tf_op jit(solution)/shard_map/ppermute | solution.py:42
  74.7 2.9 %collective-permute-start.21 = (f32[17,8,128]{2,1,0:T(8,128)S(1)}, f32[17,8,128]{2,1,0:T(8,128)S(1)}, u32[]{:S(2)}, u32[]{:S(2)}) collective-permute-start(f32[17,8,128]{2,1,0:T(8,128)S(1)} %get-tuple-element.92.refs_0_), channel_id=1, source_target_pairs={{0,4},{4,0},{8,12},{12,8},{16,20},{20,16},{24,28},{28,24},{1,5},{5... | collective-permute-start | bytes 208904 | tf_op jit(solution)/shard_map/ppermute | solution.py:42
  79.3 2.0 %collective-permute-start.45 = (f32[17,8,128]{2,1,0:T(8,128)S(1)}, f32[17,8,128]{2,1,0:T(8,128)S(1)}, u32[]{:S(2)}, u32[]{:S(2)}) collective-permute-start(f32[17,8,128]{2,1,0:T(8,128)S(1)} %get-tuple-element.119.refs_0_), channel_id=1, source_target_pairs={{0,4},{4,0},{8,12},{12,8},{16,20},{20,16},{24,28},{28,24},{1,5},{5... | collective-permute-start | bytes 208904 | tf_op jit(solution)/shard_map/ppermute | solution.py:42
  83.5 1.9 %shard_map.111 = (f32[17,8,128]{2,1,0:T(8,128)S(1)}, f32[17,8,128]{2,1,0:T(8,128)S(1)}) custom-call(s32[256]{0:T(256)S(1)} %pad_add_fusion.index_ref, bf16[128,256,128]{2,1,0:T(8,128)(2,1)S(1)} %get-tuple-element.75.tiles_ref, f32[17,8,128]{2,1,0:T(8,128)S(1)} %get-tuple-element.92.refs_0_, f32[17,8,128]{2,1,0:T(8,128)S(1)} %collective-permute-done.21.refs_1_, ...), custom_call_target="tpu_custom_call" | custom-call | tf_op jit(solution)/shard_map/pallas_call | solution.py:71
  86.5 1.9 %shard_map.121 = (f32[17,8,128]{2,1,0:T(8,128)S(1)}, f32[17,8,128]{2,1,0:T(8,128)S(1)}) custom-call(s32[256]{0:T(256)S(1)} %pad_add_fusion.index_ref, bf16[128,256,128]{2,1,0:T(8,128)(2,1)S(1)} %get-tuple-element.75.tiles_ref, f32[17,8,128]{2,1,0:T(8,128)S(1)} %get-tuple-element.119.refs_0_, f32[17,8,128]{2,1,0:T(8,128)S(1)} %collective-permute-done.45.refs_1_, ...), custom_call_target="tpu_custom_call" | custom-call | tf_op jit(solution)/shard_map/pallas_call | solution.py:71
  90.7 2.9 %collective-permute-done.25.refs_1_ = f32[17,8,128]{2,1,0:T(8,128)S(1)} collective-permute-done((f32[17,8,128]{2,1,0:T(8,128)S(1)}, f32[17,8,128]{2,1,0:T(8,128)S(1)}, u32[]{:S(2)}, u32[]{:S(2)}) %collective-permute-start.25) | collective-permute-done | bytes 69664 | tf_op jit(solution)/shard_map/ppermute | solution.py:42
  95.0 1.8 %shard_map.113 = (f32[17,8,128]{2,1,0:T(8,128)S(1)}, f32[17,8,128]{2,1,0:T(8,128)S(1)}, f32[17,8,128]{2,1,0:T(8,128)S(1)}, f32[17,8,128]{2,1,0:T(8,128)S(1)}) custom-call(s32[256]{0:T(256)S(1)} %pad_add_fusion.index_ref, bf16[128,256,128]{2,1,0:T(8,128)(2,1)S(1)} %get-tuple-element.74.tiles_ref, f32[17,8,128]{2,1,0:T(8,128)S(1)} %get-tuple-element.96.refs_0_.refs_3_, ...), custom_call_target="tpu_custom_call" | custom-call | tf_op jit(solution)/shard_map/pallas_call | solution.py:71
  100.3 1.8 %shard_map.123 = (f32[17,8,128]{2,1,0:T(8,128)S(1)}, f32[17,8,128]{2,1,0:T(8,128)S(1)}, f32[17,8,128]{2,1,0:T(8,128)S(1)}, f32[17,8,128]{2,1,0:T(8,128)S(1)}) custom-call(s32[256]{0:T(256)S(1)} %pad_add_fusion.index_ref, bf16[128,256,128]{2,1,0:T(8,128)(2,1)S(1)} %get-tuple-element.74.tiles_ref, f32[17,8,128]{2,1,0:T(8,128)S(1)} %get-tuple-element.123.refs_0_.refs_3_, ...), custom_call_target="tpu_custom_call" | custom-call | tf_op jit(solution)/shard_map/pallas_call | solution.py:71
  105.8 2.0 %collective-permute-start.30 = (f32[17,8,128]{2,1,0:T(8,128)S(1)}, f32[17,8,128]{2,1,0:T(8,128)S(1)}, u32[]{:S(2)}, u32[]{:S(2)}) collective-permute-start(f32[17,8,128]{2,1,0:T(8,128)S(1)} %add_add_fusion.3.refs_0_), channel_id=1, source_target_pairs={{0,16},{4,20},{8,24},{12,28},{16,0},{20,4},{24,8},{28,12},{1,17},{... | collective-permute-start | bytes 208904 | tf_op jit(solution)/shard_map/ppermute | solution.py:42
  112.0 2.0 %collective-permute-start.55 = (f32[17,8,128]{2,1,0:T(8,128)S(1)}, f32[17,8,128]{2,1,0:T(8,128)S(1)}, u32[]{:S(2)}, u32[]{:S(2)}) collective-permute-start(f32[17,8,128]{2,1,0:T(8,128)S(1)} %get-tuple-element.131.refs_0_), channel_id=1, source_target_pairs={{0,4},{4,0},{8,12},{12,8},{16,20},{20,16},{24,28},{28,24},{1,5},{5... | collective-permute-start | bytes 208904 | tf_op jit(solution)/shard_map/ppermute | solution.py:42
  119.8 1.9 %shard_map.125 = (f32[17,8,128]{2,1,0:T(8,128)S(1)}, f32[17,8,128]{2,1,0:T(8,128)S(1)}) custom-call(s32[256]{0:T(256)S(1)} %pad_add_fusion.index_ref, bf16[128,256,128]{2,1,0:T(8,128)(2,1)S(1)} %get-tuple-element.75.tiles_ref, f32[17,8,128]{2,1,0:T(8,128)S(1)} %get-tuple-element.131.refs_0_, f32[17,8,128]{2,1,0:T(8,128)S(1)} %collective-permute-done.55.refs_1_, ...), custom_call_target="tpu_custom_call" | custom-call | tf_op jit(solution)/shard_map/pallas_call | solution.py:71
  123.7 1.9 %shard_map.127 = (f32[17,8,128]{2,1,0:T(8,128)S(1)}, f32[17,8,128]{2,1,0:T(8,128)S(1)}) custom-call(s32[256]{0:T(256)S(1)} %pad_add_fusion.index_ref, bf16[128,256,128]{2,1,0:T(8,128)(2,1)S(1)} %get-tuple-element.75.tiles_ref, f32[17,8,128]{2,1,0:T(8,128)S(1)} %get-tuple-element.136.refs_0_, f32[17,8,128]{2,1,0:T(8,128)S(1)} %collective-permute-done.60.refs_1_, ...), custom_call_target="tpu_custom_call" | custom-call | tf_op jit(solution)/shard_map/pallas_call | solution.py:71
  127.8 2.9 %collective-permute-done.59.refs_1_ = f32[17,8,128]{2,1,0:T(8,128)S(1)} collective-permute-done((f32[17,8,128]{2,1,0:T(8,128)S(1)}, f32[17,8,128]{2,1,0:T(8,128)S(1)}, u32[]{:S(2)}, u32[]{:S(2)}) %collective-permute-start.59) | collective-permute-done | bytes 69664 | tf_op jit(solution)/shard_map/ppermute | solution.py:42
  133.7 1.9 %collective-permute-done.66 = f32[16,128]{1,0:T(8,128)S(1)} collective-permute-done((f32[16,128]{1,0:T(8,128)S(1)}, f32[16,128]{1,0:T(8,128)S(1)}, u32[]{:S(2)}, u32[]{:S(2)}) %collective-permute-start.66) | collective-permute-done | bytes 8224 | tf_op jit(solution)/shard_map/ppermute | solution.py:42
  137.7 2.1 %collective-permute-done.68 = f32[16,128]{1,0:T(8,128)S(1)} collective-permute-done((f32[16,128]{1,0:T(8,128)S(1)}, f32[16,128]{1,0:T(8,128)S(1)}, u32[]{:S(2)}, u32[]{:S(2)}) %collective-permute-start.68) | collective-permute-done | bytes 8224 | tf_op jit(solution)/shard_map/ppermute | solution.py:42
  139.8 2.1 %collective-permute-start.69 = (f32[16,128]{1,0:T(8,128)S(1)}, f32[16,128]{1,0:T(8,128)S(1)}, u32[]{:S(2)}, u32[]{:S(2)}) collective-permute-start(f32[16,128]{1,0:T(8,128)S(1)} %add.167), channel_id=1, source_target_pairs={{0,16},{4,20},{8,24},{12,28},{16,0},{20,4},{24,8},{28,12},{1,17},{... | collective-permute-start | bytes 24584 | tf_op jit(solution)/shard_map/ppermute | solution.py:42
  (169 shorter events, 69.5 us)
Async XLA Ops:
  0.6 8.1 %collective-permute-start = (f32[16,1024]{1,0:T(8,128)}, f32[16,1024]{1,0:T(8,128)S(1)}, u32[]{:S(2)}, u32[]{:S(2)}) collective-permute-start(f32[16,1024]{1,0:T(8,128)} %bitcast.27), channel_id=1, source_target_pairs={{0,2},{1,3},{2,0},{3,1},{4,6},{5,7},{6,4},{7,5},{8,10},{9,11},{10,... | collective-permute-start | bytes 196616 | tf_op jit(solution)/shard_map/ppermute | solution.py:42
  12.0 9.6 %collective-permute-start.3 = (f32[17,8,128]{2,1,0:T(8,128)S(1)}, f32[17,8,128]{2,1,0:T(8,128)S(1)}, u32[]{:S(2)}, u32[]{:S(2)}) collective-permute-start(f32[17,8,128]{2,1,0:T(8,128)S(1)} %get-tuple-element.77), channel_id=1, source_target_pairs={{0,4},{4,0},{8,12},{12,8},{16,20},{20,16},{24,28},{28,24},{1,5},{5... | collective-permute-start | bytes 208904 | tf_op jit(solution)/shard_map/ppermute | solution.py:42
  13.6 9.6 %collective-permute-start.4 = (f32[17,8,128]{2,1,0:T(8,128)S(1)}, f32[17,8,128]{2,1,0:T(8,128)S(1)}, u32[]{:S(2)}, u32[]{:S(2)}) collective-permute-start(f32[17,8,128]{2,1,0:T(8,128)S(1)} %get-tuple-element.78), channel_id=1, source_target_pairs={{0,8},{4,12},{8,0},{12,4},{16,24},{20,28},{24,16},{28,20},{1,9},{5... | collective-permute-start | bytes 208904 | tf_op jit(solution)/shard_map/ppermute | solution.py:42
  15.2 8.4 %collective-permute-start.5 = (f32[17,8,128]{2,1,0:T(8,128)S(1)}, f32[17,8,128]{2,1,0:T(8,128)S(1)}, u32[]{:S(2)}, u32[]{:S(2)}) collective-permute-start(f32[17,8,128]{2,1,0:T(8,128)S(1)} %get-tuple-element.79), channel_id=1, source_target_pairs={{0,12},{4,8},{8,4},{12,0},{16,28},{20,24},{24,20},{28,16},{1,13},{... | collective-permute-start | bytes 208904 | tf_op jit(solution)/shard_map/ppermute | solution.py:42
  15.6 14.4 %collective-permute-start.7 = (f32[33,1024]{1,0:T(8,128)S(1)}, f32[33,1024]{1,0:T(8,128)S(1)}, u32[]{:S(2)}, u32[]{:S(2)}) collective-permute-start(f32[33,1024]{1,0:T(8,128)S(1)} %get-tuple-element.80.refs_2_), channel_id=1, source_target_pairs={{0,16},{4,20},{8,24},{12,28},{16,0},{20,4},{24,8},{28,12},{1,17},{... | collective-permute-start | bytes 405512 | tf_op jit(solution)/shard_map/ppermute | solution.py:42
  23.6 6.4 %collective-permute-start.6 = (f32[17,8,128]{2,1,0:T(8,128)S(1)}, f32[17,8,128]{2,1,0:T(8,128)S(1)}, u32[]{:S(2)}, u32[]{:S(2)}) collective-permute-start(f32[17,8,128]{2,1,0:T(8,128)S(1)} %add_add_fusion.5.refs_0_), channel_id=1, source_target_pairs={{0,16},{4,20},{8,24},{12,28},{16,0},{20,4},{24,8},{28,12},{1,17},{... | collective-permute-start | bytes 208904 | tf_op jit(solution)/shard_map/ppermute | solution.py:42
  28.8 6.1 %collective-permute-start.34 = (f32[17,8,128]{2,1,0:T(8,128)S(1)}, f32[17,8,128]{2,1,0:T(8,128)S(1)}, u32[]{:S(2)}, u32[]{:S(2)}) collective-permute-start(f32[17,8,128]{2,1,0:T(8,128)S(1)} %add_add_fusion.2.refs_0_), channel_id=1, source_target_pairs={{0,16},{4,20},{8,24},{12,28},{16,0},{20,4},{24,8},{28,12},{1,17},{... | collective-permute-start | bytes 208904 | tf_op jit(solution)/shard_map/ppermute | solution.py:42
  30.1 7.0 %collective-permute-start.10 = (f32[17,8,128]{2,1,0:T(8,128)S(1)}, f32[17,8,128]{2,1,0:T(8,128)S(1)}, u32[]{:S(2)}, u32[]{:S(2)}) collective-permute-start(f32[17,8,128]{2,1,0:T(8,128)S(1)} %get-tuple-element.81.refs_0_), channel_id=1, source_target_pairs={{0,12},{4,8},{8,4},{12,0},{16,28},{20,24},{24,20},{28,16},{1,13},{... | collective-permute-start | bytes 208904 | tf_op jit(solution)/shard_map/ppermute | solution.py:42
  33.7 8.8 %collective-permute-start.12 = (f32[16,1024]{1,0:T(8,128)S(1)}, f32[16,1024]{1,0:T(8,128)S(1)}, u32[]{:S(2)}, u32[]{:S(2)}) collective-permute-start(f32[16,1024]{1,0:T(8,128)S(1)} %bitcast.34), channel_id=1, source_target_pairs={{0,4},{4,8},{8,12},{12,16},{16,20},{20,24},{24,28},{28,0},{1,5},{5... | collective-permute-start | bytes 196616 | tf_op jit(solution)/shard_map/ppermute | solution.py:47
  34.9 7.7 %collective-permute-start.13 = (f32[16,1024]{1,0:T(8,128)S(1)}, f32[16,1024]{1,0:T(8,128)S(1)}, u32[]{:S(2)}, u32[]{:S(2)}) collective-permute-start(f32[16,1024]{1,0:T(8,128)S(1)} %bitcast.35), channel_id=1, source_target_pairs={{0,8},{4,12},{8,16},{12,20},{16,24},{20,28},{24,0},{28,4},{1,9},{5... | collective-permute-start | bytes 196616 | tf_op jit(solution)/shard_map/ppermute | solution.py:47
  37.1 11.9 %collective-permute-start.35 = (f32[17,8,128]{2,1,0:T(8,128)S(1)}, f32[17,8,128]{2,1,0:T(8,128)S(1)}, u32[]{:S(2)}, u32[]{:S(2)}) collective-permute-start(f32[17,8,128]{2,1,0:T(8,128)S(1)} %get-tuple-element.108.refs_0_), channel_id=1, source_target_pairs={{0,4},{4,0},{8,12},{12,8},{16,20},{20,16},{24,28},{28,24},{1,5},{5... | collective-permute-start | bytes 208904 | tf_op jit(solution)/shard_map/ppermute | solution.py:42
  38.6 10.3 %collective-permute-start.36 = (f32[17,8,128]{2,1,0:T(8,128)S(1)}, f32[17,8,128]{2,1,0:T(8,128)S(1)}, u32[]{:S(2)}, u32[]{:S(2)}) collective-permute-start(f32[17,8,128]{2,1,0:T(8,128)S(1)} %get-tuple-element.108.refs_0_), channel_id=1, source_target_pairs={{0,8},{4,12},{8,0},{12,4},{16,24},{20,28},{24,16},{28,20},{1,9},{5... | collective-permute-start | bytes 208904 | tf_op jit(solution)/shard_map/ppermute | solution.py:42
  39.3 9.7 %collective-permute-start.37 = (f32[17,8,128]{2,1,0:T(8,128)S(1)}, f32[17,8,128]{2,1,0:T(8,128)S(1)}, u32[]{:S(2)}, u32[]{:S(2)}) collective-permute-start(f32[17,8,128]{2,1,0:T(8,128)S(1)} %get-tuple-element.108.refs_0_), channel_id=1, source_target_pairs={{0,12},{4,8},{8,4},{12,0},{16,28},{20,24},{24,20},{28,16},{1,13},{... | collective-permute-start | bytes 208904 | tf_op jit(solution)/shard_map/ppermute | solution.py:42
  42.5 8.4 %collective-permute-start.11 = (f32[17,8,128]{2,1,0:T(8,128)S(1)}, f32[17,8,128]{2,1,0:T(8,128)S(1)}, u32[]{:S(2)}, u32[]{:S(2)}) collective-permute-start(f32[17,8,128]{2,1,0:T(8,128)S(1)} %get-tuple-element.83), channel_id=1, source_target_pairs={{0,1},{1,0},{2,3},{3,2},{4,5},{5,4},{6,7},{7,6},{8,9},{9,8},{10,11... | collective-permute-start | bytes 208904 | tf_op jit(solution)/shard_map/ppermute | solution.py:42
  42.6 6.3 %collective-permute-start.14 = (f32[16,1024]{1,0:T(8,128)S(1)}, f32[16,1024]{1,0:T(8,128)S(1)}, u32[]{:S(2)}, u32[]{:S(2)}) collective-permute-start(f32[16,1024]{1,0:T(8,128)S(1)} %bitcast.36), channel_id=1, source_target_pairs={{0,12},{4,16},{8,20},{12,24},{16,28},{20,0},{24,4},{28,8},{1,13},{... | collective-permute-start | bytes 196616 | tf_op jit(solution)/shard_map/ppermute | solution.py:47
  57.1 6.1 %collective-permute-start.40 = (f32[17,8,128]{2,1,0:T(8,128)S(1)}, f32[17,8,128]{2,1,0:T(8,128)S(1)}, u32[]{:S(2)}, u32[]{:S(2)}) collective-permute-start(f32[17,8,128]{2,1,0:T(8,128)S(1)} %get-tuple-element.112.refs_0_.refs_3_), channel_id=1, source_target_pairs={{0,1},{1,0},{2,3},{3,2},{4,5},{5,4},{6,7},{7,6},{8,9},{9,8},{10,11... | collective-permute-start | bytes 208904 | tf_op jit(solution)/shard_map/ppermute | solution.py:42
  59.3 8.0 %collective-permute-start.17 = (f32[17,8,128]{2,1,0:T(8,128)S(1)}, f32[17,8,128]{2,1,0:T(8,128)S(1)}, u32[]{:S(2)}, u32[]{:S(2)}) collective-permute-start(f32[17,8,128]{2,1,0:T(8,128)S(1)} %get-tuple-element.87), channel_id=1, source_target_pairs={{0,4},{4,0},{8,12},{12,8},{16,20},{20,16},{24,28},{28,24},{1,5},{5... | collective-permute-start | bytes 208904 | tf_op jit(solution)/shard_map/ppermute | solution.py:42
  61.7 6.9 %collective-permute-start.18 = (f32[17,8,128]{2,1,0:T(8,128)S(1)}, f32[17,8,128]{2,1,0:T(8,128)S(1)}, u32[]{:S(2)}, u32[]{:S(2)}) collective-permute-start(f32[17,8,128]{2,1,0:T(8,128)S(1)} %get-tuple-element.88), channel_id=1, source_target_pairs={{0,8},{4,12},{8,0},{12,4},{16,24},{20,28},{24,16},{28,20},{1,9},{5... | collective-permute-start | bytes 208904 | tf_op jit(solution)/shard_map/ppermute | solution.py:42
  61.8 6.8 %collective-permute-start.19 = (f32[17,8,128]{2,1,0:T(8,128)S(1)}, f32[17,8,128]{2,1,0:T(8,128)S(1)}, u32[]{:S(2)}, u32[]{:S(2)}) collective-permute-start(f32[17,8,128]{2,1,0:T(8,128)S(1)} %get-tuple-element.89), channel_id=1, source_target_pairs={{0,12},{4,8},{8,4},{12,0},{16,28},{20,24},{24,20},{28,16},{1,13},{... | collective-permute-start | bytes 208904 | tf_op jit(solution)/shard_map/ppermute | solution.py:42
  68.7 5.9 %collective-permute-start.20 = (f32[17,8,128]{2,1,0:T(8,128)S(1)}, f32[17,8,128]{2,1,0:T(8,128)S(1)}, u32[]{:S(2)}, u32[]{:S(2)}) collective-permute-start(f32[17,8,128]{2,1,0:T(8,128)S(1)} %add_add_fusion.4.refs_0_), channel_id=1, source_target_pairs={{0,16},{4,20},{8,24},{12,28},{16,0},{20,4},{24,8},{28,12},{1,17},{... | collective-permute-start | bytes 208904 | tf_op jit(solution)/shard_map/ppermute | solution.py:42
  72.7 6.5 %collective-permute-start.44 = (f32[17,8,128]{2,1,0:T(8,128)S(1)}, f32[17,8,128]{2,1,0:T(8,128)S(1)}, u32[]{:S(2)}, u32[]{:S(2)}) collective-permute-start(f32[17,8,128]{2,1,0:T(8,128)S(1)} %add_add_fusion.1.refs_0_), channel_id=1, source_target_pairs={{0,16},{4,20},{8,24},{12,28},{16,0},{20,4},{24,8},{28,12},{1,17},{... | collective-permute-start | bytes 208904 | tf_op jit(solution)/shard_map/ppermute | solution.py:42
  74.7 6.6 %collective-permute-start.21 = (f32[17,8,128]{2,1,0:T(8,128)S(1)}, f32[17,8,128]{2,1,0:T(8,128)S(1)}, u32[]{:S(2)}, u32[]{:S(2)}) collective-permute-start(f32[17,8,128]{2,1,0:T(8,128)S(1)} %get-tuple-element.92.refs_0_), channel_id=1, source_target_pairs={{0,4},{4,0},{8,12},{12,8},{16,20},{20,16},{24,28},{28,24},{1,5},{5... | collective-permute-start | bytes 208904 | tf_op jit(solution)/shard_map/ppermute | solution.py:42
  77.6 5.9 %collective-permute-start.23 = (f32[17,8,128]{2,1,0:T(8,128)S(1)}, f32[17,8,128]{2,1,0:T(8,128)S(1)}, u32[]{:S(2)}, u32[]{:S(2)}) collective-permute-start(f32[17,8,128]{2,1,0:T(8,128)S(1)} %get-tuple-element.92.refs_0_), channel_id=1, source_target_pairs={{0,12},{4,8},{8,4},{12,0},{16,28},{20,24},{24,20},{28,16},{1,13},{... | collective-permute-start | bytes 208904 | tf_op jit(solution)/shard_map/ppermute | solution.py:42
  79.3 6.2 %collective-permute-start.45 = (f32[17,8,128]{2,1,0:T(8,128)S(1)}, f32[17,8,128]{2,1,0:T(8,128)S(1)}, u32[]{:S(2)}, u32[]{:S(2)}) collective-permute-start(f32[17,8,128]{2,1,0:T(8,128)S(1)} %get-tuple-element.119.refs_0_), channel_id=1, source_target_pairs={{0,4},{4,0},{8,12},{12,8},{16,20},{20,16},{24,28},{28,24},{1,5},{5... | collective-permute-start | bytes 208904 | tf_op jit(solution)/shard_map/ppermute | solution.py:42
  96.8 7.6 %collective-permute-start.27 = (f32[17,8,128]{2,1,0:T(8,128)S(1)}, f32[17,8,128]{2,1,0:T(8,128)S(1)}, u32[]{:S(2)}, u32[]{:S(2)}) collective-permute-start(f32[17,8,128]{2,1,0:T(8,128)S(1)} %get-tuple-element.98), channel_id=1, source_target_pairs={{0,4},{4,0},{8,12},{12,8},{16,20},{20,16},{24,28},{28,24},{1,5},{5... | collective-permute-start | bytes 208904 | tf_op jit(solution)/shard_map/ppermute | solution.py:42
  98.1 7.6 %collective-permute-start.28 = (f32[17,8,128]{2,1,0:T(8,128)S(1)}, f32[17,8,128]{2,1,0:T(8,128)S(1)}, u32[]{:S(2)}, u32[]{:S(2)}) collective-permute-start(f32[17,8,128]{2,1,0:T(8,128)S(1)} %get-tuple-element.99), channel_id=1, source_target_pairs={{0,8},{4,12},{8,0},{12,4},{16,24},{20,28},{24,16},{28,20},{1,9},{5... | collective-permute-start | bytes 208904 | tf_op jit(solution)/shard_map/ppermute | solution.py:42
  99.0 6.8 %collective-permute-start.29 = (f32[17,8,128]{2,1,0:T(8,128)S(1)}, f32[17,8,128]{2,1,0:T(8,128)S(1)}, u32[]{:S(2)}, u32[]{:S(2)}) collective-permute-start(f32[17,8,128]{2,1,0:T(8,128)S(1)} %get-tuple-element.100), channel_id=1, source_target_pairs={{0,12},{4,8},{8,4},{12,0},{16,28},{20,24},{24,20},{28,16},{1,13},{... | collective-permute-start | bytes 208904 | tf_op jit(solution)/shard_map/ppermute | solution.py:42
  104.4 5.8 %collective-permute-start.53 = (f32[17,8,128]{2,1,0:T(8,128)S(1)}, f32[17,8,128]{2,1,0:T(8,128)S(1)}, u32[]{:S(2)}, u32[]{:S(2)}) collective-permute-start(f32[17,8,128]{2,1,0:T(8,128)S(1)} %get-tuple-element.127), channel_id=1, source_target_pairs={{0,12},{4,8},{8,4},{12,0},{16,28},{20,24},{24,20},{28,16},{1,13},{... | collective-permute-start | bytes 208904 | tf_op jit(solution)/shard_map/ppermute | solution.py:42
  105.8 6.1 %collective-permute-start.30 = (f32[17,8,128]{2,1,0:T(8,128)S(1)}, f32[17,8,128]{2,1,0:T(8,128)S(1)}, u32[]{:S(2)}, u32[]{:S(2)}) collective-permute-start(f32[17,8,128]{2,1,0:T(8,128)S(1)} %add_add_fusion.3.refs_0_), channel_id=1, source_target_pairs={{0,16},{4,20},{8,24},{12,28},{16,0},{20,4},{24,8},{28,12},{1,17},{... | collective-permute-start | bytes 208904 | tf_op jit(solution)/shard_map/ppermute | solution.py:42
  110.2 5.9 %collective-permute-start.54 = (f32[17,8,128]{2,1,0:T(8,128)S(1)}, f32[17,8,128]{2,1,0:T(8,128)S(1)}, u32[]{:S(2)}, u32[]{:S(2)}) collective-permute-start(f32[17,8,128]{2,1,0:T(8,128)S(1)} %add_add_fusion.refs_0_), channel_id=1, source_target_pairs={{0,16},{4,20},{8,24},{12,28},{16,0},{20,4},{24,8},{28,12},{1,17},{... | collective-permute-start | bytes 208904 | tf_op jit(solution)/shard_map/ppermute | solution.py:42
  112.0 6.4 %collective-permute-start.55 = (f32[17,8,128]{2,1,0:T(8,128)S(1)}, f32[17,8,128]{2,1,0:T(8,128)S(1)}, u32[]{:S(2)}, u32[]{:S(2)}) collective-permute-start(f32[17,8,128]{2,1,0:T(8,128)S(1)} %get-tuple-element.131.refs_0_), channel_id=1, source_target_pairs={{0,4},{4,0},{8,12},{12,8},{16,20},{20,16},{24,28},{28,24},{1,5},{5... | collective-permute-start | bytes 208904 | tf_op jit(solution)/shard_map/ppermute | solution.py:42
  114.0 5.8 %collective-permute-start.56 = (f32[17,8,128]{2,1,0:T(8,128)S(1)}, f32[17,8,128]{2,1,0:T(8,128)S(1)}, u32[]{:S(2)}, u32[]{:S(2)}) collective-permute-start(f32[17,8,128]{2,1,0:T(8,128)S(1)} %get-tuple-element.131.refs_0_), channel_id=1, source_target_pairs={{0,8},{4,12},{8,0},{12,4},{16,24},{20,28},{24,16},{28,20},{1,9},{5... | collective-permute-start | bytes 208904 | tf_op jit(solution)/shard_map/ppermute | solution.py:42
  (42 other events, 248.9 us)

commit v7 on v6

--- a/solution.py
+++ b/solution.py
@@ -11,7 +11,7 @@
 ITERS = 3
 LEAD_MAX = 4
 GROUP = 128
-PIECE = 8
+PIECE = 16
 AHEAD = 16
 STREAMS = 2
 KERNEL_VMEM = 1 << 20
@@ -473,7 +473,8 @@
     square = joined("square")
     cols = lax.axis_size("col")
     square = summed(square, ("band", "col"), [square] * 3, (1, cols, cols + 1))
-    for bit in range(1, band_bits):
+    square = summed(square, "band", [square] * 3, (2, 4, 6))
+    for bit in range(3, band_bits):
         square = square + exchanged(square, "band", 1 << bit)
     weight = next_weight(joined("weight"), joined("primal_square"), square)[:, 0]
     return (joined("primal_rows").T, joined("dual_rows").T, weight)

time: 145 us -> 145 us (level)
  waiting for transfers between devices: 40.9 us -> 39.4 us
    ppermute x67 -> x68, waiting for transfers between devices: 36.4 us -> 34.9 us  [exchanged(): lax.ppermute(value, axis, [(source, source ^ mask) for source in range(co...]
    ppermute x67 -> x68, starting transfers between devices: 67.4 us -> 68.8 us  [exchanged(): lax.ppermute(value, axis, [(source, source ^ mask) for source in range(co...]
  transfers between devices with their start and end apart: 70 -> 71, of which waited for: 31 -> 31; matrix products, arithmetic and copies ran while one was open for 2% -> 2% of each run, Pallas kernels for 18% -> 17%
where the time goes in v7:
time: 145 us
  starting transfers between devices  73.9 us (51%)
  waiting for transfers between devices  39.4 us (27%)
  Pallas kernels  26.9 us (19%)
  other arithmetic  3.12 us (2%)
    ppermute x68, starting transfers between devices, exchanged(): lax.ppermute(value, axis, [(source, source ^ mask) for source in range(co...  68.8 us
    ppermute x68, waiting for transfers between devices, exchanged(): lax.ppermute(value, axis, [(source, source ^ mask) for source in range(co...  34.9 us
    pallas_call x25, Pallas kernels, call_in_vmem(): pl.pallas_call(body, out_shape=[pltpu.VMEM(shape, F32) for shape in outpu...  22.9 us
    ppermute x3, starting transfers between devices, passed_along(): lax.ppermute(value, axis, [(source, (source + steps) % count) for source...  5.06 us
    ppermute x3, waiting for transfers between devices, passed_along(): lax.ppermute(value, axis, [(source, (source + steps) % count) for source...  4.52 us
    pallas_call x1, Pallas kernels, prepared(): pl.pallas_call(body, out_shape=[pltpu.VMEM((count, 2 * tile, tile), BF16)...  3.98 us
  transfers between devices with their start and end apart: 71, of which 31 were waited for; matrix products, arithmetic and copies ran while one was open for 2% of the time, Pallas kernels for 17%

profile of v7, /device:TPU:0, one launch (start us, length us, event | category | flops | bytes accessed | tf_op | source)
XLA Modules:
  0.0 144.6 jit_solution(16631563484143119410)
XLA Ops:
  0.6 3.0 %collective-permute-start = (f32[16,1024]{1,0:T(8,128)}, f32[16,1024]{1,0:T(8,128)S(1)}, u32[]{:S(2)}, u32[]{:S(2)}) collective-permute-start(f32[16,1024]{1,0:T(8,128)} %bitcast.27), channel_id=1, source_target_pairs={{0,2},{1,3},{2,0},{3,1},{4,6},{5,7},{6,4},{7,5},{8,10},{9,11},{10,... | collective-permute-start | bytes 196616 | tf_op jit(solution)/shard_map/ppermute | solution.py:42
  4.4 4.0 %shard_map.103 = (bf16[128,256,128]{2,1,0:T(8,128)(2,1)S(1)}, bf16[128,256,128]{2,1,0:T(8,128)(2,1)S(1)}, f32[33,1024]{1,0:T(8,128)S(1)}) custom-call(f32[128,128,128]{2,1,0:T(8,128)} %bitcast.39, f32[16,1024]{1,0:T(8,128)} %bitcast.40, f32[16,1024]{1,0:T(8,128)} %bitcast.33, f32[1,1024]{1,0:T(1,128)} %bitcast.41), custom_call_target="tpu_custom_call" | custom-call | tf_op jit(solution)/shard_map/pallas_call | solution.py:139
  9.8 1.8 %shard_map.104 = (f32[17,8,128]{2,1,0:T(8,128)S(1)}, f32[17,8,128]{2,1,0:T(8,128)S(1)}, f32[17,8,128]{2,1,0:T(8,128)S(1)}, f32[17,8,128]{2,1,0:T(8,128)S(1)}) custom-call(s32[256]{0:T(256)S(1)} %pad_add_fusion.index_ref, bf16[128,256,128]{2,1,0:T(8,128)(2,1)S(1)} %get-tuple-element.74.tiles_ref, f32[16,1024]{1,0:T(8,128)S(1)} %bitcast.29, ...), custom_call_target="tpu_custom_call" | custom-call | tf_op jit(solution)/shard_map/pallas_call | solution.py:71
  15.2 2.6 %collective-permute-start.7 = (f32[33,1024]{1,0:T(8,128)S(1)}, f32[33,1024]{1,0:T(8,128)S(1)}, u32[]{:S(2)}, u32[]{:S(2)}) collective-permute-start(f32[33,1024]{1,0:T(8,128)S(1)} %get-tuple-element.80.refs_2_), channel_id=1, source_target_pairs={{0,16},{4,20},{8,24},{12,28},{16,0},{20,4},{24,8},{28,12},{1,17},{... | collective-permute-start | bytes 405512 | tf_op jit(solution)/shard_map/ppermute | solution.py:42
  17.8 1.8 %shard_map.115 = (f32[17,8,128]{2,1,0:T(8,128)S(1)}, f32[17,8,128]{2,1,0:T(8,128)S(1)}, f32[17,8,128]{2,1,0:T(8,128)S(1)}, f32[17,8,128]{2,1,0:T(8,128)S(1)}) custom-call(s32[256]{0:T(256)S(1)} %pad_add_fusion.index_ref, bf16[128,256,128]{2,1,0:T(8,128)(2,1)S(1)} %get-tuple-element.74.tiles_ref, f32[16,1024]{1,0:T(8,128)S(1)} %bitcast.30, ...), custom_call_target="tpu_custom_call" | custom-call | tf_op jit(solution)/shard_map/pallas_call | solution.py:71
  24.0 2.8 %collective-permute-done.32 = f32[17,8,128]{2,1,0:T(8,128)S(1)} collective-permute-done((f32[17,8,128]{2,1,0:T(8,128)S(1)}, f32[17,8,128]{2,1,0:T(8,128)S(1)}, u32[]{:S(2)}, u32[]{:S(2)}) %collective-permute-start.32) | collective-permute-done | bytes 69664 | tf_op jit(solution)/shard_map/ppermute | solution.py:42
  29.7 2.8 %collective-permute-start.10 = (f32[17,8,128]{2,1,0:T(8,128)S(1)}, f32[17,8,128]{2,1,0:T(8,128)S(1)}, u32[]{:S(2)}, u32[]{:S(2)}) collective-permute-start(f32[17,8,128]{2,1,0:T(8,128)S(1)} %get-tuple-element.81.refs_0_), channel_id=1, source_target_pairs={{0,12},{4,8},{8,4},{12,0},{16,28},{20,24},{24,20},{28,16},{1,13},{... | collective-permute-start | bytes 208904 | tf_op jit(solution)/shard_map/ppermute | solution.py:42
  34.5 2.0 %collective-permute-start.13 = (f32[16,1024]{1,0:T(8,128)S(1)}, f32[16,1024]{1,0:T(8,128)S(1)}, u32[]{:S(2)}, u32[]{:S(2)}) collective-permute-start(f32[16,1024]{1,0:T(8,128)S(1)} %bitcast.35), channel_id=1, source_target_pairs={{0,8},{4,12},{8,16},{12,20},{16,24},{20,28},{24,0},{28,4},{1,9},{5... | collective-permute-start | bytes 196616 | tf_op jit(solution)/shard_map/ppermute | solution.py:47
  40.2 1.9 %shard_map.106 = (f32[17,8,128]{2,1,0:T(8,128)S(1)}, f32[17,8,128]{2,1,0:T(8,128)S(1)}) custom-call(s32[256]{0:T(256)S(1)} %pad_add_fusion.index_ref, bf16[128,256,128]{2,1,0:T(8,128)(2,1)S(1)} %get-tuple-element.75.tiles_ref, f32[17,8,128]{2,1,0:T(8,128)S(1)} %get-tuple-element.81.refs_0_, f32[17,8,128]{2,1,0:T(8,128)S(1)} %collective-permute-done.8.refs_1_, ...), custom_call_target="tpu_custom_call" | custom-call | tf_op jit(solution)/shard_map/pallas_call | solution.py:71
  42.2 1.8 %collective-permute-start.14 = (f32[16,1024]{1,0:T(8,128)S(1)}, f32[16,1024]{1,0:T(8,128)S(1)}, u32[]{:S(2)}, u32[]{:S(2)}) collective-permute-start(f32[16,1024]{1,0:T(8,128)S(1)} %bitcast.36), channel_id=1, source_target_pairs={{0,12},{4,16},{8,20},{12,24},{16,28},{20,0},{24,4},{28,8},{1,13},{... | collective-permute-start | bytes 196616 | tf_op jit(solution)/shard_map/ppermute | solution.py:47
  44.0 4.5 %collective-permute-done.14.refs_2_ = f32[16,1024]{1,0:T(8,128)S(1)} collective-permute-done((f32[16,1024]{1,0:T(8,128)S(1)}, f32[16,1024]{1,0:T(8,128)S(1)}, u32[]{:S(2)}, u32[]{:S(2)}) %collective-permute-start.14) | collective-permute-done | bytes 65568 | tf_op jit(solution)/shard_map/ppermute | solution.py:47
  48.6 1.9 %shard_map.117 = (f32[17,8,128]{2,1,0:T(8,128)S(1)}, f32[17,8,128]{2,1,0:T(8,128)S(1)}) custom-call(s32[256]{0:T(256)S(1)} %pad_add_fusion.index_ref, bf16[128,256,128]{2,1,0:T(8,128)(2,1)S(1)} %get-tuple-element.75.tiles_ref, f32[17,8,128]{2,1,0:T(8,128)S(1)} %get-tuple-element.108.refs_0_, f32[17,8,128]{2,1,0:T(8,128)S(1)} %collective-permute-done.35.refs_1_, ...), custom_call_target="tpu_custom_call" | custom-call | tf_op jit(solution)/shard_map/pallas_call | solution.py:71
  52.8 2.9 %collective-permute-done.15.refs_1_ = f32[17,8,128]{2,1,0:T(8,128)S(1)} collective-permute-done((f32[17,8,128]{2,1,0:T(8,128)S(1)}, f32[17,8,128]{2,1,0:T(8,128)S(1)}, u32[]{:S(2)}, u32[]{:S(2)}) %collective-permute-start.15) | collective-permute-done | bytes 69664 | tf_op jit(solution)/shard_map/ppermute | solution.py:42
  57.0 1.8 %shard_map.109 = (f32[17,8,128]{2,1,0:T(8,128)S(1)}, f32[17,8,128]{2,1,0:T(8,128)S(1)}, f32[17,8,128]{2,1,0:T(8,128)S(1)}, f32[17,8,128]{2,1,0:T(8,128)S(1)}) custom-call(s32[256]{0:T(256)S(1)} %pad_add_fusion.index_ref, bf16[128,256,128]{2,1,0:T(8,128)(2,1)S(1)} %get-tuple-element.74.tiles_ref, f32[17,8,128]{2,1,0:T(8,128)S(1)} %get-tuple-element.85.refs_0_.refs_3_, ...), custom_call_target="tpu_custom_call" | custom-call | tf_op jit(solution)/shard_map/pallas_call | solution.py:71
  58.9 2.4 %collective-permute-start.17 = (f32[17,8,128]{2,1,0:T(8,128)S(1)}, f32[17,8,128]{2,1,0:T(8,128)S(1)}, u32[]{:S(2)}, u32[]{:S(2)}) collective-permute-start(f32[17,8,128]{2,1,0:T(8,128)S(1)} %get-tuple-element.87), channel_id=1, source_target_pairs={{0,4},{4,0},{8,12},{12,8},{16,20},{20,16},{24,28},{28,24},{1,5},{5... | collective-permute-start | bytes 208904 | tf_op jit(solution)/shard_map/ppermute | solution.py:42
  62.9 1.8 %shard_map.119 = (f32[17,8,128]{2,1,0:T(8,128)S(1)}, f32[17,8,128]{2,1,0:T(8,128)S(1)}, f32[17,8,128]{2,1,0:T(8,128)S(1)}, f32[17,8,128]{2,1,0:T(8,128)S(1)}) custom-call(s32[256]{0:T(256)S(1)} %pad_add_fusion.index_ref, bf16[128,256,128]{2,1,0:T(8,128)(2,1)S(1)} %get-tuple-element.74.tiles_ref, f32[17,8,128]{2,1,0:T(8,128)S(1)} %get-tuple-element.112.refs_0_.refs_3_, ...), custom_call_target="tpu_custom_call" | custom-call | tf_op jit(solution)/shard_map/pallas_call | solution.py:71
  64.7 2.0 %collective-permute-start.41 = (f32[17,8,128]{2,1,0:T(8,128)S(1)}, f32[17,8,128]{2,1,0:T(8,128)S(1)}, u32[]{:S(2)}, u32[]{:S(2)}) collective-permute-start(f32[17,8,128]{2,1,0:T(8,128)S(1)} %get-tuple-element.114), channel_id=1, source_target_pairs={{0,4},{4,0},{8,12},{12,8},{16,20},{20,16},{24,28},{28,24},{1,5},{5... | collective-permute-start | bytes 208904 | tf_op jit(solution)/shard_map/ppermute | solution.py:42
  70.0 2.0 %collective-permute-done.42 = f32[17,8,128]{2,1,0:T(8,128)S(1)} collective-permute-done((f32[17,8,128]{2,1,0:T(8,128)S(1)}, f32[17,8,128]{2,1,0:T(8,128)S(1)}, u32[]{:S(2)}, u32[]{:S(2)}) %collective-permute-start.42) | collective-permute-done | bytes 69664 | tf_op jit(solution)/shard_map/ppermute | solution.py:42
  72.3 1.8 %collective-permute-start.44 = (f32[17,8,128]{2,1,0:T(8,128)S(1)}, f32[17,8,128]{2,1,0:T(8,128)S(1)}, u32[]{:S(2)}, u32[]{:S(2)}) collective-permute-start(f32[17,8,128]{2,1,0:T(8,128)S(1)} %add_add_fusion.1.refs_0_), channel_id=1, source_target_pairs={{0,16},{4,20},{8,24},{12,28},{16,0},{20,4},{24,8},{28,12},{1,17},{... | collective-permute-start | bytes 208904 | tf_op jit(solution)/shard_map/ppermute | solution.py:42
  74.3 2.9 %collective-permute-start.21 = (f32[17,8,128]{2,1,0:T(8,128)S(1)}, f32[17,8,128]{2,1,0:T(8,128)S(1)}, u32[]{:S(2)}, u32[]{:S(2)}) collective-permute-start(f32[17,8,128]{2,1,0:T(8,128)S(1)} %get-tuple-element.92.refs_0_), channel_id=1, source_target_pairs={{0,4},{4,0},{8,12},{12,8},{16,20},{20,16},{24,28},{28,24},{1,5},{5... | collective-permute-start | bytes 208904 | tf_op jit(solution)/shard_map/ppermute | solution.py:42
  78.9 2.0 %collective-permute-start.45 = (f32[17,8,128]{2,1,0:T(8,128)S(1)}, f32[17,8,128]{2,1,0:T(8,128)S(1)}, u32[]{:S(2)}, u32[]{:S(2)}) collective-permute-start(f32[17,8,128]{2,1,0:T(8,128)S(1)} %get-tuple-element.119.refs_0_), channel_id=1, source_target_pairs={{0,4},{4,0},{8,12},{12,8},{16,20},{20,16},{24,28},{28,24},{1,5},{5... | collective-permute-start | bytes 208904 | tf_op jit(solution)/shard_map/ppermute | solution.py:42
  83.1 1.9 %shard_map.111 = (f32[17,8,128]{2,1,0:T(8,128)S(1)}, f32[17,8,128]{2,1,0:T(8,128)S(1)}) custom-call(s32[256]{0:T(256)S(1)} %pad_add_fusion.index_ref, bf16[128,256,128]{2,1,0:T(8,128)(2,1)S(1)} %get-tuple-element.75.tiles_ref, f32[17,8,128]{2,1,0:T(8,128)S(1)} %get-tuple-element.92.refs_0_, f32[17,8,128]{2,1,0:T(8,128)S(1)} %collective-permute-done.21.refs_1_, ...), custom_call_target="tpu_custom_call" | custom-call | tf_op jit(solution)/shard_map/pallas_call | solution.py:71
  86.1 1.9 %shard_map.121 = (f32[17,8,128]{2,1,0:T(8,128)S(1)}, f32[17,8,128]{2,1,0:T(8,128)S(1)}) custom-call(s32[256]{0:T(256)S(1)} %pad_add_fusion.index_ref, bf16[128,256,128]{2,1,0:T(8,128)(2,1)S(1)} %get-tuple-element.75.tiles_ref, f32[17,8,128]{2,1,0:T(8,128)S(1)} %get-tuple-element.119.refs_0_, f32[17,8,128]{2,1,0:T(8,128)S(1)} %collective-permute-done.45.refs_1_, ...), custom_call_target="tpu_custom_call" | custom-call | tf_op jit(solution)/shard_map/pallas_call | solution.py:71
  90.3 2.9 %collective-permute-done.25.refs_1_ = f32[17,8,128]{2,1,0:T(8,128)S(1)} collective-permute-done((f32[17,8,128]{2,1,0:T(8,128)S(1)}, f32[17,8,128]{2,1,0:T(8,128)S(1)}, u32[]{:S(2)}, u32[]{:S(2)}) %collective-permute-start.25) | collective-permute-done | bytes 69664 | tf_op jit(solution)/shard_map/ppermute | solution.py:42
  94.6 1.8 %shard_map.113 = (f32[17,8,128]{2,1,0:T(8,128)S(1)}, f32[17,8,128]{2,1,0:T(8,128)S(1)}, f32[17,8,128]{2,1,0:T(8,128)S(1)}, f32[17,8,128]{2,1,0:T(8,128)S(1)}) custom-call(s32[256]{0:T(256)S(1)} %pad_add_fusion.index_ref, bf16[128,256,128]{2,1,0:T(8,128)(2,1)S(1)} %get-tuple-element.74.tiles_ref, f32[17,8,128]{2,1,0:T(8,128)S(1)} %get-tuple-element.96.refs_0_.refs_3_, ...), custom_call_target="tpu_custom_call" | custom-call | tf_op jit(solution)/shard_map/pallas_call | solution.py:71
  100.0 1.8 %shard_map.123 = (f32[17,8,128]{2,1,0:T(8,128)S(1)}, f32[17,8,128]{2,1,0:T(8,128)S(1)}, f32[17,8,128]{2,1,0:T(8,128)S(1)}, f32[17,8,128]{2,1,0:T(8,128)S(1)}) custom-call(s32[256]{0:T(256)S(1)} %pad_add_fusion.index_ref, bf16[128,256,128]{2,1,0:T(8,128)(2,1)S(1)} %get-tuple-element.74.tiles_ref, f32[17,8,128]{2,1,0:T(8,128)S(1)} %get-tuple-element.123.refs_0_.refs_3_, ...), custom_call_target="tpu_custom_call" | custom-call | tf_op jit(solution)/shard_map/pallas_call | solution.py:71
  105.4 2.0 %collective-permute-start.30 = (f32[17,8,128]{2,1,0:T(8,128)S(1)}, f32[17,8,128]{2,1,0:T(8,128)S(1)}, u32[]{:S(2)}, u32[]{:S(2)}) collective-permute-start(f32[17,8,128]{2,1,0:T(8,128)S(1)} %add_add_fusion.3.refs_0_), channel_id=1, source_target_pairs={{0,16},{4,20},{8,24},{12,28},{16,0},{20,4},{24,8},{28,12},{1,17},{... | collective-permute-start | bytes 208904 | tf_op jit(solution)/shard_map/ppermute | solution.py:42
  111.6 2.0 %collective-permute-start.55 = (f32[17,8,128]{2,1,0:T(8,128)S(1)}, f32[17,8,128]{2,1,0:T(8,128)S(1)}, u32[]{:S(2)}, u32[]{:S(2)}) collective-permute-start(f32[17,8,128]{2,1,0:T(8,128)S(1)} %get-tuple-element.131.refs_0_), channel_id=1, source_target_pairs={{0,4},{4,0},{8,12},{12,8},{16,20},{20,16},{24,28},{28,24},{1,5},{5... | collective-permute-start | bytes 208904 | tf_op jit(solution)/shard_map/ppermute | solution.py:42
  119.5 1.9 %shard_map.125 = (f32[17,8,128]{2,1,0:T(8,128)S(1)}, f32[17,8,128]{2,1,0:T(8,128)S(1)}) custom-call(s32[256]{0:T(256)S(1)} %pad_add_fusion.index_ref, bf16[128,256,128]{2,1,0:T(8,128)(2,1)S(1)} %get-tuple-element.75.tiles_ref, f32[17,8,128]{2,1,0:T(8,128)S(1)} %get-tuple-element.131.refs_0_, f32[17,8,128]{2,1,0:T(8,128)S(1)} %collective-permute-done.55.refs_1_, ...), custom_call_target="tpu_custom_call" | custom-call | tf_op jit(solution)/shard_map/pallas_call | solution.py:71
  123.3 1.9 %shard_map.127 = (f32[17,8,128]{2,1,0:T(8,128)S(1)}, f32[17,8,128]{2,1,0:T(8,128)S(1)}) custom-call(s32[256]{0:T(256)S(1)} %pad_add_fusion.index_ref, bf16[128,256,128]{2,1,0:T(8,128)(2,1)S(1)} %get-tuple-element.75.tiles_ref, f32[17,8,128]{2,1,0:T(8,128)S(1)} %get-tuple-element.136.refs_0_, f32[17,8,128]{2,1,0:T(8,128)S(1)} %collective-permute-done.60.refs_1_, ...), custom_call_target="tpu_custom_call" | custom-call | tf_op jit(solution)/shard_map/pallas_call | solution.py:71
  127.4 2.9 %collective-permute-done.59.refs_1_ = f32[17,8,128]{2,1,0:T(8,128)S(1)} collective-permute-done((f32[17,8,128]{2,1,0:T(8,128)S(1)}, f32[17,8,128]{2,1,0:T(8,128)S(1)}, u32[]{:S(2)}, u32[]{:S(2)}) %collective-permute-start.59) | collective-permute-done | bytes 69664 | tf_op jit(solution)/shard_map/ppermute | solution.py:42
  141.2 2.6 %collective-permute-done.70 = f32[16,128]{1,0:T(8,128)S(1)} collective-permute-done((f32[16,128]{1,0:T(8,128)S(1)}, f32[16,128]{1,0:T(8,128)S(1)}, u32[]{:S(2)}, u32[]{:S(2)}) %collective-permute-start.70) | collective-permute-done | bytes 8224 | tf_op jit(solution)/shard_map/ppermute | solution.py:42
  (170 shorter events, 69.2 us)
Async XLA Ops:
  0.6 7.7 %collective-permute-start = (f32[16,1024]{1,0:T(8,128)}, f32[16,1024]{1,0:T(8,128)S(1)}, u32[]{:S(2)}, u32[]{:S(2)}) collective-permute-start(f32[16,1024]{1,0:T(8,128)} %bitcast.27), channel_id=1, source_target_pairs={{0,2},{1,3},{2,0},{3,1},{4,6},{5,7},{6,4},{7,5},{8,10},{9,11},{10,... | collective-permute-start | bytes 196616 | tf_op jit(solution)/shard_map/ppermute | solution.py:42
  11.7 9.6 %collective-permute-start.3 = (f32[17,8,128]{2,1,0:T(8,128)S(1)}, f32[17,8,128]{2,1,0:T(8,128)S(1)}, u32[]{:S(2)}, u32[]{:S(2)}) collective-permute-start(f32[17,8,128]{2,1,0:T(8,128)S(1)} %get-tuple-element.77), channel_id=1, source_target_pairs={{0,4},{4,0},{8,12},{12,8},{16,20},{20,16},{24,28},{28,24},{1,5},{5... | collective-permute-start | bytes 208904 | tf_op jit(solution)/shard_map/ppermute | solution.py:42
  13.3 9.6 %collective-permute-start.4 = (f32[17,8,128]{2,1,0:T(8,128)S(1)}, f32[17,8,128]{2,1,0:T(8,128)S(1)}, u32[]{:S(2)}, u32[]{:S(2)}) collective-permute-start(f32[17,8,128]{2,1,0:T(8,128)S(1)} %get-tuple-element.78), channel_id=1, source_target_pairs={{0,8},{4,12},{8,0},{12,4},{16,24},{20,28},{24,16},{28,20},{1,9},{5... | collective-permute-start | bytes 208904 | tf_op jit(solution)/shard_map/ppermute | solution.py:42
  14.8 8.4 %collective-permute-start.5 = (f32[17,8,128]{2,1,0:T(8,128)S(1)}, f32[17,8,128]{2,1,0:T(8,128)S(1)}, u32[]{:S(2)}, u32[]{:S(2)}) collective-permute-start(f32[17,8,128]{2,1,0:T(8,128)S(1)} %get-tuple-element.79), channel_id=1, source_target_pairs={{0,12},{4,8},{8,4},{12,0},{16,28},{20,24},{24,20},{28,16},{1,13},{... | collective-permute-start | bytes 208904 | tf_op jit(solution)/shard_map/ppermute | solution.py:42
  15.2 14.4 %collective-permute-start.7 = (f32[33,1024]{1,0:T(8,128)S(1)}, f32[33,1024]{1,0:T(8,128)S(1)}, u32[]{:S(2)}, u32[]{:S(2)}) collective-permute-start(f32[33,1024]{1,0:T(8,128)S(1)} %get-tuple-element.80.refs_2_), channel_id=1, source_target_pairs={{0,16},{4,20},{8,24},{12,28},{16,0},{20,4},{24,8},{28,12},{1,17},{... | collective-permute-start | bytes 405512 | tf_op jit(solution)/shard_map/ppermute | solution.py:42
  23.2 6.4 %collective-permute-start.6 = (f32[17,8,128]{2,1,0:T(8,128)S(1)}, f32[17,8,128]{2,1,0:T(8,128)S(1)}, u32[]{:S(2)}, u32[]{:S(2)}) collective-permute-start(f32[17,8,128]{2,1,0:T(8,128)S(1)} %add_add_fusion.5.refs_0_), channel_id=1, source_target_pairs={{0,16},{4,20},{8,24},{12,28},{16,0},{20,4},{24,8},{28,12},{1,17},{... | collective-permute-start | bytes 208904 | tf_op jit(solution)/shard_map/ppermute | solution.py:42
  28.4 6.1 %collective-permute-start.34 = (f32[17,8,128]{2,1,0:T(8,128)S(1)}, f32[17,8,128]{2,1,0:T(8,128)S(1)}, u32[]{:S(2)}, u32[]{:S(2)}) collective-permute-start(f32[17,8,128]{2,1,0:T(8,128)S(1)} %add_add_fusion.2.refs_0_), channel_id=1, source_target_pairs={{0,16},{4,20},{8,24},{12,28},{16,0},{20,4},{24,8},{28,12},{1,17},{... | collective-permute-start | bytes 208904 | tf_op jit(solution)/shard_map/ppermute | solution.py:42
  29.7 7.0 %collective-permute-start.10 = (f32[17,8,128]{2,1,0:T(8,128)S(1)}, f32[17,8,128]{2,1,0:T(8,128)S(1)}, u32[]{:S(2)}, u32[]{:S(2)}) collective-permute-start(f32[17,8,128]{2,1,0:T(8,128)S(1)} %get-tuple-element.81.refs_0_), channel_id=1, source_target_pairs={{0,12},{4,8},{8,4},{12,0},{16,28},{20,24},{24,20},{28,16},{1,13},{... | collective-permute-start | bytes 208904 | tf_op jit(solution)/shard_map/ppermute | solution.py:42
  33.3 8.8 %collective-permute-start.12 = (f32[16,1024]{1,0:T(8,128)S(1)}, f32[16,1024]{1,0:T(8,128)S(1)}, u32[]{:S(2)}, u32[]{:S(2)}) collective-permute-start(f32[16,1024]{1,0:T(8,128)S(1)} %bitcast.34), channel_id=1, source_target_pairs={{0,4},{4,8},{8,12},{12,16},{16,20},{20,24},{24,28},{28,0},{1,5},{5... | collective-permute-start | bytes 196616 | tf_op jit(solution)/shard_map/ppermute | solution.py:47
  34.5 7.7 %collective-permute-start.13 = (f32[16,1024]{1,0:T(8,128)S(1)}, f32[16,1024]{1,0:T(8,128)S(1)}, u32[]{:S(2)}, u32[]{:S(2)}) collective-permute-start(f32[16,1024]{1,0:T(8,128)S(1)} %bitcast.35), channel_id=1, source_target_pairs={{0,8},{4,12},{8,16},{12,20},{16,24},{20,28},{24,0},{28,4},{1,9},{5... | collective-permute-start | bytes 196616 | tf_op jit(solution)/shard_map/ppermute | solution.py:47
  36.7 11.9 %collective-permute-start.35 = (f32[17,8,128]{2,1,0:T(8,128)S(1)}, f32[17,8,128]{2,1,0:T(8,128)S(1)}, u32[]{:S(2)}, u32[]{:S(2)}) collective-permute-start(f32[17,8,128]{2,1,0:T(8,128)S(1)} %get-tuple-element.108.refs_0_), channel_id=1, source_target_pairs={{0,4},{4,0},{8,12},{12,8},{16,20},{20,16},{24,28},{28,24},{1,5},{5... | collective-permute-start | bytes 208904 | tf_op jit(solution)/shard_map/ppermute | solution.py:42
  38.2 10.3 %collective-permute-start.36 = (f32[17,8,128]{2,1,0:T(8,128)S(1)}, f32[17,8,128]{2,1,0:T(8,128)S(1)}, u32[]{:S(2)}, u32[]{:S(2)}) collective-permute-start(f32[17,8,128]{2,1,0:T(8,128)S(1)} %get-tuple-element.108.refs_0_), channel_id=1, source_target_pairs={{0,8},{4,12},{8,0},{12,4},{16,24},{20,28},{24,16},{28,20},{1,9},{5... | collective-permute-start | bytes 208904 | tf_op jit(solution)/shard_map/ppermute | solution.py:42
  38.9 9.7 %collective-permute-start.37 = (f32[17,8,128]{2,1,0:T(8,128)S(1)}, f32[17,8,128]{2,1,0:T(8,128)S(1)}, u32[]{:S(2)}, u32[]{:S(2)}) collective-permute-start(f32[17,8,128]{2,1,0:T(8,128)S(1)} %get-tuple-element.108.refs_0_), channel_id=1, source_target_pairs={{0,12},{4,8},{8,4},{12,0},{16,28},{20,24},{24,20},{28,16},{1,13},{... | collective-permute-start | bytes 208904 | tf_op jit(solution)/shard_map/ppermute | solution.py:42
  42.1 8.4 %collective-permute-start.11 = (f32[17,8,128]{2,1,0:T(8,128)S(1)}, f32[17,8,128]{2,1,0:T(8,128)S(1)}, u32[]{:S(2)}, u32[]{:S(2)}) collective-permute-start(f32[17,8,128]{2,1,0:T(8,128)S(1)} %get-tuple-element.83), channel_id=1, source_target_pairs={{0,1},{1,0},{2,3},{3,2},{4,5},{5,4},{6,7},{7,6},{8,9},{9,8},{10,11... | collective-permute-start | bytes 208904 | tf_op jit(solution)/shard_map/ppermute | solution.py:42
  42.2 6.3 %collective-permute-start.14 = (f32[16,1024]{1,0:T(8,128)S(1)}, f32[16,1024]{1,0:T(8,128)S(1)}, u32[]{:S(2)}, u32[]{:S(2)}) collective-permute-start(f32[16,1024]{1,0:T(8,128)S(1)} %bitcast.36), channel_id=1, source_target_pairs={{0,12},{4,16},{8,20},{12,24},{16,28},{20,0},{24,4},{28,8},{1,13},{... | collective-permute-start | bytes 196616 | tf_op jit(solution)/shard_map/ppermute | solution.py:47
  56.7 6.1 %collective-permute-start.40 = (f32[17,8,128]{2,1,0:T(8,128)S(1)}, f32[17,8,128]{2,1,0:T(8,128)S(1)}, u32[]{:S(2)}, u32[]{:S(2)}) collective-permute-start(f32[17,8,128]{2,1,0:T(8,128)S(1)} %get-tuple-element.112.refs_0_.refs_3_), channel_id=1, source_target_pairs={{0,1},{1,0},{2,3},{3,2},{4,5},{5,4},{6,7},{7,6},{8,9},{9,8},{10,11... | collective-permute-start | bytes 208904 | tf_op jit(solution)/shard_map/ppermute | solution.py:42
  58.9 8.0 %collective-permute-start.17 = (f32[17,8,128]{2,1,0:T(8,128)S(1)}, f32[17,8,128]{2,1,0:T(8,128)S(1)}, u32[]{:S(2)}, u32[]{:S(2)}) collective-permute-start(f32[17,8,128]{2,1,0:T(8,128)S(1)} %get-tuple-element.87), channel_id=1, source_target_pairs={{0,4},{4,0},{8,12},{12,8},{16,20},{20,16},{24,28},{28,24},{1,5},{5... | collective-permute-start | bytes 208904 | tf_op jit(solution)/shard_map/ppermute | solution.py:42
  61.3 6.9 %collective-permute-start.18 = (f32[17,8,128]{2,1,0:T(8,128)S(1)}, f32[17,8,128]{2,1,0:T(8,128)S(1)}, u32[]{:S(2)}, u32[]{:S(2)}) collective-permute-start(f32[17,8,128]{2,1,0:T(8,128)S(1)} %get-tuple-element.88), channel_id=1, source_target_pairs={{0,8},{4,12},{8,0},{12,4},{16,24},{20,28},{24,16},{28,20},{1,9},{5... | collective-permute-start | bytes 208904 | tf_op jit(solution)/shard_map/ppermute | solution.py:42
  61.4 6.8 %collective-permute-start.19 = (f32[17,8,128]{2,1,0:T(8,128)S(1)}, f32[17,8,128]{2,1,0:T(8,128)S(1)}, u32[]{:S(2)}, u32[]{:S(2)}) collective-permute-start(f32[17,8,128]{2,1,0:T(8,128)S(1)} %get-tuple-element.89), channel_id=1, source_target_pairs={{0,12},{4,8},{8,4},{12,0},{16,28},{20,24},{24,20},{28,16},{1,13},{... | collective-permute-start | bytes 208904 | tf_op jit(solution)/shard_map/ppermute | solution.py:42
  68.3 5.9 %collective-permute-start.20 = (f32[17,8,128]{2,1,0:T(8,128)S(1)}, f32[17,8,128]{2,1,0:T(8,128)S(1)}, u32[]{:S(2)}, u32[]{:S(2)}) collective-permute-start(f32[17,8,128]{2,1,0:T(8,128)S(1)} %add_add_fusion.4.refs_0_), channel_id=1, source_target_pairs={{0,16},{4,20},{8,24},{12,28},{16,0},{20,4},{24,8},{28,12},{1,17},{... | collective-permute-start | bytes 208904 | tf_op jit(solution)/shard_map/ppermute | solution.py:42
  72.3 6.5 %collective-permute-start.44 = (f32[17,8,128]{2,1,0:T(8,128)S(1)}, f32[17,8,128]{2,1,0:T(8,128)S(1)}, u32[]{:S(2)}, u32[]{:S(2)}) collective-permute-start(f32[17,8,128]{2,1,0:T(8,128)S(1)} %add_add_fusion.1.refs_0_), channel_id=1, source_target_pairs={{0,16},{4,20},{8,24},{12,28},{16,0},{20,4},{24,8},{28,12},{1,17},{... | collective-permute-start | bytes 208904 | tf_op jit(solution)/shard_map/ppermute | solution.py:42
  74.3 6.6 %collective-permute-start.21 = (f32[17,8,128]{2,1,0:T(8,128)S(1)}, f32[17,8,128]{2,1,0:T(8,128)S(1)}, u32[]{:S(2)}, u32[]{:S(2)}) collective-permute-start(f32[17,8,128]{2,1,0:T(8,128)S(1)} %get-tuple-element.92.refs_0_), channel_id=1, source_target_pairs={{0,4},{4,0},{8,12},{12,8},{16,20},{20,16},{24,28},{28,24},{1,5},{5... | collective-permute-start | bytes 208904 | tf_op jit(solution)/shard_map/ppermute | solution.py:42
  77.2 5.9 %collective-permute-start.23 = (f32[17,8,128]{2,1,0:T(8,128)S(1)}, f32[17,8,128]{2,1,0:T(8,128)S(1)}, u32[]{:S(2)}, u32[]{:S(2)}) collective-permute-start(f32[17,8,128]{2,1,0:T(8,128)S(1)} %get-tuple-element.92.refs_0_), channel_id=1, source_target_pairs={{0,12},{4,8},{8,4},{12,0},{16,28},{20,24},{24,20},{28,16},{1,13},{... | collective-permute-start | bytes 208904 | tf_op jit(solution)/shard_map/ppermute | solution.py:42
  78.9 6.2 %collective-permute-start.45 = (f32[17,8,128]{2,1,0:T(8,128)S(1)}, f32[17,8,128]{2,1,0:T(8,128)S(1)}, u32[]{:S(2)}, u32[]{:S(2)}) collective-permute-start(f32[17,8,128]{2,1,0:T(8,128)S(1)} %get-tuple-element.119.refs_0_), channel_id=1, source_target_pairs={{0,4},{4,0},{8,12},{12,8},{16,20},{20,16},{24,28},{28,24},{1,5},{5... | collective-permute-start | bytes 208904 | tf_op jit(solution)/shard_map/ppermute | solution.py:42
  96.4 7.6 %collective-permute-start.27 = (f32[17,8,128]{2,1,0:T(8,128)S(1)}, f32[17,8,128]{2,1,0:T(8,128)S(1)}, u32[]{:S(2)}, u32[]{:S(2)}) collective-permute-start(f32[17,8,128]{2,1,0:T(8,128)S(1)} %get-tuple-element.98), channel_id=1, source_target_pairs={{0,4},{4,0},{8,12},{12,8},{16,20},{20,16},{24,28},{28,24},{1,5},{5... | collective-permute-start | bytes 208904 | tf_op jit(solution)/shard_map/ppermute | solution.py:42
  97.8 7.6 %collective-permute-start.28 = (f32[17,8,128]{2,1,0:T(8,128)S(1)}, f32[17,8,128]{2,1,0:T(8,128)S(1)}, u32[]{:S(2)}, u32[]{:S(2)}) collective-permute-start(f32[17,8,128]{2,1,0:T(8,128)S(1)} %get-tuple-element.99), channel_id=1, source_target_pairs={{0,8},{4,12},{8,0},{12,4},{16,24},{20,28},{24,16},{28,20},{1,9},{5... | collective-permute-start | bytes 208904 | tf_op jit(solution)/shard_map/ppermute | solution.py:42
  98.6 6.8 %collective-permute-start.29 = (f32[17,8,128]{2,1,0:T(8,128)S(1)}, f32[17,8,128]{2,1,0:T(8,128)S(1)}, u32[]{:S(2)}, u32[]{:S(2)}) collective-permute-start(f32[17,8,128]{2,1,0:T(8,128)S(1)} %get-tuple-element.100), channel_id=1, source_target_pairs={{0,12},{4,8},{8,4},{12,0},{16,28},{20,24},{24,20},{28,16},{1,13},{... | collective-permute-start | bytes 208904 | tf_op jit(solution)/shard_map/ppermute | solution.py:42
  104.0 5.8 %collective-permute-start.53 = (f32[17,8,128]{2,1,0:T(8,128)S(1)}, f32[17,8,128]{2,1,0:T(8,128)S(1)}, u32[]{:S(2)}, u32[]{:S(2)}) collective-permute-start(f32[17,8,128]{2,1,0:T(8,128)S(1)} %get-tuple-element.127), channel_id=1, source_target_pairs={{0,12},{4,8},{8,4},{12,0},{16,28},{20,24},{24,20},{28,16},{1,13},{... | collective-permute-start | bytes 208904 | tf_op jit(solution)/shard_map/ppermute | solution.py:42
  105.4 6.1 %collective-permute-start.30 = (f32[17,8,128]{2,1,0:T(8,128)S(1)}, f32[17,8,128]{2,1,0:T(8,128)S(1)}, u32[]{:S(2)}, u32[]{:S(2)}) collective-permute-start(f32[17,8,128]{2,1,0:T(8,128)S(1)} %add_add_fusion.3.refs_0_), channel_id=1, source_target_pairs={{0,16},{4,20},{8,24},{12,28},{16,0},{20,4},{24,8},{28,12},{1,17},{... | collective-permute-start | bytes 208904 | tf_op jit(solution)/shard_map/ppermute | solution.py:42
  109.8 5.9 %collective-permute-start.54 = (f32[17,8,128]{2,1,0:T(8,128)S(1)}, f32[17,8,128]{2,1,0:T(8,128)S(1)}, u32[]{:S(2)}, u32[]{:S(2)}) collective-permute-start(f32[17,8,128]{2,1,0:T(8,128)S(1)} %add_add_fusion.refs_0_), channel_id=1, source_target_pairs={{0,16},{4,20},{8,24},{12,28},{16,0},{20,4},{24,8},{28,12},{1,17},{... | collective-permute-start | bytes 208904 | tf_op jit(solution)/shard_map/ppermute | solution.py:42
  111.6 6.4 %collective-permute-start.55 = (f32[17,8,128]{2,1,0:T(8,128)S(1)}, f32[17,8,128]{2,1,0:T(8,128)S(1)}, u32[]{:S(2)}, u32[]{:S(2)}) collective-permute-start(f32[17,8,128]{2,1,0:T(8,128)S(1)} %get-tuple-element.131.refs_0_), channel_id=1, source_target_pairs={{0,4},{4,0},{8,12},{12,8},{16,20},{20,16},{24,28},{28,24},{1,5},{5... | collective-permute-start | bytes 208904 | tf_op jit(solution)/shard_map/ppermute | solution.py:42
  113.6 5.8 %collective-permute-start.56 = (f32[17,8,128]{2,1,0:T(8,128)S(1)}, f32[17,8,128]{2,1,0:T(8,128)S(1)}, u32[]{:S(2)}, u32[]{:S(2)}) collective-permute-start(f32[17,8,128]{2,1,0:T(8,128)S(1)} %get-tuple-element.131.refs_0_), channel_id=1, source_target_pairs={{0,8},{4,12},{8,0},{12,4},{16,24},{20,28},{24,16},{28,20},{1,9},{5... | collective-permute-start | bytes 208904 | tf_op jit(solution)/shard_map/ppermute | solution.py:42
  (43 other events, 255.7 us)
